TPU v7x, 768 devices: a whole 4x8x12 slice. The times are simulated.
768 devices in a mesh: gx: 96 (over x, z, y_hi), gy: 8 (over y_lo, core).
Axes of the slice: x: 4, y: 8 (y_hi: 2, y_lo: 4; y = y_hi * 4 + y_lo), z: 12, core: 2. Of those that a mesh axis runs over, the one named last changes fastest.
Arguments:
- distribution_values: float32 [19, 192, 64, 128], P(None, 'gx', 'gy'), may hold values from 0.02 to 0.09
- thermal_field: float32 [192, 64, 128], P('gx', 'gy'), may hold values from -0.5 to 0.5
- site_kind_code: int32 [192, 64, 128], P('gx', 'gy'), may hold values from 0 to 2, as said below
- entry_level_matrix: float32 [19, 128], replicated, may hold values from -16 to 16
- entry_level_offset: float32 [128], replicated, may hold values from -3 to 3
- inner_level_matrix: float32 [128, 128], replicated, may hold values from -0.5 to 0.5
- inner_level_offset: float32 [128], replicated, may hold values from -3 to 3
- exit_level_matrix: float32 [128, 19], replicated, may hold values from -0.125 to 0.125
- exit_level_offset: float32 [19], replicated, may hold values from -0.75 to 0.75
- closing_density_adjoint: float32 [19, 192, 64, 128], P(None, 'gx', 'gy'), may hold values from -6 to 6
- closing_thermal_adjoint: float32 [192, 64, 128], P('gx', 'gy'), may hold values from -6 to 6
Outputs:
- adjoint_populations: float32 [19, 192, 64, 128], P(None, 'gx', 'gy')
- adjoint_temperature: float32 [192, 64, 128], P('gx', 'gy')
- grad_first_weight: float32 [19, 128], replicated
- grad_first_bias: float32 [128], replicated
- grad_second_weight: float32 [128, 128], replicated
- grad_second_bias: float32 [128], replicated
- grad_third_weight: float32 [128, 19], replicated
- grad_third_bias: float32 [19], replicated
Inputs may be any that keep to these rules, and one draw needn't show every extreme that they name: `site_kind_code`: 0 marks a fluid cell, 1 a solid cell whose temperature is held, 2 a solid heater cell.
All inputs are finite; a program needn't handle non-finite values.
Results may differ from a plain program's by a relative error of at most 0.0003.
Values sent between devices are 32-bit elements; how exact they have to be, the bound alone decides.
No kernel may reach another device: no remote copies, remote signals or barrier semaphores. Data moves between devices by JAX's collectives and lax.ppermute only.
A program may use at most 64 MiB of HBM per device.

v0:
```python
import math

import jax
import jax.numpy as jnp
import numpy as np
from jax import lax
from jax.sharding import PartitionSpec as P

STEPS = 2


VELOCITIES = np.array(
    [
        [0, 0, 0],
        [1, 0, 0],
        [-1, 0, 0],
        [0, 1, 0],
        [0, -1, 0],
        [0, 0, 1],
        [0, 0, -1],
        [1, 1, 0],
        [-1, -1, 0],
        [1, -1, 0],
        [-1, 1, 0],
        [1, 0, 1],
        [-1, 0, -1],
        [1, 0, -1],
        [-1, 0, 1],
        [0, 1, 1],
        [0, -1, -1],
        [0, 1, -1],
        [0, -1, 1],
    ]
)
OPPOSITE = np.array([0, 2, 1, 4, 3, 6, 5, 8, 7, 10, 9, 12, 11, 14, 13, 16, 15, 18, 17])
LATTICE_WEIGHTS = np.array([1.0 / 3.0] + [1.0 / 18.0] * 6 + [1.0 / 36.0] * 12)
BUOYANCY = 0.3 * LATTICE_WEIGHTS * VELOCITIES[:, 2]
PLANE_DIRECTIONS = [(0, 1), (0, -1), (1, 1), (1, -1)]
CONDUCTIVITY = 0.1
HOT_WALL = 0.5
COLD_WALL = -0.5
HEATER = 0.5
PRECISE_MODE = lax.Precision.HIGHEST
CONTRACT = (((0,), (0,)), ((), ()))


def passed_along(value, axis, by):
    count = lax.axis_size(axis)
    return lax.ppermute(value, axis, [(i, (i + by) % count) for i in range(count)])


def in_one(arrays, axis):
    ends = [0]
    for a in arrays:
        ends.append(ends[-1] + a.size)
    running = lax.psum(jnp.concatenate([a.ravel() for a in arrays]), axis)
    return tuple((running[b:e].reshape(a.shape) for a, b, e in zip(arrays, ends, ends[1:])))


def propagation_offset(window, step_z):
    lead = [(0, 0)] * (window.ndim - 1)
    if step_z == 1:
        return jnp.pad(window[..., :-1], lead + [(1, 0)])
    if step_z == -1:
        return jnp.pad(window[..., 1:], lead + [(0, 1)])
    return window


def boundary(cells):
    depths = jnp.arange(cells)
    masks = []
    for i in range(19):
        step_z = int(VELOCITIES[i, 2])
        if step_z == 1:
            masks.append(depths == 0)
        elif step_z == -1:
            masks.append(depths == cells - 1)
        else:
            masks.append(depths < 0)
    return jnp.stack(masks).astype(jnp.float32)[:, None, None, :]


def collide(current_fields, current_thermal, site_kind_code, learned_coefficients):
    (
        entry_level_matrix,
        entry_level_offset,
        inner_level_matrix,
        inner_level_offset,
        exit_level_matrix,
        exit_level_offset,
    ) = learned_coefficients
    flattened = current_fields.reshape(19, -1)
    hidden_one = jnp.tanh(
        lax.dot_general(entry_level_matrix, flattened, CONTRACT, precision=PRECISE_MODE)
        + entry_level_offset[:, None]
    )
    hidden_two = jnp.tanh(
        lax.dot_general(inner_level_matrix, hidden_one, CONTRACT, precision=PRECISE_MODE)
        + inner_level_offset[:, None]
    )
    output = (
        lax.dot_general(exit_level_matrix, hidden_two, CONTRACT, precision=PRECISE_MODE)
        + exit_level_offset[:, None]
    )
    lifting = jnp.asarray(BUOYANCY, jnp.float32).reshape((19,) + (1,) * current_thermal.ndim)
    relaxed = (
        current_fields + output.reshape(current_fields.shape) + lifting * current_thermal[None]
    )
    bounced = current_fields[OPPOSITE]
    return jnp.where(site_kind_code[None] == 0, relaxed, bounced)


def motion_of(current_fields):
    lookup_table = jnp.asarray(VELOCITIES.T, jnp.float32)
    return jnp.tensordot(lookup_table, current_fields, axes=1, precision=PRECISE_MODE)


def depth_pad(heat_rim):
    span_along_x, span_along_y, discarded_outcome = heat_rim.shape
    bottom = jnp.full((span_along_x, span_along_y, 1), HOT_WALL, jnp.float32)
    upper = jnp.full((span_along_x, span_along_y, 1), COLD_WALL, jnp.float32)
    return jnp.concatenate([bottom, heat_rim, upper], axis=2)


def advance_temp(padded, current_thermal, motion, site_kind_code):
    span_along_x, span_along_y, span_along_z = current_thermal.shape
    summed = (1.0 - 6.0 * CONDUCTIVITY) * current_thermal
    for a in range(3):
        for s in (1, -1):
            anchor = [1, 1, 1]
            anchor[a] += s
            nearby = padded[
                anchor[0] : anchor[0] + span_along_x,
                anchor[1] : anchor[1] + span_along_y,
                anchor[2] : anchor[2] + span_along_z,
            ]
            summed = summed + (CONDUCTIVITY - 0.5 * s * motion[a]) * nearby
    return jnp.where(
        site_kind_code == 0, summed, jnp.where(site_kind_code == 1, current_thermal, HEATER)
    )


def stream_pull(planes, orient):
    span_along_x = planes[0].shape[0] - 2
    span_along_y = planes[0].shape[1] - 2
    pulled = []
    for i in range(19):
        step_x = int(VELOCITIES[i, 0]) * orient
        step_y = int(VELOCITIES[i, 1]) * orient
        step_z = int(VELOCITIES[i, 2]) * orient
        window = planes[i][
            1 - step_x : 1 - step_x + span_along_x, 1 - step_y : 1 - step_y + span_along_y, :
        ]
        pulled.append(propagation_offset(window, step_z))
    return jnp.stack(pulled)


def cross_first(message, offset):
    return passed_along(message, "gx", offset)


def cross_second(message, offset):
    return passed_along(message, "gy", offset)


def frame_rims(centre, rim_list):
    span_along_x, span_along_y, span_along_z = centre.shape
    pieces = []
    for k in range(4):
        length = span_along_y if k < 2 else span_along_x
        if rim_list[k] is None:
            pieces.append(jnp.zeros((length, span_along_z), jnp.float32))
        else:
            pieces.append(rim_list[k])
    middle = jnp.concatenate([pieces[0][None], centre, pieces[1][None]], axis=0)
    left_edge = jnp.pad(pieces[2], ((1, 1), (0, 0)))
    right_edge = jnp.pad(pieces[3], ((1, 1), (0, 0)))
    return jnp.concatenate([left_edge[:, None], middle, right_edge[:, None]], axis=1)


def face_exchange(values, extras, orient):
    span_along_x, span_along_y = (values.shape[1], values.shape[2])
    lower_first = [i for i in range(19) if int(VELOCITIES[i, 0]) * orient == 1]
    upper_first = [i for i in range(19) if int(VELOCITIES[i, 0]) * orient == -1]
    lower_second = [i for i in range(19) if int(VELOCITIES[i, 1]) * orient == 1]
    upper_second = [i for i in range(19) if int(VELOCITIES[i, 1]) * orient == -1]
    from_below = cross_first(
        jnp.concatenate(
            [values[np.array(lower_first), span_along_x - 1], extras[0][span_along_x - 1][None]],
            axis=0,
        ),
        1,
    )
    from_above = cross_first(
        jnp.concatenate([values[np.array(upper_first), 0], extras[1][0][None]], axis=0), -1
    )
    blank_plane = jnp.zeros_like(values[0, :1])
    extended = []
    for i in range(19):
        below_part = from_below[lower_first.index(i)][None] if i in lower_first else blank_plane
        above_part = from_above[upper_first.index(i)][None] if i in upper_first else blank_plane
        extended.append(jnp.concatenate([below_part, values[i], above_part], axis=0))

    def column_rows(i, column):
        step_x = int(VELOCITIES[i, 0]) * orient
        return extended[i][1 - step_x : 1 - step_x + span_along_x, column]

    up_message = jnp.stack(
        [column_rows(i, span_along_y - 1) for i in lower_second] + [extras[2][:, span_along_y - 1]]
    )
    down_message = jnp.stack([column_rows(i, 0) for i in upper_second] + [extras[3][:, 0]])
    from_left = cross_second(up_message, 1)
    from_right = cross_second(down_message, -1)
    blank_column = jnp.zeros_like(extended[0][:, 0])
    planes = []
    for i in range(19):
        step_x = int(VELOCITIES[i, 0]) * orient
        margins = ((1 - step_x, 1 + step_x), (0, 0))
        left_edge = (
            jnp.pad(from_left[lower_second.index(i)], margins)
            if i in lower_second
            else blank_column
        )
        right_edge = (
            jnp.pad(from_right[upper_second.index(i)], margins)
            if i in upper_second
            else blank_column
        )
        planes.append(
            jnp.concatenate([left_edge[:, None], extended[i], right_edge[:, None]], axis=1)
        )
    return (planes, (from_below[-1], from_above[-1], from_left[-1], from_right[-1]))


def forward_rims(post_collide, current_thermal):
    planes, rim_list = face_exchange(
        post_collide, (current_thermal, current_thermal, current_thermal, current_thermal), 1
    )
    return (planes, frame_rims(current_thermal, rim_list))


def adjoint_rims(current_adjoint, fluxes):
    planes, rim_list = face_exchange(
        current_adjoint, (fluxes[0], fluxes[1], fluxes[2], fluxes[3]), -1
    )
    framed = [
        frame_rims(fluxes[j], [rim_list[k] if k == j else None for k in range(4)]) for j in range(4)
    ]
    return (planes, jnp.stack(framed))


def per_device(
    distribution_values,
    thermal_field,
    site_kind_code,
    entry_level_matrix,
    entry_level_offset,
    inner_level_matrix,
    inner_level_offset,
    exit_level_matrix,
    exit_level_offset,
    closing_density_adjoint,
    closing_thermal_adjoint,
):
    learned_coefficients = (
        entry_level_matrix,
        entry_level_offset,
        inner_level_matrix,
        inner_level_offset,
        exit_level_matrix,
        exit_level_offset,
    )
    span_along_x, span_along_y, span_along_z = thermal_field.shape
    walls = boundary(span_along_z)
    history = []
    current_fields, current_thermal = (distribution_values, thermal_field)
    for i in range(STEPS):
        post_collide = collide(
            current_fields, current_thermal, site_kind_code, learned_coefficients
        )
        planes, heat_rim = forward_rims(post_collide, current_thermal)
        read = stream_pull(planes, 1) + walls * post_collide[OPPOSITE]
        motion = motion_of(current_fields)
        heated = advance_temp(depth_pad(heat_rim), current_thermal, motion, site_kind_code)
        history.append((current_fields, current_thermal, heat_rim, motion))
        current_fields, current_thermal = (read, heated)
    is_fluid = (site_kind_code == 0).astype(jnp.float32)
    constant_inputs = (site_kind_code == 1).astype(jnp.float32)
    lookup_table = jnp.asarray(VELOCITIES, jnp.float32)
    current_adjoint, thermal_adjoint = (closing_density_adjoint, closing_thermal_adjoint)
    accumulated = None
    for i in reversed(range(STEPS)):
        current_fields, current_thermal, heat_rim, motion = history[i]
        liquid_adjoint = is_fluid * thermal_adjoint
        fluxes = jnp.stack(
            [(CONDUCTIVITY - 0.5 * s * motion[a]) * liquid_adjoint for a, s in PLANE_DIRECTIONS]
        )
        planes, flux_rim = adjoint_rims(current_adjoint, fluxes)
        postcollision_gradient = stream_pull(planes, -1) + (walls * current_adjoint)[OPPOSITE]
        thermal_adjoint_increment = (
            1.0 - 6.0 * CONDUCTIVITY
        ) * liquid_adjoint + constant_inputs * thermal_adjoint
        for j in range(4):
            along, s = PLANE_DIRECTIONS[j]
            anchor = [1, 1]
            anchor[along] -= s
            thermal_adjoint_increment = (
                thermal_adjoint_increment
                + flux_rim[
                    j, anchor[0] : anchor[0] + span_along_x, anchor[1] : anchor[1] + span_along_y, :
                ]
            )
        for s in (1, -1):
            thermal_adjoint_increment = thermal_adjoint_increment + propagation_offset(
                (CONDUCTIVITY - 0.5 * s * motion[2]) * liquid_adjoint, s
            )
        full_rim = depth_pad(heat_rim)
        motion_gradient = []
        for a in range(3):
            summed = jnp.zeros_like(current_thermal)
            for s in (1, -1):
                anchor = [1, 1, 1]
                anchor[a] += s
                nearby = full_rim[
                    anchor[0] : anchor[0] + span_along_x,
                    anchor[1] : anchor[1] + span_along_y,
                    anchor[2] : anchor[2] + span_along_z,
                ]
                summed = summed - 0.5 * s * nearby
            motion_gradient.append(liquid_adjoint * summed)
        discarded_outcome, backpropagation_function = jax.vjp(
            lambda p, h, w: collide(p, h, site_kind_code, w),
            current_fields,
            current_thermal,
            learned_coefficients,
        )
        collision_gradient, relaxation_thermal_adjoint, adjoint_sequence = backpropagation_function(
            postcollision_gradient
        )
        current_adjoint = collision_gradient + jnp.tensordot(
            lookup_table, jnp.stack(motion_gradient), axes=1, precision=PRECISE_MODE
        )
        thermal_adjoint = thermal_adjoint_increment + relaxation_thermal_adjoint
        accumulated = (
            adjoint_sequence
            if accumulated is None
            else jax.tree.map(jnp.add, accumulated, adjoint_sequence)
        )
    finals = in_one(
        (
            accumulated[0],
            accumulated[1],
            accumulated[2],
            accumulated[3],
            accumulated[4],
            accumulated[5],
        ),
        ("gx", "gy"),
    )
    factor = 1.0 / math.sqrt(
        span_along_x * lax.axis_size("gx") * span_along_y * lax.axis_size("gy") * span_along_z
    )
    return (
        current_adjoint,
        thermal_adjoint,
        finals[0] * factor,
        finals[1] * factor,
        finals[2] * factor,
        finals[3] * factor,
        finals[4] * factor,
        finals[5] * factor,
    )


def solution(mesh):
    in_specs = (
        P(None, "gx", "gy", None),
        P("gx", "gy", None),
        P("gx", "gy", None),
        P(),
        P(),
        P(),
        P(),
        P(),
        P(),
        P(None, "gx", "gy", None),
        P("gx", "gy", None),
    )
    out_specs = (P(None, "gx", "gy", None), P("gx", "gy", None), P(), P(), P(), P(), P(), P())
    return jax.shard_map(
        per_device, mesh=mesh, in_specs=in_specs, out_specs=out_specs, check_vma=False
    )
```

profile of v0, /device:TPU:1, one launch (start us, length us, event | category | flops | bytes accessed | tf_op | source)
XLA Modules:
  0.0 708.7 jit_solution(1194189634799353391)
XLA Ops:
  8.7 1.5 gather_fusion.1
  12.1 1.8 fusion.4
  17.2 22.6 %collective-permute-start.1 = (f32[6,8,128]{2,0,1:T(8,128)S(1)}, f32[6,8,128]{2,0,1:T(8,128)S(1)}, u32[]{:S(2)}, u32[]{:S(2)}) collective-permute-start(f32[6,8,128]{2,0,1:T(8,128)S(1)} %pad_maximum_fusion.25), channel_id=1, source_target_pairs={{0,760},{8,0},{16,8},{24,16},{32,24},{40,32},{48,40},{56,48},{64,5... | collective-permute-start | bytes 73736 | tf_op jit(solution)/shard_map/ppermute | solution.py:49
  40.4 1.9 collective-permute-start
  48.8 4.7 collective-permute-done
  53.6 3.9 collective-permute-start.3
  57.4 2.3 collective-permute-start.2
  67.1 2.1 stack.470
  69.8 2.9 fusion
  87.5 6.4 collective-permute-start.8
  95.1 1.8 gather_fusion.6
  99.9 3.1 collective-permute-start.9
  104.0 8.9 %collective-permute-done.9 = f32[6,8,128]{2,0,1:T(8,128)S(1)} collective-permute-done((f32[6,8,128]{2,0,1:T(8,128)S(1)}, f32[6,8,128]{2,0,1:T(8,128)S(1)}, u32[]{:S(2)}, u32[]{:S(2)}) %collective-permute-start.9) | collective-permute-done | bytes 24608 | tf_op jit(solution)/shard_map/ppermute | solution.py:49
  116.2 5.7 collective-permute-start.11
  121.9 3.1 collective-permute-start.10
  128.7 1.9 collective-permute-start.5
  130.6 11.5 %collective-permute-start.4 = (f32[6,8,128]{2,0,1:T(8,128)S(1)}, f32[6,8,128]{2,0,1:T(8,128)S(1)}, u32[]{:S(2)}, u32[]{:S(2)}) collective-permute-start(f32[6,8,128]{2,0,1:T(8,128)S(1)} %pad_maximum_fusion.26), channel_id=1, source_target_pairs={{0,760},{8,0},{16,8},{24,16},{32,24},{40,32},{48,40},{56,48},{64,5... | collective-permute-start | bytes 73736 | tf_op jit(solution)/shard_map/ppermute | solution.py:49
  146.0 5.3 collective-permute-start.6
  155.3 1.9 collective-permute-start.7
  178.7 3.5 stack.450
  182.3 2.6 fusion.21
  185.0 2.4 fusion.164
  187.3 1.8 fusion.168
  195.8 1.8 scatter_fusion
  203.1 11.0 %collective-permute-start.12 = (f32[6,8,128]{2,0,1:T(8,128)S(1)}, f32[6,8,128]{2,0,1:T(8,128)S(1)}, u32[]{:S(2)}, u32[]{:S(2)}) collective-permute-start(f32[6,8,128]{2,0,1:T(8,128)S(1)} %pad_maximum_fusion.30), channel_id=1, source_target_pairs={{0,760},{8,0},{16,8},{24,16},{32,24},{40,32},{48,40},{56,48},{64,5... | collective-permute-start | bytes 73736 | tf_op jit(solution)/shard_map/ppermute | solution.py:49
  214.1 2.1 collective-permute-start.13
  218.1 8.8 %collective-permute-done.13 = f32[6,8,128]{2,0,1:T(8,128)S(1)} collective-permute-done((f32[6,8,128]{2,0,1:T(8,128)S(1)}, f32[6,8,128]{2,0,1:T(8,128)S(1)}, u32[]{:S(2)}, u32[]{:S(2)}) %collective-permute-start.13) | collective-permute-done | bytes 24608 | tf_op jit(solution)/shard_map/ppermute | solution.py:49
  227.0 7.5 %collective-permute-start.14 = (f32[6,2,128]{2,1,0:T(2,128)S(1)}, f32[6,2,128]{2,1,0:T(2,128)S(1)}, u32[]{:S(2)}, u32[]{:S(2)}) collective-permute-start(f32[6,2,128]{2,1,0:T(2,128)S(1)} %constant_dynamic-update-slice_fusion.74), channel_id=1, source_target_pairs={{0,7},{1,0},{2,1},{3,2},{4,3},{5,4},{6,5},{7,6},{8,15},{9,8},{10,9... | collective-permute-start | bytes 18440 | tf_op jit(solution)/shard_map/ppermute | solution.py:49
  234.6 1.9 collective-permute-start.15
  241.2 1.8 fusion.165
  252.9 1.8 scatter_fusion.1
  254.7 443.3 %all-reduce.87.cloned.1.call-done = f32[21523]{0:T(1024)} async-done(((f32[21523]{0:T(1024)}), f32[21523]{0:T(1024)}) %all-reduce.87.cloned.1.call-update) | async-done | bytes 86108 | tf_op jit(solution)/shard_map/psum | solution.py:56
  (638 shorter events, 108.7 us)
Async XLA Ops:
  7.2 690.8 %all-reduce.87.cloned.1.call-start = ((), (), s32[]{:S(2)}) async-start(), calls=%async_computation | async-start | bytes 180224 | tf_op jit(solution)/shard_map/psum | solution.py:56
  8.7 54.8 %copy-start.111 = (s32[1024]{0:T(1024)}, s32[1024]{0:T(1024)S(1)}, u32[]{:S(2)}) copy-start(s32[1024]{0:T(1024)S(1)} %pad_clamp_fusion) | copy-start | bytes 12292
  15.9 28.6 %copy-start.4 = (f32[19,2,8,128]{3,1,2,0:T(2,128)}, f32[19,2,8,128]{3,1,2,0:T(2,128)S(1)}, u32[]{:S(2)}) copy-start(f32[19,2,8,128]{3,1,2,0:T(2,128)S(1)} %copy_select_fusion.1) | copy-start | bytes 466948
  17.2 22.6 %copy-start.31 = (s32[5]{0:T(128)S(1)}, s32[5]{0:T(128)}, u32[]{:S(2)}) copy-start(s32[5]{0:T(128)} %constant.374) | copy-start | bytes 64
  17.2 31.5 %collective-permute-start.1 = (f32[6,8,128]{2,0,1:T(8,128)S(1)}, f32[6,8,128]{2,0,1:T(8,128)S(1)}, u32[]{:S(2)}, u32[]{:S(2)}) collective-permute-start(f32[6,8,128]{2,0,1:T(8,128)S(1)} %pad_maximum_fusion.25), channel_id=1, source_target_pairs={{0,760},{8,0},{16,8},{24,16},{32,24},{40,32},{48,40},{56,48},{64,5... | collective-permute-start | bytes 73736 | tf_op jit(solution)/shard_map/ppermute | solution.py:49
  40.4 13.0 %collective-permute-start = (f32[6,8,128]{2,0,1:T(8,128)S(1)}, f32[6,8,128]{2,0,1:T(8,128)S(1)}, u32[]{:S(2)}, u32[]{:S(2)}) collective-permute-start(f32[6,8,128]{2,0,1:T(8,128)S(1)} %pad_maximum_fusion.24), channel_id=1, source_target_pairs={{0,8},{8,16},{16,24},{24,32},{32,40},{40,48},{48,56},{56,64},{64,7... | collective-permute-start | bytes 73736 | tf_op jit(solution)/shard_map/ppermute | solution.py:49
  42.7 22.2 %copy-start.48 = (f32[1,2,8,128]{3,0,2,1:T(1,128)}, f32[1,2,8,128]{3,0,2,1:T(1,128)S(1)}, u32[]{:S(2)}) copy-start(f32[1,2,8,128]{3,0,2,1:T(1,128)S(1)} %get-tuple-element.253) | copy-start | bytes 24580
  42.7 22.2 %copy-start.50 = (f32[1,2,8,128]{3,0,2,1:T(1,128)}, f32[1,2,8,128]{3,0,2,1:T(1,128)S(1)}, u32[]{:S(2)}) copy-start(f32[1,2,8,128]{3,0,2,1:T(1,128)S(1)} %get-tuple-element.254) | copy-start | bytes 24580
  46.0 15.6 %copy-start.32 = (f32[19,128]{1,0:T(8,128)}, f32[19,128]{1,0:T(8,128)S(1)}, u32[]{:S(2)}) copy-start(f32[19,128]{1,0:T(8,128)S(1)} %convert_element_type.98) | copy-start | bytes 29188
  48.7 16.2 %copy-start.34 = (f32[1,8,128]{2,0,1:T(1,128)}, f32[1,8,128]{2,0,1:T(1,128)S(1)}, u32[]{:S(2)}) copy-start(f32[1,8,128]{2,0,1:T(1,128)S(1)} %get-tuple-element.261) | copy-start | bytes 12292
  53.4 11.5 %copy-start.36 = (f32[1,8,128]{2,0,1:T(1,128)}, f32[1,8,128]{2,0,1:T(1,128)S(1)}, u32[]{:S(2)}) copy-start(f32[1,8,128]{2,0,1:T(1,128)S(1)} %get-tuple-element.255) | copy-start | bytes 12292
  53.6 6.2 collective-permute-start.3
  57.4 3.1 collective-permute-start.2
  86.9 7.0 copy-start.109
  87.5 15.5 %collective-permute-start.8 = (f32[6,8,128]{2,0,1:T(8,128)}, f32[6,8,128]{2,0,1:T(8,128)}, u32[]{:S(2)}, u32[]{:S(2)}) collective-permute-start(f32[6,8,128]{2,0,1:T(8,128)} %pad_maximum_fusion.28), channel_id=1, source_target_pairs={{0,760},{8,0},{16,8},{24,16},{32,24},{40,32},{48,40},{56,48},{64,5... | collective-permute-start | bytes 73736 | tf_op jit(solution)/shard_map/ppermute | solution.py:49
  99.9 12.9 %collective-permute-start.9 = (f32[6,8,128]{2,0,1:T(8,128)S(1)}, f32[6,8,128]{2,0,1:T(8,128)S(1)}, u32[]{:S(2)}, u32[]{:S(2)}) collective-permute-start(f32[6,8,128]{2,0,1:T(8,128)S(1)} %copy-done.95), channel_id=1, source_target_pairs={{0,8},{8,16},{16,24},{24,32},{32,40},{40,48},{48,56},{56,64},{64,7... | collective-permute-start | bytes 73736 | tf_op jit(solution)/shard_map/ppermute | solution.py:49
  104.0 8.9 %copy-start.93 = (f32[2,8,128]{2,0,1:T(2,128)S(1)}, f32[2,8,128]{2,0,1:T(2,128)}, u32[]{:S(2)}) copy-start(f32[2,8,128]{2,0,1:T(2,128)} %get-tuple-element.172) | copy-start | bytes 24580
  115.5 9.5 %copy-start.102 = (f32[2,8,128]{2,1,0:T(8,128)S(1)}, f32[2,8,128]{2,1,0:T(8,128)}, u32[]{:S(2)}) copy-start(f32[2,8,128]{2,1,0:T(8,128)} %param.52) | copy-start | bytes 24580
  116.2 10.3 %collective-permute-start.11 = (f32[6,2,128]{2,1,0:T(2,128)S(1)}, f32[6,2,128]{2,1,0:T(2,128)S(1)}, u32[]{:S(2)}, u32[]{:S(2)}) collective-permute-start(f32[6,2,128]{2,1,0:T(2,128)S(1)} %get-tuple-element.296), channel_id=1, source_target_pairs={{0,1},{1,2},{2,3},{3,4},{4,5},{5,6},{6,7},{7,0},{8,9},{9,10},{10,1... | collective-permute-start | bytes 18440 | tf_op jit(solution)/shard_map/ppermute | solution.py:49
  121.9 5.2 collective-permute-start.10
  128.0 18.0 %copy-start.58 = (f32[2,8,128]{2,0,1:T(2,128)}, f32[2,8,128]{2,0,1:T(2,128)S(1)}, u32[]{:S(2)}) copy-start(f32[2,8,128]{2,0,1:T(2,128)S(1)} %get-tuple-element.292) | copy-start | bytes 24580
  128.0 24.8 %copy-start.56 = (f32[2,8,128]{2,0,1:T(2,128)}, f32[2,8,128]{2,0,1:T(2,128)S(1)}, u32[]{:S(2)}) copy-start(f32[2,8,128]{2,0,1:T(2,128)S(1)} %get-tuple-element.293) | copy-start | bytes 24580
  128.7 16.0 %collective-permute-start.5 = (f32[6,8,128]{2,0,1:T(8,128)S(1)}, f32[6,8,128]{2,0,1:T(8,128)S(1)}, u32[]{:S(2)}, u32[]{:S(2)}) collective-permute-start(f32[6,8,128]{2,0,1:T(8,128)S(1)} %pad_maximum_fusion.27), channel_id=1, source_target_pairs={{0,8},{8,16},{16,24},{24,32},{32,40},{40,48},{48,56},{56,64},{64,7... | collective-permute-start | bytes 73736 | tf_op jit(solution)/shard_map/ppermute | solution.py:49
  130.6 13.3 %collective-permute-start.4 = (f32[6,8,128]{2,0,1:T(8,128)S(1)}, f32[6,8,128]{2,0,1:T(8,128)S(1)}, u32[]{:S(2)}, u32[]{:S(2)}) collective-permute-start(f32[6,8,128]{2,0,1:T(8,128)S(1)} %pad_maximum_fusion.26), channel_id=1, source_target_pairs={{0,760},{8,0},{16,8},{24,16},{32,24},{40,32},{48,40},{56,48},{64,5... | collective-permute-start | bytes 73736 | tf_op jit(solution)/shard_map/ppermute | solution.py:49
  145.3 6.0 copy-start.45
  146.0 11.2 %collective-permute-start.6 = (f32[6,2,128]{2,1,0:T(2,128)S(1)}, f32[6,2,128]{2,1,0:T(2,128)S(1)}, u32[]{:S(2)}, u32[]{:S(2)}) collective-permute-start(f32[6,2,128]{2,1,0:T(2,128)S(1)} %constant_dynamic-update-slice_fusion.31), channel_id=1, source_target_pairs={{0,7},{1,0},{2,1},{3,2},{4,3},{5,4},{6,5},{7,6},{8,15},{9,8},{10,9... | collective-permute-start | bytes 18440 | tf_op jit(solution)/shard_map/ppermute | solution.py:49
  155.3 5.5 collective-permute-start.7
  203.1 14.9 %collective-permute-start.12 = (f32[6,8,128]{2,0,1:T(8,128)S(1)}, f32[6,8,128]{2,0,1:T(8,128)S(1)}, u32[]{:S(2)}, u32[]{:S(2)}) collective-permute-start(f32[6,8,128]{2,0,1:T(8,128)S(1)} %pad_maximum_fusion.30), channel_id=1, source_target_pairs={{0,760},{8,0},{16,8},{24,16},{32,24},{40,32},{48,40},{56,48},{64,5... | collective-permute-start | bytes 73736 | tf_op jit(solution)/shard_map/ppermute | solution.py:49
  214.1 12.8 %collective-permute-start.13 = (f32[6,8,128]{2,0,1:T(8,128)S(1)}, f32[6,8,128]{2,0,1:T(8,128)S(1)}, u32[]{:S(2)}, u32[]{:S(2)}) collective-permute-start(f32[6,8,128]{2,0,1:T(8,128)S(1)} %pad_maximum_fusion.31), channel_id=1, source_target_pairs={{0,8},{8,16},{16,24},{24,32},{32,40},{40,48},{48,56},{56,64},{64,7... | collective-permute-start | bytes 73736 | tf_op jit(solution)/shard_map/ppermute | solution.py:49
  227.0 10.7 %collective-permute-start.14 = (f32[6,2,128]{2,1,0:T(2,128)S(1)}, f32[6,2,128]{2,1,0:T(2,128)S(1)}, u32[]{:S(2)}, u32[]{:S(2)}) collective-permute-start(f32[6,2,128]{2,1,0:T(2,128)S(1)} %constant_dynamic-update-slice_fusion.74), channel_id=1, source_target_pairs={{0,7},{1,0},{2,1},{3,2},{4,3},{5,4},{6,5},{7,6},{8,15},{9,8},{10,9... | collective-permute-start | bytes 18440 | tf_op jit(solution)/shard_map/ppermute | solution.py:49
  234.6 3.1 collective-permute-start.15
  254.7 447.2 %copy-start.13 = (f32[19,2,8,128]{3,2,1,0:T(8,128)}, f32[19,2,8,128]{3,2,1,0:T(8,128)S(1)}, u32[]{:S(2)}) copy-start(f32[19,2,8,128]{3,2,1,0:T(8,128)S(1)} %scatter_fusion.1) | copy-start | bytes 466948
  (123 other events, 145.2 us)
Sparse Core Ops, SparseCore 0:
  251.7 446.2 all-reduce.86
where the time goes:
time: 712 us; the launch traced here: 709 us
  waiting for transfers between devices  469 us (66%)
  starting transfers between devices  92.1 us (13%)
  local copies, waits for them, and re-layouts  76.5 us (11%)
  matrix products  27.8 us (4%)
  other arithmetic  26.7 us (4%)
  between operations  16.5 us (2%)
    psum x1, waiting for transfers between devices, in_one(): running = lax.psum(jnp.concatenate([a.ravel() for a in arrays]), axis)  443 us
    ppermute x16, starting transfers between devices, passed_along(): lax.ppermute(value, axis, [(i, (i + by) % count) for i in range(count)])  92.1 us
    unnamed x336, local copies, waits for them, and re-layouts  37.8 us
    ppermute x16, waiting for transfers between devices, passed_along(): lax.ppermute(value, axis, [(i, (i + by) % count) for i in range(count)])  25.9 us
  transfers between devices with their start and end apart: 17, of which 8 were waited for; matrix products, arithmetic and copies ran while one was open for 3% of the time, Pallas kernels for 0%

commit v1 on v0

v1 whole, which is shorter than its diff:
```python
import math

import jax
import jax.numpy as jnp
import numpy as np
from jax import lax
from jax.experimental import pallas as pl
from jax.experimental.pallas import tpu as pltpu
from jax.sharding import PartitionSpec as P

VELOCITIES = [
    (0, 0, 0), (1, 0, 0), (-1, 0, 0), (0, 1, 0), (0, -1, 0), (0, 0, 1), (0, 0, -1),
    (1, 1, 0), (-1, -1, 0), (1, -1, 0), (-1, 1, 0), (1, 0, 1), (-1, 0, -1), (1, 0, -1),
    (-1, 0, 1), (0, 1, 1), (0, -1, -1), (0, 1, -1), (0, -1, 1),
]
Q = 19
OPPOSITE = [VELOCITIES.index((-a, -b, -c)) for a, b, c in VELOCITIES]
WEIGHTS = [1.0 / 3.0] + [1.0 / 18.0] * 6 + [1.0 / 36.0] * 12
BUOYANCY = [float(np.float32(0.3 * w * c[2])) for w, c in zip(WEIGHTS, VELOCITIES)]
CONDUCTIVITY = 0.1
HOT_WALL = 0.5
COLD_WALL = -0.5
HEATER = 0.5
HID = 128
KP = 32
ROWS = 16
LANES = 128
CH = 512
PACK = 176
F32 = jnp.float32
BF16 = jnp.bfloat16


def moving(axis, sign, orient):
    return [i for i in range(Q) if VELOCITIES[i][axis] * orient == sign]


def diagonal(sx, sy, orient):
    return VELOCITIES.index((sx * orient, sy * orient, 0))


def split(x):
    hi = x.astype(BF16)
    lo = (x - hi.astype(F32)).astype(BF16)
    return hi, lo


def stacked(x):
    return jnp.concatenate(split(x), axis=0)


def nn(a, b):
    return lax.dot_general(a, b, (((1,), (0,)), ((), ())), preferred_element_type=F32)


def nt(a, b):
    return lax.dot_general(a, b, (((1,), (1,)), ((), ())), preferred_element_type=F32)


def left(w):
    hi, lo = split(w)
    return jnp.concatenate(
        [jnp.concatenate([hi, hi], axis=1), jnp.concatenate([lo, lo], axis=1)], axis=0
    )


def product(a, b, rows):
    d = nn(a, b)
    return d[:rows] + d[rows:]


def four_blocks(d, rows):
    return d[:rows, :HID] + d[:rows, HID:] + d[rows:, :HID] + d[rows:, HID:]


def lanes_of(shape):
    return lax.broadcasted_iota(jnp.int32, shape, 1)


def subs_of(shape):
    return lax.broadcasted_iota(jnp.int32, shape, 0)


def shift_z(v, step, fill):
    if step == 1:
        return jnp.where(lanes_of(v.shape) == 0, fill, pltpu.roll(v, 1, 1))
    return jnp.where(lanes_of(v.shape) == LANES - 1, fill, pltpu.roll(v, LANES - 1, 1))


def shift_y(v, step, row):
    if step == 1:
        return jnp.where(subs_of(v.shape) == 0, row, pltpu.roll(v, 1, 0))
    return jnp.where(subs_of(v.shape) == 7, row, pltpu.roll(v, 7, 0))


def tile(ref, i, x):
    k = i * ROWS + x * 8
    return ref[k : k + 8, :]


def transposed(w_ref, b_ref, pad_ref):
    pad_ref[...] = jnp.zeros((HID, HID), F32)
    pad_ref[0:Q, :] = w_ref[...]
    if b_ref is not None:
        pad_ref[Q : Q + 1, :] = b_ref[...]
    return pad_ref[...]


def column(b_ref, n, pad_ref):
    pad_ref[...] = jnp.zeros((HID, HID), F32)
    pad_ref[:, 0:n] = jnp.broadcast_to(b_ref[...], (HID, n))
    return jnp.transpose(pad_ref[...])


def across(ref, r0, rows):
    return jnp.concatenate(
        [ref[pl.ds(r0 + j, KP, stride=ROWS), :] for j in range(rows)], axis=1
    )


def back(ref, r0, value):
    for j in range(value.shape[1] // LANES):
        ref[pl.ds(r0 + j, KP, stride=ROWS), :] = value[:, j * LANES : (j + 1) * LANES]


def fill_features(s_ref, f_ref):
    s_ref[0 : Q * ROWS, :] = f_ref[...]
    s_ref[Q * ROWS : (Q + 1) * ROWS, :] = jnp.ones((ROWS, LANES), F32)
    s_ref[(Q + 1) * ROWS :, :] = jnp.zeros(((KP - Q - 1) * ROWS, LANES), F32)


def wide(b):
    return jnp.concatenate([b] * (CH // LANES), axis=1)


def put_messages(value, orient, xp, xm, yp, ym, at, row):
    for k, i in enumerate(moving(0, 1, orient)):
        xp[at + 8 * k : at + 8 * k + 8, :] = value(i, 1)
    for k, i in enumerate(moving(0, -1, orient)):
        xm[at + 8 * k : at + 8 * k + 8, :] = value(i, 0)
    for k, i in enumerate(moving(1, 1, orient)):
        for x in range(2):
            yp[row + 2 * k + x : row + 2 * k + x + 1, :] = value(i, x)[7:8]
    for k, i in enumerate(moving(1, -1, orient)):
        for x in range(2):
            ym[row + 2 * k + x : row + 2 * k + x + 1, :] = value(i, x)[0:1]


def put_corners(leftward, rightward, orient, xp, xm, row, at):
    for sx, to in ((1, xp), (-1, xm)):
        for k, (sy, come) in enumerate(((1, leftward), (-1, rightward))):
            j = row + 2 * moving(1, sy, orient).index(diagonal(sx, sy, orient)) + (sx == 1)
            to[at + k : at + k + 1, :] = come[j : j + 1, :]


def streamed(ref, halo, orient, i, x):
    below, above, leftward, rightward, at, row, corner = halo
    sx, sy, sz = (orient * c for c in VELOCITIES[i])
    xs = x - sx
    if xs in (0, 1):
        v = tile(ref, i, xs)
    else:
        k = at + 8 * moving(0, sx, orient).index(i)
        v = (below if sx == 1 else above)[k : k + 8, :]
    if sy:
        if xs in (0, 1):
            k = row + 2 * moving(1, sy, orient).index(i) + xs
            edge = (leftward if sy == 1 else rightward)[k : k + 1, :]
        else:
            k = corner + (sy == -1)
            edge = (below if sx == 1 else above)[k : k + 1, :]
        v = shift_y(v, sy, edge)
    if sz:
        v = shift_z(v, sz, tile(ref, OPPOSITE[i], x))
    return v


def motion(ref, x):
    us = []
    for a in range(3):
        total = None
        for i in range(Q):
            c = VELOCITIES[i][a]
            if c:
                v = tile(ref, i, x)
                total = (v if c == 1 else -v) if total is None else (total + v if c == 1 else total - v)
        us.append(total)
    return us


def warm_neighbours(t_ref, rims, x):
    below, above, leftward, rightward = rims
    t = [t_ref[0:8, :], t_ref[8:16, :]]
    lower = below if x == 0 else t[0]
    upper = t[1] if x == 0 else above
    return [
        (upper, lower),
        (shift_y(t[x], -1, rightward[x]), shift_y(t[x], 1, leftward[x])),
        (shift_z(t[x], -1, COLD_WALL), shift_z(t[x], 1, HOT_WALL)),
    ]


def flux(u, a, s, liquid):
    return (CONDUCTIVITY - (0.5 * s) * u[a]) * liquid


def heat_adjoint(us, liquids, theta, codes, flux_rims):
    below, above, leftward, rightward = flux_rims
    out = []
    for x in range(2):
        u, liquid = us[x], liquids[x]
        total = 0.4 * liquid + jnp.where(codes[x] == 1, theta[x], 0.0)
        total = total + (below if x == 0 else flux(us[0], 0, 1, liquids[0]))
        total = total + (flux(us[1], 0, -1, liquids[1]) if x == 0 else above)
        total = total + shift_y(flux(u, 1, 1, liquid), 1, leftward[x])
        total = total + shift_y(flux(u, 1, -1, liquid), -1, rightward[x])
        total = total + shift_z(flux(u, 2, 1, liquid), 1, 0.0)
        total = total + shift_z(flux(u, 2, -1, liquid), -1, 0.0)
        out.append(total)
    return out


def motion_adjoint(t_ref, rims, liquids):
    return [
        [-0.5 * liquids[x] * (plus - minus) for plus, minus in warm_neighbours(t_ref, rims, x)]
        for x in range(2)
    ]


def with_motion(value, ubar, i):
    for a in range(3):
        c = VELOCITIES[i][a]
        if c:
            value = value + ubar[a] if c == 1 else value - ubar[a]
    return value


def hidden(fx, a1, a2, b2):
    h1 = jnp.tanh(product(a1, fx, HID))
    h1x = stacked(h1)
    h2 = jnp.tanh(product(a2, h1x, HID) + b2)
    return h1, h1x, h2


def network_back(fx, h1, h1x, h2, d, w3b, w2b, w1b, acc2, acc1, acc3, accb, first):
    dx = stacked(d)
    p2 = product(w3b, dx, HID) * (1.0 - h2 * h2)
    px = stacked(p2)
    p1 = product(w2b, px, HID) * (1.0 - h1 * h1)
    qx = stacked(p1)
    df = product(w1b, qx, KP)
    parts = (
        (acc2, nt(h1x, px)),
        (acc1, nt(fx, jnp.concatenate([qx, px], axis=0))),
        (acc3, nt(dx, stacked(h2))),
        (accb, sum(d[:, j * LANES : (j + 1) * LANES] for j in range(CH // LANES))),
    )
    for ref, value in parts:
        if first:
            ref[...] = value
        else:
            ref[...] = ref[...] + value
    return df


def write_pack(pack, acc2, acc1, acc3, accb, pad_ref):
    pack[0:HID, :] = four_blocks(acc2[...], HID)
    d = acc1[...]
    w1 = four_blocks(d[:, : 2 * HID], KP)
    pack[HID : HID + 24, :] = w1[0:24]
    d3 = acc3[...]
    w3 = four_blocks(d3, KP)
    pack[HID + 24 : HID + 48, :] = w3[0:24]
    b2 = four_blocks(d[:, 2 * HID :], KP)[Q : Q + 1]
    pad_ref[...] = jnp.zeros((HID, HID), F32)
    pad_ref[0:KP, :] = accb[...]
    b3 = jnp.sum(jnp.transpose(pad_ref[...]), axis=0, keepdims=True)
    pack[HID + 21 : HID + 22, :] = b2
    pack[HID + 22 : HID + 23, :] = b3


def forward_kernel(
    f, t, code, adj, w1, b1, w2, b2, w3, b3,
    post, h1s, h2s, xp, xm, yp, ym,
    feat, outs, pad,
):
    put_messages(lambda i, x: tile(adj, i, x), -1, xp, xm, yp, ym, 48, 12)
    fill_features(feat, f)
    l1 = left_narrow(jnp.transpose(transposed(w1, b1, pad)))
    l2 = left(jnp.transpose(w2[...]))
    pad[...] = jnp.zeros((HID, HID), F32)
    pad[0:Q, :] = w3[...]
    l3 = left(pad[0:KP, :])
    b2t = wide(column(b2, HID, pad))
    b3t = wide(column(b3, Q, pad)[0:KP])
    n = CH // LANES
    for c in range(ROWS * LANES // CH):
        fx = stacked(across(feat, c * n, n))
        h1, h1x, h2 = hidden(fx, l1, l2, b2t)
        h1s[c] = h1
        h2s[c] = h2
        back(outs, c * n, product(l3, stacked(h2), KP) + b3t)
    fluid = code[...] == 0
    warm = t[...]
    for i in range(Q):
        k = i * ROWS
        relaxed = f[k : k + ROWS, :] + outs[k : k + ROWS, :]
        if BUOYANCY[i]:
            relaxed = relaxed + BUOYANCY[i] * warm
        o = OPPOSITE[i] * ROWS
        post[k : k + ROWS, :] = jnp.where(fluid, relaxed, f[o : o + ROWS, :])
    put_messages(lambda i, x: tile(post, i, x), 1, xp, xm, yp, ym, 0, 0)
    xp[40:48, :] = t[8:16, :]
    xm[40:48, :] = t[0:8, :]
    for x in range(2):
        yp[10 + x : 11 + x, :] = t[8 * x + 7 : 8 * x + 8, :]
        ym[10 + x : 11 + x, :] = t[8 * x : 8 * x + 1, :]


def left_narrow(w):
    hi, lo = split(w + pltpu.roll(w, KP, 1))
    return jnp.concatenate([hi, lo], axis=0)[:, : 2 * KP]


def rims_of(below, above, leftward, rightward, at, row):
    return (
        below[at : at + 8, :],
        above[at : at + 8, :],
        [leftward[row + x : row + x + 1, :] for x in range(2)],
        [rightward[row + x : row + x + 1, :] for x in range(2)],
    )


def stream_kernel(
    post, f, t, code, theta, below, above, leftward, rightward,
    f1, t1, xp, xm, yp, ym,
):
    halo = (below, above, leftward, rightward, 0, 0, 88)
    for i in range(Q):
        for x in range(2):
            k = i * ROWS + 8 * x
            f1[k : k + 8, :] = streamed(post, halo, 1, i, x)
    rims = rims_of(below, above, leftward, rightward, 40, 10)
    for x in range(2):
        u = motion(f, x)
        here = t[8 * x : 8 * x + 8, :]
        total = 0.4 * here
        for a, (plus, minus) in enumerate(warm_neighbours(t, rims, x)):
            total = total + (CONDUCTIVITY - 0.5 * u[a]) * plus
            total = total + (CONDUCTIVITY + 0.5 * u[a]) * minus
        kind = code[8 * x : 8 * x + 8, :]
        new = jnp.where(kind == 0, total, jnp.where(kind == 1, here, HEATER))
        t1[8 * x : 8 * x + 8, :] = new
        liquid = jnp.where(kind == 0, theta[8 * x : 8 * x + 8, :], 0.0)
        un = motion(f1, x)
        if x == 0:
            xm[0:8, :] = new
            xm[8:16, :] = flux(un, 0, -1, liquid)
        else:
            xp[0:8, :] = new
            xp[8:16, :] = flux(un, 0, 1, liquid)
        yp[x : x + 1, :] = new[7:8]
        yp[2 + x : 3 + x, :] = flux(un, 1, 1, liquid)[7:8]
        ym[x : x + 1, :] = new[0:1]
        ym[2 + x : 3 + x, :] = flux(un, 1, -1, liquid)[0:1]


def collision_gradient(adj, halo, code, grad, masked, lift):
    for x in range(2):
        fluid = code[8 * x : 8 * x + 8, :] == 0
        total = None
        for i in range(Q):
            k = i * ROWS + 8 * x
            g = streamed(adj, halo, -1, i, x)
            grad[k : k + 8, :] = g
            g = jnp.where(fluid, g, 0.0)
            masked[k : k + 8, :] = g
            if BUOYANCY[i]:
                total = BUOYANCY[i] * g if total is None else total + BUOYANCY[i] * g
        lift[8 * x : 8 * x + 8, :] = total
    masked[Q * ROWS :, :] = jnp.zeros(((KP - Q) * ROWS, LANES), F32)


def back_weights(w1, w2, w3, pad):
    pad[...] = jnp.zeros((HID, HID), F32)
    pad[0:Q, :] = w3[...]
    w3b = left_narrow(jnp.transpose(pad[...]))
    w2b = left(w2[...])
    pad[...] = jnp.zeros((HID, HID), F32)
    pad[0:Q, :] = w1[...]
    w1b = left(pad[0:KP, :])
    return w3b, w2b, w1b


def last_step_kernel(
    f, adj, below, above, leftward, rightward, code, w1, b1, w2, b2, w3,
    fbar, lift, pack,
    feat, grad, masked, dfs, pad, acc2, acc1, acc3, accb,
):
    halo = (below, above, leftward, rightward, 48, 12, 90)
    collision_gradient(adj, halo, code, grad, masked, lift)
    fill_features(feat, f)
    l1 = left_narrow(jnp.transpose(transposed(w1, b1, pad)))
    l2 = left(jnp.transpose(w2[...]))
    b2t = wide(column(b2, HID, pad))
    w3b, w2b, w1b = back_weights(w1, w2, w3, pad)
    n = CH // LANES
    for c in range(ROWS * LANES // CH):
        fx = stacked(across(feat, c * n, n))
        h1, h1x, h2 = hidden(fx, l1, l2, b2t)
        d = across(masked, c * n, n)
        df = network_back(fx, h1, h1x, h2, d, w3b, w2b, w1b, acc2, acc1, acc3, accb, c == 0)
        back(dfs, c * n, df)
    fluid = code[...] == 0
    for i in range(Q):
        k, o = i * ROWS, OPPOSITE[i] * ROWS
        fbar[k : k + ROWS, :] = jnp.where(
            fluid, grad[k : k + ROWS, :] + dfs[k : k + ROWS, :], grad[o : o + ROWS, :]
        )
    write_pack(pack, acc2, acc1, acc3, accb, pad)


def halves(ref):
    return [ref[0:8, :], ref[8:16, :]]


def join_kernel(
    fbar, lift, f1, t1, f0, theta, code, below, above, leftward, rightward,
    adj, theta1, xp, xm, yp, ym,
):
    codes, thetas = halves(code), halves(theta)
    liquids = [jnp.where(k == 0, v, 0.0) for k, v in zip(codes, thetas)]
    rims = rims_of(below, above, leftward, rightward, 0, 0)
    flux_rims = rims_of(below, above, leftward, rightward, 8, 2)
    ubar = motion_adjoint(t1, rims, liquids)
    for i in range(Q):
        for x in range(2):
            k = i * ROWS + 8 * x
            adj[k : k + 8, :] = with_motion(fbar[k : k + 8, :], ubar[x], i)
    new = heat_adjoint([motion(f1, x) for x in range(2)], liquids, thetas, codes, flux_rims)
    for x in range(2):
        value = new[x] + lift[8 * x : 8 * x + 8, :]
        theta1[8 * x : 8 * x + 8, :] = value
        liquid = jnp.where(codes[x] == 0, value, 0.0)
        u = motion(f0, x)
        if x == 0:
            xm[40:48, :] = flux(u, 0, -1, liquid)
        else:
            xp[40:48, :] = flux(u, 0, 1, liquid)
        yp[10 + x : 11 + x, :] = flux(u, 1, 1, liquid)[7:8]
        ym[10 + x : 11 + x, :] = flux(u, 1, -1, liquid)[0:1]
    put_messages(lambda i, x: tile(adj, i, x), -1, xp, xm, yp, ym, 0, 0)


def first_step_kernel(
    scale,
    f, t, theta, adj, below, above, leftward, rightward,
    tbelow, tabove, tleft, tright, code, h1s, h2s, w1, w2, w3, pack1,
    fbar, thetabar, pack,
    feat, grad, masked, dfs, pad, acc2, acc1, acc3, accb, lift, total,
):
    halo = (below, above, leftward, rightward, 0, 0, 48)
    collision_gradient(adj, halo, code, grad, masked, lift)
    fill_features(feat, f)
    w3b, w2b, w1b = back_weights(w1, w2, w3, pad)
    n = CH // LANES
    for c in range(ROWS * LANES // CH):
        fx = stacked(across(feat, c * n, n))
        h1 = h1s[c]
        d = across(masked, c * n, n)
        df = network_back(
            fx, h1, stacked(h1), h2s[c], d, w3b, w2b, w1b, acc2, acc1, acc3, accb, c == 0
        )
        back(dfs, c * n, df)
    write_pack(total, acc2, acc1, acc3, accb, pad)
    parts, part, _ = pack.shape
    total[PACK:, :] = jnp.zeros((parts * part - PACK, HID), F32)
    total[0:PACK, :] = (total[0:PACK, :] + pack1[...]) * scale
    for k in range(parts):
        pack[k] = total[k * part : (k + 1) * part, :]
    codes, thetas = halves(code), halves(theta)
    liquids = [jnp.where(k == 0, v, 0.0) for k, v in zip(codes, thetas)]
    rims = rims_of(tbelow, tabove, tleft, tright, 40, 10)
    flux_rims = rims_of(below, above, leftward, rightward, 40, 10)
    ubar = motion_adjoint(t, rims, liquids)
    new = heat_adjoint([motion(f, x) for x in range(2)], liquids, thetas, codes, flux_rims)
    for x in range(2):
        thetabar[8 * x : 8 * x + 8, :] = new[x] + lift[8 * x : 8 * x + 8, :]
        fluid = codes[x] == 0
        for i in range(Q):
            k, o = i * ROWS + 8 * x, OPPOSITE[i] * ROWS + 8 * x
            value = jnp.where(fluid, grad[k : k + 8, :] + dfs[k : k + 8, :], grad[o : o + 8, :])
            fbar[k : k + 8, :] = with_motion(value, ubar[x], i)


def struct(*shape):
    return jax.ShapeDtypeStruct(shape, F32)


def call(kernel, outs, scratch, name):
    return pl.pallas_call(
        kernel,
        out_shape=outs,
        scratch_shapes=[pltpu.VMEM(s, F32) for s in scratch],
        compiler_params=pltpu.CompilerParams(vmem_limit_bytes=40 * 1024 * 1024),
        name=name,
    )


FULL = (KP * ROWS, LANES)
POPS = struct(Q * ROWS, LANES)
WARM = struct(ROWS, LANES)


def shifted(value, axis, by):
    count = lax.axis_size(axis)
    return lax.ppermute(value, axis, [(s, (s + by) % count) for s in range(count)])


def along(axis, plus, minus):
    return shifted(plus, axis, 1), shifted(minus, axis, -1)


def edge_kernel(blocks, xp, xm, leftward, rightward, xp_out, xm_out):
    xp_out[...] = xp[...]
    xm_out[...] = xm[...]
    for orient, row, at in blocks:
        put_corners(leftward, rightward, orient, xp_out, xm_out, row, at)


def exchange(xp, xm, yp, ym, blocks):
    leftward, rightward = along("gy", yp, ym)
    xp, xm = call(
        lambda *refs: edge_kernel(blocks, *refs),
        [struct(*xp.shape), struct(*xm.shape)],
        [],
        "edge",
    )(xp, xm, leftward, rightward)
    below, above = along("gx", xp, xm)
    return below, above, leftward, rightward


def swapped(value, groups):
    return lax.all_to_all(
        value, ("gx", "gy"), 0, 0, axis_index_groups=groups, tiled=True
    )


def outer_of(nx):
    return nx // 24 if nx % 24 == 0 else (2 if nx % 2 == 0 else 1)


def groups_of(nx, ny):
    outer = outer_of(nx)
    at = np.arange(nx * ny).reshape(outer, nx // outer, ny)
    return (
        at.transpose(1, 0, 2).reshape(nx // outer, outer * ny).tolist(),
        at.transpose(0, 2, 1).reshape(outer * ny, nx // outer).tolist(),
    )


def total_kernel(parts, out):
    value = parts[0]
    for k in range(1, parts.shape[0]):
        value = value + parts[k]
    for k in range(out.shape[0]):
        out[k] = value


def summed(parts, copies):
    return call(total_kernel, struct(copies, *parts.shape[1:]), [], "total")(parts)


def reduced(pack):
    share, same = groups_of(lax.axis_size("gx"), lax.axis_size("gy"))
    part = summed(swapped(pack, share), len(same[0]))
    part = summed(swapped(part, same), len(share[0]))
    return swapped(part, share)


def unpack_kernel(parts, w1, b1, w2, b2, w3, b3, pack):
    count, part, _ = parts.shape
    for k in range(count):
        pack[k * part : (k + 1) * part, :] = parts[k]
    w2[...] = pack[0:HID, :]
    w1[...] = pack[HID : HID + Q, :]
    b1[...] = pack[HID + Q : HID + Q + 1, :]
    b2[...] = pack[HID + 21 : HID + 22, :]
    b3[...] = pack[HID + 22 : HID + 23, 0:Q]
    w3[...] = pack[HID + 24 : HID + 24 + Q, :]


def per_device(f, t, code, w1, b1, w2, b2, w3, b3, adj, theta):
    sx, sy, sz = t.shape
    cells = sx * lax.axis_size("gx") * sy * lax.axis_size("gy") * sz
    f, adj = f.reshape(Q * ROWS, LANES), adj.reshape(Q * ROWS, LANES)
    t, code, theta = (v.reshape(ROWS, LANES) for v in (t, code, theta))
    b1, b2, b3 = (v.reshape(1, -1) for v in (b1, b2, b3))
    w3 = w3.T
    chunks = struct(ROWS * LANES // CH, HID, CH)
    outs = call(
        forward_kernel,
        [POPS, chunks, chunks, struct(96, LANES), struct(96, LANES), struct(24, LANES), struct(24, LANES)],
        [FULL, FULL, (HID, HID)],
        "forward",
    )(f, t, code, adj, w1, b1, w2, b2, w3, b3)
    post, h1s, h2s = outs[:3]
    halo0 = exchange(*outs[3:], ((1, 0, 88), (-1, 12, 90)))
    f1, t1, *rim_messages = call(
        stream_kernel,
        [POPS, WARM, struct(16, LANES), struct(16, LANES), struct(8, LANES), struct(8, LANES)],
        [],
        "stream",
    )(post, f, t, code, theta, *halo0)
    left1, right1 = along("gy", *rim_messages[2:])
    rims1 = (*along("gx", *rim_messages[:2]), left1, right1)
    accs = [(2 * HID, 2 * HID), (2 * KP, 4 * HID), (2 * KP, 2 * HID), (KP, LANES)]
    fbar, lift, pack1 = call(
        last_step_kernel,
        [POPS, WARM, struct(PACK, HID)],
        [FULL, (Q * ROWS, LANES), FULL, FULL, (HID, HID), *accs],
        "last_step",
    )(f1, adj, *halo0, code, w1, b1, w2, b2, w3)
    adj1, theta1, *messages = call(
        join_kernel,
        [POPS, WARM, struct(56, LANES), struct(56, LANES), struct(16, LANES), struct(16, LANES)],
        [],
        "join",
    )(fbar, lift, f1, t1, f, theta, code, *rims1)
    halo1 = exchange(*messages, ((-1, 0, 48),))
    scale = 1.0 / math.sqrt(cells)
    parts = outer_of(lax.axis_size("gx")) * lax.axis_size("gy")
    part = -(-(PACK + 8) // parts)
    fbar0, theta0, pack = call(
        lambda *refs: first_step_kernel(scale, *refs),
        [POPS, WARM, struct(parts, part, HID)],
        [FULL, (Q * ROWS, LANES), FULL, FULL, (HID, HID), *accs, (ROWS, LANES), (parts * part, HID)],
        "first_step",
    )(f, t, theta1, adj1, *halo1, *halo0, code, h1s, h2s, w1, w2, w3, pack1)
    total = reduced(pack)
    g1, gb1, g2, gb2, g3, gb3 = call(
        unpack_kernel,
        [struct(Q, HID), struct(1, HID), struct(HID, HID), struct(1, HID), struct(Q, HID), struct(1, Q)],
        [(parts * part, HID)],
        "unpack",
    )(total)
    return (
        fbar0.reshape(Q, sx, sy, sz),
        theta0.reshape(sx, sy, sz),
        g1,
        gb1.reshape(HID),
        g2,
        gb2.reshape(HID),
        g3.T,
        gb3.reshape(Q),
    )


def solution(mesh):
    pops, cells = P(None, "gx", "gy", None), P("gx", "gy", None)
    return jax.shard_map(
        per_device,
        mesh=mesh,
        in_specs=(pops, cells, cells, P(), P(), P(), P(), P(), P(), pops, cells),
        out_specs=(pops, cells, P(), P(), P(), P(), P(), P()),
        check_vma=False,
    )
```

time: 712 us -> 152 us (0.21)
  waiting for transfers between devices: 469 us -> 3.72 us
  local copies, waits for them, and re-layouts: 76.5 us -> 5.48 us
  blocking collectives: 0 us -> 57 us
  matrix products: 27.8 us -> 0 us
  other arithmetic: 26.7 us -> 0 us
  starting transfers between devices: 92.1 us -> 73 us
  between operations: 16.5 us -> 0.92 us
  Pallas kernels: 0 us -> 11.5 us
    psum x1 -> x0, waiting for transfers between devices: 443 us -> none  [in_one(): running = lax.psum(jnp.concatenate([a.ravel() for a in arrays]), axis)]
    all_to_all x0 -> x3, blocking collectives: none -> 57 us  [swapped(): lax.all_to_all(value, ('gx', 'gy'), 0, 0, axis_index_groups=groups, tiled...]
    unnamed x336 -> x34, local copies, waits for them, and re-layouts: 37.8 us -> 5.48 us
    dot_general x22 -> x0, matrix products: 27.8 us -> none  [the longest x6 9.54 us: collide(): lax.dot_general(exit_level_matrix, hidden_two, CONTRACT, precision=PRECIS...]
    ppermute x16 -> x12, waiting for transfers between devices: 25.9 us -> 3.72 us  [shifted(): lax.ppermute(value, axis, [(s, (s + by) % count) for s in range(count)])]
    ppermute x16 -> x12, starting transfers between devices: 92.1 us -> 73 us  [shifted(): lax.ppermute(value, axis, [(s, (s + by) % count) for s in range(count)])]
    gather x22 -> x0, local copies, waits for them, and re-layouts: 13.5 us -> none  [the longest x8 3.68 us: face_exchange(): values[np.array(lower_first), span_along_x - 1]]
    pallas_call x0 -> x10, Pallas kernels: none -> 11.5 us  [the longest x1 4.58 us: per_device(): call(last_step_kernel, [POPS, WARM, struct(PACK, HID)], [FULL, (Q * ROWS,...]
  transfers between devices with their start and end apart: 17 -> 12, of which waited for: 8 -> 4; matrix products, arithmetic and copies ran while one was open for 3% -> 0% of each run, Pallas kernels for 0% -> 3%
where the time goes in v1:
time: 152 us
  starting transfers between devices  73 us (48%)
  blocking collectives  57 us (38%)
  Pallas kernels  11.5 us (8%)
  local copies, waits for them, and re-layouts  5.48 us (4%)
  waiting for transfers between devices  3.72 us (2%)
    ppermute x12, starting transfers between devices, shifted(): lax.ppermute(value, axis, [(s, (s + by) % count) for s in range(count)])  73 us
    all_to_all x3, blocking collectives, swapped(): lax.all_to_all(value, ('gx', 'gy'), 0, 0, axis_index_groups=groups, tiled...  57 us
    unnamed x34, local copies, waits for them, and re-layouts  5.48 us
    pallas_call x1, Pallas kernels, per_device(): call(last_step_kernel, [POPS, WARM, struct(PACK, HID)], [FULL, (Q * ROWS,...  4.58 us
    pallas_call x1, Pallas kernels, per_device(): call(lambda *refs: first_step_kernel(scale, *refs), [POPS, WARM, struct(p...  3.8 us
    ppermute x12, waiting for transfers between devices, shifted(): lax.ppermute(value, axis, [(s, (s + by) % count) for s in range(count)])  3.72 us
  transfers between devices with their start and end apart: 12, of which 4 were waited for; matrix products, arithmetic and copies ran while one was open for 0% of the time, Pallas kernels for 3%

profile of v1, /device:TPU:1, one launch (start us, length us, event | category | flops | bytes accessed | tf_op | source)
XLA Modules:
  0.0 151.6 jit_solution(7694796953309802557)
XLA Ops:
  0.7 0.7 copy-done.6
  1.3 0.9 copy-done
  2.3 0.9 copy-done.2
  3.2 0.8 copy-done.4
  4.0 0.7 copy-done.7
  4.7 0.7 copy-done.9
  5.4 0.7 copy-done.11
  6.1 2.2 %forward.1 = (f32[304,128]{1,0:T(8,128)S(1)}, f32[4,128,512]{2,1,0:T(8,128)S(1)}, f32[4,128,512]{2,1,0:T(8,128)S(1)}, f32[96,128]{1,0:T(8,128)S(1)}, f32[96,128]...) custom-call(f32[304,128]{1,0:T(8,128)S(1)} %bitcast.15, f32[16,128]{1,0:T(8,128)S(1)} %bitcast.29, ...), custom_call_target="tpu_custom_call" | custom-call | tf_op jit(solution)/shard_map/forward/pallas_call | solution.py:601
  8.3 4.6 %collective-permute-start = (f32[24,128]{1,0:T(8,128)S(1)}, f32[24,128]{1,0:T(8,128)S(1)}, u32[]{:S(2)}, u32[]{:S(2)}) collective-permute-start(f32[24,128]{1,0:T(8,128)S(1)} %get-tuple-element.46), channel_id=1, source_target_pairs={{0,1},{1,2},{2,3},{3,4},{4,5},{5,6},{6,7},{7,0},{8,9},{9,10},{10,1... | collective-permute-start | bytes 36872 | tf_op jit(solution)/shard_map/ppermute | solution.py:517
  12.9 9.7 %collective-permute-start.1 = (f32[24,128]{1,0:T(8,128)S(1)}, f32[24,128]{1,0:T(8,128)S(1)}, u32[]{:S(2)}, u32[]{:S(2)}) collective-permute-start(f32[24,128]{1,0:T(8,128)S(1)} %get-tuple-element.47), channel_id=1, source_target_pairs={{0,7},{1,0},{2,1},{3,2},{4,3},{5,4},{6,5},{7,6},{8,15},{9,8},{10,9... | collective-permute-start | bytes 36872 | tf_op jit(solution)/shard_map/ppermute | solution.py:517
  22.6 0.8 collective-permute-done.1.refs_3_.rightward.refs_11_
  23.5 2.1 %collective-permute-start.2 = (f32[96,128]{1,0:T(8,128)S(1)}, f32[96,128]{1,0:T(8,128)S(1)}, u32[]{:S(2)}, u32[]{:S(2)}) collective-permute-start(f32[96,128]{1,0:T(8,128)S(1)} %get-tuple-element.48), channel_id=1, source_target_pairs={{0,8},{8,16},{16,24},{24,32},{32,40},{40,48},{48,56},{56,64},{64,7... | collective-permute-start | bytes 147464 | tf_op jit(solution)/shard_map/ppermute | solution.py:517
  25.5 15.3 %collective-permute-start.3 = (f32[96,128]{1,0:T(8,128)S(1)}, f32[96,128]{1,0:T(8,128)S(1)}, u32[]{:S(2)}, u32[]{:S(2)}) collective-permute-start(f32[96,128]{1,0:T(8,128)S(1)} %get-tuple-element.49), channel_id=1, source_target_pairs={{0,760},{8,0},{16,8},{24,16},{32,24},{40,32},{48,40},{56,48},{64,5... | collective-permute-start | bytes 147464 | tf_op jit(solution)/shard_map/ppermute | solution.py:517
  40.9 1.1 collective-permute-done.3.above.refs_9_
  42.1 0.1 stream.1
  42.2 1.9 %collective-permute-start.4 = (f32[16,128]{1,0:T(8,128)S(1)}, f32[16,128]{1,0:T(8,128)S(1)}, u32[]{:S(2)}, u32[]{:S(2)}) collective-permute-start(f32[16,128]{1,0:T(8,128)S(1)} %get-tuple-element.54), channel_id=1, source_target_pairs={{0,8},{8,16},{16,24},{24,32},{32,40},{40,48},{48,56},{56,64},{64,7... | collective-permute-start | bytes 24584 | tf_op jit(solution)/shard_map/ppermute | solution.py:517
  44.1 12.1 %collective-permute-start.5 = (f32[16,128]{1,0:T(8,128)S(1)}, f32[16,128]{1,0:T(8,128)S(1)}, u32[]{:S(2)}, u32[]{:S(2)}) collective-permute-start(f32[16,128]{1,0:T(8,128)S(1)} %get-tuple-element.55), channel_id=1, source_target_pairs={{0,760},{8,0},{16,8},{24,16},{32,24},{40,32},{48,40},{56,48},{64,5... | collective-permute-start | bytes 24584 | tf_op jit(solution)/shard_map/ppermute | solution.py:517
  56.2 3.5 %collective-permute-start.6 = (f32[8,128]{1,0:T(8,128)S(1)}, f32[8,128]{1,0:T(8,128)S(1)}, u32[]{:S(2)}, u32[]{:S(2)}) collective-permute-start(f32[8,128]{1,0:T(8,128)S(1)} %get-tuple-element.56), channel_id=1, source_target_pairs={{0,1},{1,2},{2,3},{3,4},{4,5},{5,6},{6,7},{7,0},{8,9},{9,10},{10,1... | collective-permute-start | bytes 12296 | tf_op jit(solution)/shard_map/ppermute | solution.py:517
  59.7 3.0 %collective-permute-start.7 = (f32[8,128]{1,0:T(8,128)S(1)}, f32[8,128]{1,0:T(8,128)S(1)}, u32[]{:S(2)}, u32[]{:S(2)}) collective-permute-start(f32[8,128]{1,0:T(8,128)S(1)} %get-tuple-element.57), channel_id=1, source_target_pairs={{0,7},{1,0},{2,1},{3,2},{4,3},{5,4},{6,5},{7,6},{8,15},{9,8},{10,9... | collective-permute-start | bytes 12296 | tf_op jit(solution)/shard_map/ppermute | solution.py:517
  62.8 4.6 %last_step.1 = (f32[304,128]{1,0:T(8,128)S(1)}, f32[16,128]{1,0:T(8,128)S(1)}, f32[176,128]{1,0:T(8,128)S(1)}) custom-call(f32[304,128]{1,0:T(8,128)S(1)} %get-tuple-element.50.f.f1, f32[304,128]{1,0:T(8,128)S(1)} %bitcast.20, f32[96,128]{1,0:T(8,128)S(1)} %collective-permute-done.2.below.refs_8_, f32[96,128]{1,0:T(8,128)S(1)} %collective-permute-done.3.above.refs_9_, ...), custom_call_target="tpu_custom_call" | custom-call | tf_op jit(solution)/shard_map/last_step/pallas_call | solution.py:618
  67.4 0.1 join.1
  67.5 2.5 %collective-permute-start.8 = (f32[16,128]{1,0:T(8,128)S(1)}, f32[16,128]{1,0:T(8,128)S(1)}, u32[]{:S(2)}, u32[]{:S(2)}) collective-permute-start(f32[16,128]{1,0:T(8,128)S(1)} %get-tuple-element.62), channel_id=1, source_target_pairs={{0,1},{1,2},{2,3},{3,4},{4,5},{5,6},{6,7},{7,0},{8,9},{9,10},{10,1... | collective-permute-start | bytes 24584 | tf_op jit(solution)/shard_map/ppermute | solution.py:517
  70.1 4.8 %collective-permute-start.9 = (f32[16,128]{1,0:T(8,128)S(1)}, f32[16,128]{1,0:T(8,128)S(1)}, u32[]{:S(2)}, u32[]{:S(2)}) collective-permute-start(f32[16,128]{1,0:T(8,128)S(1)} %get-tuple-element.63), channel_id=1, source_target_pairs={{0,7},{1,0},{2,1},{3,2},{4,3},{5,4},{6,5},{7,6},{8,15},{9,8},{10,9... | collective-permute-start | bytes 24584 | tf_op jit(solution)/shard_map/ppermute | solution.py:517
  74.9 0.8 collective-permute-done.9.refs_3_.refs_7_
  75.7 1.9 %collective-permute-start.10 = (f32[56,128]{1,0:T(8,128)S(1)}, f32[56,128]{1,0:T(8,128)S(1)}, u32[]{:S(2)}, u32[]{:S(2)}) collective-permute-start(f32[56,128]{1,0:T(8,128)S(1)} %get-tuple-element.64), channel_id=1, source_target_pairs={{0,8},{8,16},{16,24},{24,32},{32,40},{40,48},{48,56},{56,64},{64,7... | collective-permute-start | bytes 86024 | tf_op jit(solution)/shard_map/ppermute | solution.py:517
  77.6 11.5 %collective-permute-start.11 = (f32[56,128]{1,0:T(8,128)S(1)}, f32[56,128]{1,0:T(8,128)S(1)}, u32[]{:S(2)}, u32[]{:S(2)}) collective-permute-start(f32[56,128]{1,0:T(8,128)S(1)} %get-tuple-element.65), channel_id=1, source_target_pairs={{0,760},{8,0},{16,8},{24,16},{32,24},{40,32},{48,40},{56,48},{64,5... | collective-permute-start | bytes 86024 | tf_op jit(solution)/shard_map/ppermute | solution.py:517
  89.1 1.0 collective-permute-done.11.refs_5_
  90.1 3.8 %first_step.1 = (f32[304,128]{1,0:T(8,128)}, f32[16,128]{1,0:T(8,128)}, f32[32,6,128]{2,1,0:T(8,128)S(1)}) custom-call(f32[304,128]{1,0:T(8,128)S(1)} %bitcast.18, f32[16,128]{1,0:T(8,128)S(1)} %bitcast.31, f32[16,128]{1,0:T(8,128)S(1)} %get-tuple-element.58.refs_2_, f32[304,128]{1,0:T(8,128)S(1)} %get-tuple-element.59.refs_3_, ...), custom_call_target="tpu_custom_call" | custom-call | tf_op jit(solution)/shard_map/first_step/pallas_call | solution.py:634
  93.9 17.5 %all_to_all.15.parts = f32[32,6,128]{2,1,0:T(8,128)S(1)} all-to-all(f32[32,6,128]{2,1,0:T(8,128)S(1)} %get-tuple-element.71), channel_id=1, replica_groups={{0,1,2,3,4,5,6,7,192,193,194,195,196,197,198,199,384,385,386,387,388,38..., dimensions={0} | all-to-all | bytes 196608 | tf_op jit(solution)/shard_map/all_to_all | solution.py:544
  111.4 25.2 %all_to_all.16.parts = f32[24,6,128]{2,1,0:T(8,128)S(1)} all-to-all(f32[24,6,128]{2,1,0:T(8,128)S(1)} %total.2), channel_id=1, replica_groups={{0,8,16,24,32,40,48,56,64,72,80,88,96,104,112,120,128,136,144,152,160,1..., dimensions={0} | all-to-all | bytes 147456 | tf_op jit(solution)/shard_map/all_to_all | solution.py:544
  136.7 14.3 %all_to_all.17.parts = f32[32,6,128]{2,1,0:T(8,128)S(1)} all-to-all(f32[32,6,128]{2,1,0:T(8,128)S(1)} %total.3), channel_id=1, replica_groups={{0,1,2,3,4,5,6,7,192,193,194,195,196,197,198,199,384,385,386,387,388,38..., dimensions={0} | all-to-all | bytes 196608 | tf_op jit(solution)/shard_map/all_to_all | solution.py:544
  150.9 0.7 unpack.1
  (39 shorter events, 0.2 us)
Async XLA Ops:
  0.6 0.7 copy-start.6
  0.6 0.7 copy-start.14
  0.7 0.7 copy-start.15
  0.7 0.7 copy-start.16
  1.3 0.9 copy-start
  2.3 0.9 copy-start.2
  3.2 0.8 copy-start.4
  4.0 0.7 copy-start.7
  4.7 0.7 copy-start.9
  5.4 0.7 copy-start.11
  6.1 35.9 %copy-start.1 = (f32[19,2,8,128]{3,2,1,0:T(8,128)S(1)}, f32[19,2,8,128]{3,2,1,0:T(8,128)}, u32[]{:S(2)}) copy-start(f32[19,2,8,128]{3,2,1,0:T(8,128)} %param.11) | copy-start | bytes 466948
  8.3 14.3 %collective-permute-start = (f32[24,128]{1,0:T(8,128)S(1)}, f32[24,128]{1,0:T(8,128)S(1)}, u32[]{:S(2)}, u32[]{:S(2)}) collective-permute-start(f32[24,128]{1,0:T(8,128)S(1)} %get-tuple-element.46), channel_id=1, source_target_pairs={{0,1},{1,2},{2,3},{3,4},{4,5},{5,6},{6,7},{7,0},{8,9},{9,10},{10,1... | collective-permute-start | bytes 36872 | tf_op jit(solution)/shard_map/ppermute | solution.py:517
  12.9 10.5 %collective-permute-start.1 = (f32[24,128]{1,0:T(8,128)S(1)}, f32[24,128]{1,0:T(8,128)S(1)}, u32[]{:S(2)}, u32[]{:S(2)}) collective-permute-start(f32[24,128]{1,0:T(8,128)S(1)} %get-tuple-element.47), channel_id=1, source_target_pairs={{0,7},{1,0},{2,1},{3,2},{4,3},{5,4},{6,5},{7,6},{8,15},{9,8},{10,9... | collective-permute-start | bytes 36872 | tf_op jit(solution)/shard_map/ppermute | solution.py:517
  23.4 18.6 %copy-start.12 = (f32[2,8,128]{2,1,0:T(8,128)S(1)}, f32[2,8,128]{2,1,0:T(8,128)}, u32[]{:S(2)}) copy-start(f32[2,8,128]{2,1,0:T(8,128)} %param.12) | copy-start | bytes 24580
  23.4 18.6 %copy-start.13 = (f32[2,8,128]{2,1,0:T(8,128)S(1)}, f32[2,8,128]{2,1,0:T(8,128)}, u32[]{:S(2)}) copy-start(f32[2,8,128]{2,1,0:T(8,128)} %param.21) | copy-start | bytes 24580
  23.5 17.4 %collective-permute-start.2 = (f32[96,128]{1,0:T(8,128)S(1)}, f32[96,128]{1,0:T(8,128)S(1)}, u32[]{:S(2)}, u32[]{:S(2)}) collective-permute-start(f32[96,128]{1,0:T(8,128)S(1)} %get-tuple-element.48), channel_id=1, source_target_pairs={{0,8},{8,16},{16,24},{24,32},{32,40},{40,48},{48,56},{56,64},{64,7... | collective-permute-start | bytes 147464 | tf_op jit(solution)/shard_map/ppermute | solution.py:517
  25.5 16.5 %collective-permute-start.3 = (f32[96,128]{1,0:T(8,128)S(1)}, f32[96,128]{1,0:T(8,128)S(1)}, u32[]{:S(2)}, u32[]{:S(2)}) collective-permute-start(f32[96,128]{1,0:T(8,128)S(1)} %get-tuple-element.49), channel_id=1, source_target_pairs={{0,760},{8,0},{16,8},{24,16},{32,24},{40,32},{48,40},{56,48},{64,5... | collective-permute-start | bytes 147464 | tf_op jit(solution)/shard_map/ppermute | solution.py:517
  42.0 20.7 %copy-start.3 = (f32[19,2,8,128]{3,2,1,0:T(8,128)S(1)}, f32[19,2,8,128]{3,2,1,0:T(8,128)}, u32[]{:S(2)}) copy-start(f32[19,2,8,128]{3,2,1,0:T(8,128)} %param.20) | copy-start | bytes 466948
  42.0 20.7 %copy-start.5 = (f32[128,128]{1,0:T(8,128)S(1)}, f32[128,128]{1,0:T(8,128)}, u32[]{:S(2)}) copy-start(f32[128,128]{1,0:T(8,128)} %refs_16_.1) | copy-start | bytes 196612
  42.1 20.7 %copy-start.8 = (f32[19,128]{1,0:T(8,128)S(1)}, f32[19,128]{1,0:T(8,128)}, u32[]{:S(2)}) copy-start(f32[19,128]{1,0:T(8,128)} %refs_15_.1) | copy-start | bytes 29188
  42.1 20.7 %copy-start.10 = (f32[128,19]{0,1:T(8,128)S(1)}, f32[128,19]{0,1:T(8,128)}, u32[]{:S(2)}) copy-start(f32[128,19]{0,1:T(8,128)} %param.18) | copy-start | bytes 29188
  42.2 25.2 %collective-permute-start.4 = (f32[16,128]{1,0:T(8,128)S(1)}, f32[16,128]{1,0:T(8,128)S(1)}, u32[]{:S(2)}, u32[]{:S(2)}) collective-permute-start(f32[16,128]{1,0:T(8,128)S(1)} %get-tuple-element.54), channel_id=1, source_target_pairs={{0,8},{8,16},{16,24},{24,32},{32,40},{40,48},{48,56},{56,64},{64,7... | collective-permute-start | bytes 24584 | tf_op jit(solution)/shard_map/ppermute | solution.py:517
  44.1 23.3 %collective-permute-start.5 = (f32[16,128]{1,0:T(8,128)S(1)}, f32[16,128]{1,0:T(8,128)S(1)}, u32[]{:S(2)}, u32[]{:S(2)}) collective-permute-start(f32[16,128]{1,0:T(8,128)S(1)} %get-tuple-element.55), channel_id=1, source_target_pairs={{0,760},{8,0},{16,8},{24,16},{32,24},{40,32},{48,40},{56,48},{64,5... | collective-permute-start | bytes 24584 | tf_op jit(solution)/shard_map/ppermute | solution.py:517
  56.2 11.2 %collective-permute-start.6 = (f32[8,128]{1,0:T(8,128)S(1)}, f32[8,128]{1,0:T(8,128)S(1)}, u32[]{:S(2)}, u32[]{:S(2)}) collective-permute-start(f32[8,128]{1,0:T(8,128)S(1)} %get-tuple-element.56), channel_id=1, source_target_pairs={{0,1},{1,2},{2,3},{3,4},{4,5},{5,6},{6,7},{7,0},{8,9},{9,10},{10,1... | collective-permute-start | bytes 12296 | tf_op jit(solution)/shard_map/ppermute | solution.py:517
  59.7 7.7 %collective-permute-start.7 = (f32[8,128]{1,0:T(8,128)S(1)}, f32[8,128]{1,0:T(8,128)S(1)}, u32[]{:S(2)}, u32[]{:S(2)}) collective-permute-start(f32[8,128]{1,0:T(8,128)S(1)} %get-tuple-element.57), channel_id=1, source_target_pairs={{0,7},{1,0},{2,1},{3,2},{4,3},{5,4},{6,5},{7,6},{8,15},{9,8},{10,9... | collective-permute-start | bytes 12296 | tf_op jit(solution)/shard_map/ppermute | solution.py:517
  67.5 7.4 %collective-permute-start.8 = (f32[16,128]{1,0:T(8,128)S(1)}, f32[16,128]{1,0:T(8,128)S(1)}, u32[]{:S(2)}, u32[]{:S(2)}) collective-permute-start(f32[16,128]{1,0:T(8,128)S(1)} %get-tuple-element.62), channel_id=1, source_target_pairs={{0,1},{1,2},{2,3},{3,4},{4,5},{5,6},{6,7},{7,0},{8,9},{9,10},{10,1... | collective-permute-start | bytes 24584 | tf_op jit(solution)/shard_map/ppermute | solution.py:517
  70.1 5.6 %collective-permute-start.9 = (f32[16,128]{1,0:T(8,128)S(1)}, f32[16,128]{1,0:T(8,128)S(1)}, u32[]{:S(2)}, u32[]{:S(2)}) collective-permute-start(f32[16,128]{1,0:T(8,128)S(1)} %get-tuple-element.63), channel_id=1, source_target_pairs={{0,7},{1,0},{2,1},{3,2},{4,3},{5,4},{6,5},{7,6},{8,15},{9,8},{10,9... | collective-permute-start | bytes 24584 | tf_op jit(solution)/shard_map/ppermute | solution.py:517
  75.7 13.4 %collective-permute-start.10 = (f32[56,128]{1,0:T(8,128)S(1)}, f32[56,128]{1,0:T(8,128)S(1)}, u32[]{:S(2)}, u32[]{:S(2)}) collective-permute-start(f32[56,128]{1,0:T(8,128)S(1)} %get-tuple-element.64), channel_id=1, source_target_pairs={{0,8},{8,16},{16,24},{24,32},{32,40},{40,48},{48,56},{56,64},{64,7... | collective-permute-start | bytes 86024 | tf_op jit(solution)/shard_map/ppermute | solution.py:517
  77.6 12.5 %collective-permute-start.11 = (f32[56,128]{1,0:T(8,128)S(1)}, f32[56,128]{1,0:T(8,128)S(1)}, u32[]{:S(2)}, u32[]{:S(2)}) collective-permute-start(f32[56,128]{1,0:T(8,128)S(1)} %get-tuple-element.65), channel_id=1, source_target_pairs={{0,760},{8,0},{16,8},{24,16},{32,24},{40,32},{48,40},{56,48},{64,5... | collective-permute-start | bytes 86024 | tf_op jit(solution)/shard_map/ppermute | solution.py:517

commit v2 on v1

--- a/solution.py
+++ b/solution.py
@@ -280,12 +280,17 @@
 
 
 def forward_kernel(
-    f, t, code, adj, w1, b1, w2, b2, w3, b3,
+    f_in, t_in, code_in, adj_in, w1_in, b1_in, w2_in, b2_in, w3_in, b3_in,
     post, h1s, h2s, xp, xm, yp, ym,
-    feat, outs, pad,
+    feat, outs, pad, f, t, code, adj, w1, b1, w2, b2, w3, b3, sems,
 ):
-    put_messages(lambda i, x: tile(adj, i, x), -1, xp, xm, yp, ym, 48, 12)
-    fill_features(feat, f)
+    ins = (w1_in, b1_in, w2_in, b2_in, w3_in, b3_in, f_in, t_in, code_in, adj_in)
+    here = (w1, b1, w2, b2, w3, b3, f, t, code, adj)
+    copies = [pltpu.make_async_copy(a, b, sems.at[k]) for k, (a, b) in enumerate(zip(ins, here))]
+    for c in copies:
+        c.start()
+    for c in copies[:6]:
+        c.wait()
     l1 = left_narrow(jnp.transpose(transposed(w1, b1, pad)))
     l2 = left(jnp.transpose(w2[...]))
     pad[...] = jnp.zeros((HID, HID), F32)
@@ -293,6 +298,8 @@
     l3 = left(pad[0:KP, :])
     b2t = wide(column(b2, HID, pad))
     b3t = wide(column(b3, Q, pad)[0:KP])
+    copies[6].wait()
+    fill_features(feat, f)
     n = CH // LANES
     for c in range(ROWS * LANES // CH):
         fx = stacked(across(feat, c * n, n))
@@ -300,6 +307,9 @@
         h1s[c] = h1
         h2s[c] = h2
         back(outs, c * n, product(l3, stacked(h2), KP) + b3t)
+    for c in copies[7:]:
+        c.wait()
+    put_messages(lambda i, x: tile(adj, i, x), -1, xp, xm, yp, ym, 48, 12)
     fluid = code[...] == 0
     warm = t[...]
     for i in range(Q):
@@ -331,10 +341,7 @@
     )
 
 
-def stream_kernel(
-    post, f, t, code, theta, below, above, leftward, rightward,
-    f1, t1, xp, xm, yp, ym,
-):
+def stream_kernel(post, f, t, code, below, above, leftward, rightward, f1, t1):
     halo = (below, above, leftward, rightward, 0, 0, 88)
     for i in range(Q):
         for x in range(2):
@@ -349,20 +356,9 @@
             total = total + (CONDUCTIVITY - 0.5 * u[a]) * plus
             total = total + (CONDUCTIVITY + 0.5 * u[a]) * minus
         kind = code[8 * x : 8 * x + 8, :]
-        new = jnp.where(kind == 0, total, jnp.where(kind == 1, here, HEATER))
-        t1[8 * x : 8 * x + 8, :] = new
-        liquid = jnp.where(kind == 0, theta[8 * x : 8 * x + 8, :], 0.0)
-        un = motion(f1, x)
-        if x == 0:
-            xm[0:8, :] = new
-            xm[8:16, :] = flux(un, 0, -1, liquid)
-        else:
-            xp[0:8, :] = new
-            xp[8:16, :] = flux(un, 0, 1, liquid)
-        yp[x : x + 1, :] = new[7:8]
-        yp[2 + x : 3 + x, :] = flux(un, 1, 1, liquid)[7:8]
-        ym[x : x + 1, :] = new[0:1]
-        ym[2 + x : 3 + x, :] = flux(un, 1, -1, liquid)[0:1]
+        t1[8 * x : 8 * x + 8, :] = jnp.where(
+            kind == 0, total, jnp.where(kind == 1, here, HEATER)
+        )
 
 
 def collision_gradient(adj, halo, code, grad, masked, lift):
@@ -424,42 +420,152 @@
     return [ref[0:8, :], ref[8:16, :]]
 
 
-def join_kernel(
-    fbar, lift, f1, t1, f0, theta, code, below, above, leftward, rightward,
-    adj, theta1, xp, xm, yp, ym,
-):
+def coefficient(u, a, s, kind):
+    return jnp.where(kind == 0, CONDUCTIVITY - (0.5 * s) * u[a], 0.0)
+
+
+def adjoint_parts(fbar, lift, f1, t1, theta, code, t_rims, flux_rims):
     codes, thetas = halves(code), halves(theta)
     liquids = [jnp.where(k == 0, v, 0.0) for k, v in zip(codes, thetas)]
-    rims = rims_of(below, above, leftward, rightward, 0, 0)
-    flux_rims = rims_of(below, above, leftward, rightward, 8, 2)
-    ubar = motion_adjoint(t1, rims, liquids)
-    for i in range(Q):
+    us = [motion(f1, x) for x in range(2)]
+    ubar = motion_adjoint(t1, t_rims, liquids)
+    warm = heat_adjoint(us, liquids, thetas, codes, flux_rims)
+    warm = [v + w for v, w in zip(warm, halves(lift))]
+
+    def adj(i, x):
+        return with_motion(tile(fbar, i, x), ubar[x], i)
+
+    return codes, liquids, us, adj, warm
+
+
+def no_rims():
+    blank, row = jnp.zeros((8, LANES), F32), jnp.zeros((1, LANES), F32)
+    return blank, blank, [row, row], [row, row]
+
+
+def rows_of(ref, at):
+    return [ref[at + x : at + x + 1, :] for x in range(2)]
+
+
+def along_y_kernel(fbar, lift, f1, t1, f0, theta, code, yp, ym):
+    codes, liquids, us, adj, warm = adjoint_parts(
+        fbar, lift, f1, t1, theta, code, no_rims(), no_rims()
+    )
+    ts = halves(t1)
+    for s, e, out in ((1, 7, yp), (-1, 0, ym)):
         for x in range(2):
+            u0 = motion(f0, x)
+            parts = [adj(i, x) for i in moving(1, s, -1)]
+            parts += [ts[x], flux(us[x], 1, s, liquids[x]), liquids[x], warm[x]]
+            parts.append(coefficient(u0, 1, s, codes[x]))
+            for k, v in enumerate(parts):
+                out[2 * k + x : 2 * k + x + 1, :] = v[e : e + 1]
+        out[20:21, :] = flux(us[1], 0, 1, liquids[1])[e : e + 1]
+        out[21:22, :] = flux(us[0], 0, -1, liquids[0])[e : e + 1]
+
+
+def along_x_kernel(
+    fbar, lift, f1, t1, f0, theta, code, leftward, rightward, xp, xm, yl, yr
+):
+    zero, _, _, _ = no_rims()
+    codes, liquids, us, adj, warm = adjoint_parts(
+        fbar, lift, f1, t1, theta, code,
+        (zero, zero, rows_of(leftward, 10), rows_of(rightward, 10)),
+        (zero, zero, rows_of(leftward, 12), rows_of(rightward, 12)),
+    )
+    ts = halves(t1)
+    for s, x, out in ((1, 1, xp), (-1, 0, xm)):
+        parts = [adj(i, x) for i in moving(0, s, -1)]
+        parts += [ts[x], liquids[x], warm[x]]
+        parts.append(coefficient(motion(f0, x), 0, s, codes[x]))
+        parts.append(flux(us[x], 0, s, liquids[x]))
+        for k, v in enumerate(parts):
+            out[8 * k : 8 * k + 8, :] = v
+    for k, (s, e, come, out) in enumerate(((1, 0, leftward, yl), (-1, 7, rightward, yr))):
+        t_come, flux_come, liquid, warm_come, factor = (
+            rows_of(come, 10 + 2 * j) for j in range(5)
+        )
+        for x in range(2):
+            for j in range(5):
+                r = 2 * j + x
+                out[r : r + 1, :] = (
+                    come[r : r + 1, :] + 0.5 * liquid[x] * ts[x][e : e + 1]
+                )
+            done = warm_come[x] + flux(us[x], 1, -s, liquids[x])[e : e + 1]
+            for j, v in enumerate((t_come[x], liquid[x], done, factor[x], flux_come[x])):
+                r = 10 + 2 * j + x
+                out[r : r + 1, :] = v
+        for sx, x, to in ((1, 1, xp), (-1, 0, xm)):
+            r = 2 * moving(1, s, -1).index(diagonal(sx, s, -1)) + x
+            for j, v in enumerate(
+                (out[r : r + 1, :], liquid[x], t_come[x], come[21 - x : 22 - x, :])
+            ):
+                to[80 + 4 * k + j : 81 + 4 * k + j, :] = v
+
+
+def complete(
+    fbar, lift, f1, t1, theta, code, below, above, yl, yr,
+    adj1, warm1, hbelow, habove, hleft, hright,
+):
+    _, liquids, us, adj, warm = adjoint_parts(
+        fbar, lift, f1, t1, theta, code,
+        (below[40:48, :], above[40:48, :], rows_of(yl, 10), rows_of(yr, 10)),
+        (below[72:80, :], above[72:80, :], rows_of(yl, 18), rows_of(yr, 18)),
+    )
+    ts = halves(t1)
+    for x in range(2):
+        warm1[8 * x : 8 * x + 8, :] = warm[x]
+        for i in range(Q):
             k = i * ROWS + 8 * x
-            adj[k : k + 8, :] = with_motion(fbar[k : k + 8, :], ubar[x], i)
-    new = heat_adjoint([motion(f1, x) for x in range(2)], liquids, thetas, codes, flux_rims)
-    for x in range(2):
-        value = new[x] + lift[8 * x : 8 * x + 8, :]
-        theta1[8 * x : 8 * x + 8, :] = value
-        liquid = jnp.where(codes[x] == 0, value, 0.0)
-        u = motion(f0, x)
-        if x == 0:
-            xm[40:48, :] = flux(u, 0, -1, liquid)
-        else:
-            xp[40:48, :] = flux(u, 0, 1, liquid)
-        yp[10 + x : 11 + x, :] = flux(u, 1, 1, liquid)[7:8]
-        ym[10 + x : 11 + x, :] = flux(u, 1, -1, liquid)[0:1]
-    put_messages(lambda i, x: tile(adj, i, x), -1, xp, xm, yp, ym, 0, 0)
+            adj1[k : k + 8, :] = adj(i, x)
+    faces = []
+    for s, x, come, out in ((1, 0, below, hbelow), (-1, 1, above, habove)):
+        for k in range(5):
+            out[8 * k : 8 * k + 8, :] = (
+                come[8 * k : 8 * k + 8, :] + 0.5 * come[48:56, :] * ts[x]
+            )
+        for k, rows in enumerate((yl, yr)):
+            j = 80 + 4 * k
+            out[40 + k : 41 + k, :] = (
+                come[j : j + 1, :] + 0.5 * come[j + 1 : j + 2, :] * rows[10 + x : 11 + x, :]
+            )
+        faces.append(come[64:72, :] * (come[56:64, :] + flux(us[x], 0, -s, liquids[x])))
+    edges = []
+    for k, (s, rows, out) in enumerate(((1, yl, hleft), (-1, yr, hright))):
+        j = 80 + 4 * k
+        out[0:10, :] = rows[0:10, :]
+        edge = []
+        for sx, x, come in ((1, 0, below), (-1, 1, above)):
+            r = 2 * moving(1, s, -1).index(diagonal(sx, s, -1)) + x
+            out[r : r + 1, :] = (
+                rows[r : r + 1, :]
+                - 0.5 * rows[12 + x : 13 + x, :] * come[j + 2 : j + 3, :]
+            )
+            edge.append(
+                rows[16 + x : 17 + x, :]
+                * (rows[14 + x : 15 + x, :] + come[j + 3 : j + 4, :])
+            )
+        edges.append(edge)
+    return (*faces, *edges)
+
+
+def halves(ref):
+    return [ref[0:8, :], ref[8:16, :]]
 
 
 def first_step_kernel(
     scale,
-    f, t, theta, adj, below, above, leftward, rightward,
+    fbar1, lift1, f1, t1, theta2, f, t, below, above, yl, yr,
     tbelow, tabove, tleft, tright, code, h1s, h2s, w1, w2, w3, pack1,
     fbar, thetabar, pack,
     feat, grad, masked, dfs, pad, acc2, acc1, acc3, accb, lift, total,
+    adj, theta, hbelow, habove, hleft, hright,
 ):
-    halo = (below, above, leftward, rightward, 0, 0, 48)
+    flux_rims = complete(
+        fbar1, lift1, f1, t1, theta2, code, below, above, yl, yr,
+        adj, theta, hbelow, habove, hleft, hright,
+    )
+    halo = (hbelow, habove, hleft, hright, 0, 0, 40)
     collision_gradient(adj, halo, code, grad, masked, lift)
     fill_features(feat, f)
     w3b, w2b, w1b = back_weights(w1, w2, w3, pad)
@@ -481,7 +587,6 @@
     codes, thetas = halves(code), halves(theta)
     liquids = [jnp.where(k == 0, v, 0.0) for k, v in zip(codes, thetas)]
     rims = rims_of(tbelow, tabove, tleft, tright, 40, 10)
-    flux_rims = rims_of(below, above, leftward, rightward, 40, 10)
     ubar = motion_adjoint(t, rims, liquids)
     new = heat_adjoint([motion(f, x) for x in range(2)], liquids, thetas, codes, flux_rims)
     for x in range(2):
@@ -497,11 +602,12 @@
     return jax.ShapeDtypeStruct(shape, F32)
 
 
-def call(kernel, outs, scratch, name):
+def call(kernel, outs, scratch, name, more=(), **specs):
     return pl.pallas_call(
         kernel,
         out_shape=outs,
-        scratch_shapes=[pltpu.VMEM(s, F32) for s in scratch],
+        scratch_shapes=[pltpu.VMEM(s, F32) for s in scratch] + list(more),
+        **specs,
         compiler_params=pltpu.CompilerParams(vmem_limit_bytes=40 * 1024 * 1024),
         name=name,
     )
@@ -603,17 +709,13 @@
         [POPS, chunks, chunks, struct(96, LANES), struct(96, LANES), struct(24, LANES), struct(24, LANES)],
         [FULL, FULL, (HID, HID)],
         "forward",
-    )(f, t, code, adj, w1, b1, w2, b2, w3, b3)
+        [pltpu.VMEM(v.shape, v.dtype) for v in (f, t, code, adj, w1, b1, w2, b2, w3, b3)]
+        + [pltpu.SemaphoreType.DMA((10,))],
+        in_specs=[pl.BlockSpec(memory_space=pltpu.HBM)] * 10,
+    )(*(pltpu.with_memory_space_constraint(v, pltpu.HBM) for v in (f, t, code, adj, w1, b1, w2, b2, w3, b3)))
     post, h1s, h2s = outs[:3]
     halo0 = exchange(*outs[3:], ((1, 0, 88), (-1, 12, 90)))
-    f1, t1, *rim_messages = call(
-        stream_kernel,
-        [POPS, WARM, struct(16, LANES), struct(16, LANES), struct(8, LANES), struct(8, LANES)],
-        [],
-        "stream",
-    )(post, f, t, code, theta, *halo0)
-    left1, right1 = along("gy", *rim_messages[2:])
-    rims1 = (*along("gx", *rim_messages[:2]), left1, right1)
+    f1, t1 = call(stream_kernel, [POPS, WARM], [], "stream")(post, f, t, code, *halo0)
     accs = [(2 * HID, 2 * HID), (2 * KP, 4 * HID), (2 * KP, 2 * HID), (KP, LANES)]
     fbar, lift, pack1 = call(
         last_step_kernel,
@@ -621,22 +723,23 @@
         [FULL, (Q * ROWS, LANES), FULL, FULL, (HID, HID), *accs],
         "last_step",
     )(f1, adj, *halo0, code, w1, b1, w2, b2, w3)
-    adj1, theta1, *messages = call(
-        join_kernel,
-        [POPS, WARM, struct(56, LANES), struct(56, LANES), struct(16, LANES), struct(16, LANES)],
-        [],
-        "join",
-    )(fbar, lift, f1, t1, f, theta, code, *rims1)
-    halo1 = exchange(*messages, ((-1, 0, 48),))
+    known = (fbar, lift, f1, t1, f, theta, code)
+    yp, ym = call(along_y_kernel, [struct(24, LANES)] * 2, [], "along_y")(*known)
+    come = along("gy", yp, ym)
+    xp, xm, yl, yr = call(
+        along_x_kernel, [struct(88, LANES)] * 2 + [struct(24, LANES)] * 2, [], "along_x"
+    )(*known, *come)
+    faces = along("gx", xp, xm)
     scale = 1.0 / math.sqrt(cells)
     parts = outer_of(lax.axis_size("gx")) * lax.axis_size("gy")
     part = -(-(PACK + 8) // parts)
     fbar0, theta0, pack = call(
         lambda *refs: first_step_kernel(scale, *refs),
         [POPS, WARM, struct(parts, part, HID)],
-        [FULL, (Q * ROWS, LANES), FULL, FULL, (HID, HID), *accs, (ROWS, LANES), (parts * part, HID)],
+        [FULL, (Q * ROWS, LANES), FULL, FULL, (HID, HID), *accs, (ROWS, LANES), (parts * part, HID),
+         (Q * ROWS, LANES), (ROWS, LANES), (48, LANES), (48, LANES), (16, LANES), (16, LANES)],
         "first_step",
-    )(f, t, theta1, adj1, *halo1, *halo0, code, h1s, h2s, w1, w2, w3, pack1)
+    )(fbar, lift, f1, t1, theta, f, t, *faces, yl, yr, *halo0, code, h1s, h2s, w1, w2, w3, pack1)
     total = reduced(pack)
     g1, gb1, g2, gb2, g3, gb3 = call(
         unpack_kernel,

time: 152 us -> 130 us (0.86)
  starting transfers between devices: 73 us -> 52.1 us
  local copies, waits for them, and re-layouts: 5.48 us -> 0.8 us
    ppermute x12 -> x8, starting transfers between devices: 73 us -> 52.1 us  [shifted(): lax.ppermute(value, axis, [(s, (s + by) % count) for s in range(count)])]
    unnamed x34 -> x20, local copies, waits for them, and re-layouts: 5.48 us -> 0.8 us
    ppermute x12 -> x8, waiting for transfers between devices: 3.72 us -> 5.1 us  [shifted(): lax.ppermute(value, axis, [(s, (s + by) % count) for s in range(count)])]
  transfers between devices with their start and end apart: 12 -> 8, of which waited for: 4 -> 4; matrix products, arithmetic and copies ran while one was open for 0% -> 0% of each run, Pallas kernels for 3% -> 0%
where the time goes in v2:
time: 130 us; the launch traced here: 129 us
  blocking collectives  57.4 us (44%)
  starting transfers between devices  52.1 us (40%)
  Pallas kernels  12.8 us (10%)
  waiting for transfers between devices  5.1 us (4%)
    all_to_all x3, blocking collectives, swapped(): lax.all_to_all(value, ('gx', 'gy'), 0, 0, axis_index_groups=groups, tiled...  57.4 us
    ppermute x8, starting transfers between devices, shifted(): lax.ppermute(value, axis, [(s, (s + by) % count) for s in range(count)])  52.1 us
    ppermute x8, waiting for transfers between devices, shifted(): lax.ppermute(value, axis, [(s, (s + by) % count) for s in range(count)])  5.1 us
    pallas_call x1, Pallas kernels, per_device(): call(last_step_kernel, [POPS, WARM, struct(PACK, HID)], [FULL, (Q * ROWS,...  4.57 us
    pallas_call x1, Pallas kernels, per_device(): call(lambda *refs: first_step_kernel(scale, *refs), [POPS, WARM, struct(p...  3.88 us
    pallas_call x1, Pallas kernels, per_device(): call(forward_kernel, [POPS, chunks, chunks, struct(96, LANES), struct(96,...  3.31 us
  transfers between devices with their start and end apart: 8, of which 4 were waited for; matrix products, arithmetic and copies ran while one was open for 0% of the time, Pallas kernels for 0%

profile of v2, /device:TPU:1, one launch (start us, length us, event | category | flops | bytes accessed | tf_op | source)
XLA Modules:
  0.0 129.1 jit_solution(4197469950992082235)
XLA Ops:
  0.6 3.3 %forward.1 = (f32[304,128]{1,0:T(8,128)S(1)}, f32[4,128,512]{2,1,0:T(8,128)S(1)}, f32[4,128,512]{2,1,0:T(8,128)S(1)}, f32[96,128]{1,0:T(8,128)S(1)}, f32[96,128]...) custom-call(f32[304,128]{1,0:T(8,128)} %bitcast.15, f32[16,128]{1,0:T(8,128)} %bitcast.34, ...), custom_call_target="tpu_custom_call" | custom-call | tf_op jit(solution)/shard_map/forward/pallas_call | solution.py:707
  4.0 4.6 %collective-permute-start = (f32[24,128]{1,0:T(8,128)S(1)}, f32[24,128]{1,0:T(8,128)S(1)}, u32[]{:S(2)}, u32[]{:S(2)}) collective-permute-start(f32[24,128]{1,0:T(8,128)S(1)} %get-tuple-element.40), channel_id=1, source_target_pairs={{0,1},{1,2},{2,3},{3,4},{4,5},{5,6},{6,7},{7,0},{8,9},{9,10},{10,1... | collective-permute-start | bytes 36872 | tf_op jit(solution)/shard_map/ppermute | solution.py:623
  8.6 9.7 %collective-permute-start.1 = (f32[24,128]{1,0:T(8,128)S(1)}, f32[24,128]{1,0:T(8,128)S(1)}, u32[]{:S(2)}, u32[]{:S(2)}) collective-permute-start(f32[24,128]{1,0:T(8,128)S(1)} %get-tuple-element.41), channel_id=1, source_target_pairs={{0,7},{1,0},{2,1},{3,2},{4,3},{5,4},{6,5},{7,6},{8,15},{9,8},{10,9... | collective-permute-start | bytes 36872 | tf_op jit(solution)/shard_map/ppermute | solution.py:623
  18.3 0.0 collective-permute-done.refs_2_.leftward.refs_13_
  18.3 0.8 collective-permute-done.1.refs_3_.rightward.refs_14_
  19.1 2.1 %collective-permute-start.2 = (f32[96,128]{1,0:T(8,128)S(1)}, f32[96,128]{1,0:T(8,128)S(1)}, u32[]{:S(2)}, u32[]{:S(2)}) collective-permute-start(f32[96,128]{1,0:T(8,128)S(1)} %get-tuple-element.42), channel_id=1, source_target_pairs={{0,8},{8,16},{16,24},{24,32},{32,40},{40,48},{48,56},{56,64},{64,7... | collective-permute-start | bytes 147464 | tf_op jit(solution)/shard_map/ppermute | solution.py:623
  21.2 15.3 %collective-permute-start.3 = (f32[96,128]{1,0:T(8,128)S(1)}, f32[96,128]{1,0:T(8,128)S(1)}, u32[]{:S(2)}, u32[]{:S(2)}) collective-permute-start(f32[96,128]{1,0:T(8,128)S(1)} %get-tuple-element.43), channel_id=1, source_target_pairs={{0,760},{8,0},{16,8},{24,16},{32,24},{40,32},{48,40},{56,48},{64,5... | collective-permute-start | bytes 147464 | tf_op jit(solution)/shard_map/ppermute | solution.py:623
  36.5 0.0 collective-permute-done.2.below.refs_11_
  36.5 1.1 collective-permute-done.3.above.refs_12_
  37.7 0.0 copy-start.2
  37.7 0.0 copy-start.4
  37.7 0.0 copy-start.5
  37.7 0.1 stream.1
  37.8 0.0 copy-start.9
  37.8 0.7 copy-done.1
  38.6 0.0 copy-start.6
  38.6 4.6 %last_step.1 = (f32[304,128]{1,0:T(8,128)S(1)}, f32[16,128]{1,0:T(8,128)S(1)}, f32[176,128]{1,0:T(8,128)S(1)}) custom-call(f32[304,128]{1,0:T(8,128)S(1)} %get-tuple-element.44.f.f1.refs_2_, f32[304,128]{1,0:T(8,128)S(1)} %bitcast.21, f32[96,128]{1,0:T(8,128)S(1)} %collective-permute-done.2.below.refs_11_, ...), custom_call_target="tpu_custom_call" | custom-call | tf_op jit(solution)/shard_map/last_step/pallas_call | solution.py:720
  43.2 0.1 along_y.1
  43.3 3.0 %collective-permute-start.4 = (f32[24,128]{1,0:T(8,128)S(1)}, f32[24,128]{1,0:T(8,128)S(1)}, u32[]{:S(2)}, u32[]{:S(2)}) collective-permute-start(f32[24,128]{1,0:T(8,128)S(1)} %get-tuple-element.48), channel_id=1, source_target_pairs={{0,1},{1,2},{2,3},{3,4},{4,5},{5,6},{6,7},{7,0},{8,9},{9,10},{10,1... | collective-permute-start | bytes 36872 | tf_op jit(solution)/shard_map/ppermute | solution.py:623
  46.3 3.3 %collective-permute-start.5 = (f32[24,128]{1,0:T(8,128)S(1)}, f32[24,128]{1,0:T(8,128)S(1)}, u32[]{:S(2)}, u32[]{:S(2)}) collective-permute-start(f32[24,128]{1,0:T(8,128)S(1)} %get-tuple-element.49), channel_id=1, source_target_pairs={{0,7},{1,0},{2,1},{3,2},{4,3},{5,4},{6,5},{7,6},{8,15},{9,8},{10,9... | collective-permute-start | bytes 36872 | tf_op jit(solution)/shard_map/ppermute | solution.py:623
  49.5 0.0 collective-permute-done.4.leftward
  49.6 2.0 %collective-permute-done.5.rightward = f32[24,128]{1,0:T(8,128)S(1)} collective-permute-done((f32[24,128]{1,0:T(8,128)S(1)}, f32[24,128]{1,0:T(8,128)S(1)}, u32[]{:S(2)}, u32[]{:S(2)}) %collective-permute-start.5) | collective-permute-done | bytes 12320 | tf_op jit(solution)/shard_map/ppermute | solution.py:623
  51.6 0.1 along_x.1
  51.7 1.9 %collective-permute-start.6 = (f32[88,128]{1,0:T(8,128)S(1)}, f32[88,128]{1,0:T(8,128)S(1)}, u32[]{:S(2)}, u32[]{:S(2)}) collective-permute-start(f32[88,128]{1,0:T(8,128)S(1)} %get-tuple-element.50), channel_id=1, source_target_pairs={{0,8},{8,16},{16,24},{24,32},{32,40},{40,48},{48,56},{56,64},{64,7... | collective-permute-start | bytes 135176 | tf_op jit(solution)/shard_map/ppermute | solution.py:623
  53.6 12.3 %collective-permute-start.7 = (f32[88,128]{1,0:T(8,128)S(1)}, f32[88,128]{1,0:T(8,128)S(1)}, u32[]{:S(2)}, u32[]{:S(2)}) collective-permute-start(f32[88,128]{1,0:T(8,128)S(1)} %get-tuple-element.51), channel_id=1, source_target_pairs={{0,760},{8,0},{16,8},{24,16},{32,24},{40,32},{48,40},{56,48},{64,5... | collective-permute-start | bytes 135176 | tf_op jit(solution)/shard_map/ppermute | solution.py:623
  65.9 0.0 collective-permute-done.6.refs_7_
  66.0 1.1 collective-permute-done.7.refs_8_
  67.1 3.9 %first_step.1 = (f32[304,128]{1,0:T(8,128)}, f32[16,128]{1,0:T(8,128)}, f32[32,6,128]{2,1,0:T(8,128)S(1)}) custom-call(f32[304,128]{1,0:T(8,128)S(1)} %get-tuple-element.45.fbar.refs_0_, f32[16,128]{1,0:T(8,128)S(1)} %get-tuple-element.46.lift.refs_1_, f32[304,128]{1,0:T(8,128)S(1)} %get-tuple-element.44.f.f1.refs_2_, ...), custom_call_target="tpu_custom_call" | custom-call | tf_op jit(solution)/shard_map/first_step/pallas_call | solution.py:736
  70.9 16.1 %all_to_all.15.parts = f32[32,6,128]{2,1,0:T(8,128)S(1)} all-to-all(f32[32,6,128]{2,1,0:T(8,128)S(1)} %get-tuple-element.59), channel_id=1, replica_groups={{0,1,2,3,4,5,6,7,192,193,194,195,196,197,198,199,384,385,386,387,388,38..., dimensions={0} | all-to-all | bytes 196608 | tf_op jit(solution)/shard_map/all_to_all | solution.py:650
  87.1 27.1 %all_to_all.16.parts = f32[24,6,128]{2,1,0:T(8,128)S(1)} all-to-all(f32[24,6,128]{2,1,0:T(8,128)S(1)} %total.2), channel_id=1, replica_groups={{0,8,16,24,32,40,48,56,64,72,80,88,96,104,112,120,128,136,144,152,160,1..., dimensions={0} | all-to-all | bytes 147456 | tf_op jit(solution)/shard_map/all_to_all | solution.py:650
  114.2 14.3 %all_to_all.17.parts = f32[32,6,128]{2,1,0:T(8,128)S(1)} all-to-all(f32[32,6,128]{2,1,0:T(8,128)S(1)} %total.3), channel_id=1, replica_groups={{0,1,2,3,4,5,6,7,192,193,194,195,196,197,198,199,384,385,386,387,388,38..., dimensions={0} | all-to-all | bytes 196608 | tf_op jit(solution)/shard_map/all_to_all | solution.py:650
  128.4 0.7 unpack.1
  (17 shorter events, 0.1 us)
Async XLA Ops:
  0.6 37.0 %copy-start = (f32[19,2,8,128]{3,2,1,0:T(8,128)S(1)}, f32[19,2,8,128]{3,2,1,0:T(8,128)}, u32[]{:S(2)}) copy-start(f32[19,2,8,128]{3,2,1,0:T(8,128)} %param.11) | copy-start | bytes 466948
  4.0 14.3 %collective-permute-start = (f32[24,128]{1,0:T(8,128)S(1)}, f32[24,128]{1,0:T(8,128)S(1)}, u32[]{:S(2)}, u32[]{:S(2)}) collective-permute-start(f32[24,128]{1,0:T(8,128)S(1)} %get-tuple-element.40), channel_id=1, source_target_pairs={{0,1},{1,2},{2,3},{3,4},{4,5},{5,6},{6,7},{7,0},{8,9},{9,10},{10,1... | collective-permute-start | bytes 36872 | tf_op jit(solution)/shard_map/ppermute | solution.py:623
  8.6 10.5 %collective-permute-start.1 = (f32[24,128]{1,0:T(8,128)S(1)}, f32[24,128]{1,0:T(8,128)S(1)}, u32[]{:S(2)}, u32[]{:S(2)}) collective-permute-start(f32[24,128]{1,0:T(8,128)S(1)} %get-tuple-element.41), channel_id=1, source_target_pairs={{0,7},{1,0},{2,1},{3,2},{4,3},{5,4},{6,5},{7,6},{8,15},{9,8},{10,9... | collective-permute-start | bytes 36872 | tf_op jit(solution)/shard_map/ppermute | solution.py:623
  19.1 18.6 %copy-start.3 = (s32[2,8,128]{2,1,0:T(8,128)S(1)}, s32[2,8,128]{2,1,0:T(8,128)}, u32[]{:S(2)}) copy-start(s32[2,8,128]{2,1,0:T(8,128)} %param.13) | copy-start | bytes 24580
  19.1 18.6 %copy-start.7 = (f32[2,8,128]{2,1,0:T(8,128)S(1)}, f32[2,8,128]{2,1,0:T(8,128)}, u32[]{:S(2)}) copy-start(f32[2,8,128]{2,1,0:T(8,128)} %param.12) | copy-start | bytes 24580
  19.1 17.4 %collective-permute-start.2 = (f32[96,128]{1,0:T(8,128)S(1)}, f32[96,128]{1,0:T(8,128)S(1)}, u32[]{:S(2)}, u32[]{:S(2)}) collective-permute-start(f32[96,128]{1,0:T(8,128)S(1)} %get-tuple-element.42), channel_id=1, source_target_pairs={{0,8},{8,16},{16,24},{24,32},{32,40},{40,48},{48,56},{56,64},{64,7... | collective-permute-start | bytes 147464 | tf_op jit(solution)/shard_map/ppermute | solution.py:623
  21.2 16.5 %collective-permute-start.3 = (f32[96,128]{1,0:T(8,128)S(1)}, f32[96,128]{1,0:T(8,128)S(1)}, u32[]{:S(2)}, u32[]{:S(2)}) collective-permute-start(f32[96,128]{1,0:T(8,128)S(1)} %get-tuple-element.43), channel_id=1, source_target_pairs={{0,760},{8,0},{16,8},{24,16},{32,24},{40,32},{48,40},{56,48},{64,5... | collective-permute-start | bytes 147464 | tf_op jit(solution)/shard_map/ppermute | solution.py:623
  37.7 0.9 copy-start.1
  37.7 0.9 copy-start.2
  37.7 0.9 copy-start.4
  37.7 0.9 copy-start.5
  37.8 0.8 copy-start.8
  37.8 0.8 copy-start.9
  38.6 4.6 %copy-start.6 = (f32[2,8,128]{2,1,0:T(8,128)S(1)}, f32[2,8,128]{2,1,0:T(8,128)}, u32[]{:S(2)}) copy-start(f32[2,8,128]{2,1,0:T(8,128)} %param.21) | copy-start | bytes 24580
  43.3 6.2 %collective-permute-start.4 = (f32[24,128]{1,0:T(8,128)S(1)}, f32[24,128]{1,0:T(8,128)S(1)}, u32[]{:S(2)}, u32[]{:S(2)}) collective-permute-start(f32[24,128]{1,0:T(8,128)S(1)} %get-tuple-element.48), channel_id=1, source_target_pairs={{0,1},{1,2},{2,3},{3,4},{4,5},{5,6},{6,7},{7,0},{8,9},{9,10},{10,1... | collective-permute-start | bytes 36872 | tf_op jit(solution)/shard_map/ppermute | solution.py:623
  46.3 5.3 %collective-permute-start.5 = (f32[24,128]{1,0:T(8,128)S(1)}, f32[24,128]{1,0:T(8,128)S(1)}, u32[]{:S(2)}, u32[]{:S(2)}) collective-permute-start(f32[24,128]{1,0:T(8,128)S(1)} %get-tuple-element.49), channel_id=1, source_target_pairs={{0,7},{1,0},{2,1},{3,2},{4,3},{5,4},{6,5},{7,6},{8,15},{9,8},{10,9... | collective-permute-start | bytes 36872 | tf_op jit(solution)/shard_map/ppermute | solution.py:623
  51.7 14.3 %collective-permute-start.6 = (f32[88,128]{1,0:T(8,128)S(1)}, f32[88,128]{1,0:T(8,128)S(1)}, u32[]{:S(2)}, u32[]{:S(2)}) collective-permute-start(f32[88,128]{1,0:T(8,128)S(1)} %get-tuple-element.50), channel_id=1, source_target_pairs={{0,8},{8,16},{16,24},{24,32},{32,40},{40,48},{48,56},{56,64},{64,7... | collective-permute-start | bytes 135176 | tf_op jit(solution)/shard_map/ppermute | solution.py:623
  53.6 13.5 %collective-permute-start.7 = (f32[88,128]{1,0:T(8,128)S(1)}, f32[88,128]{1,0:T(8,128)S(1)}, u32[]{:S(2)}, u32[]{:S(2)}) collective-permute-start(f32[88,128]{1,0:T(8,128)S(1)} %get-tuple-element.51), channel_id=1, source_target_pairs={{0,760},{8,0},{16,8},{24,16},{32,24},{40,32},{48,40},{56,48},{64,5... | collective-permute-start | bytes 135176 | tf_op jit(solution)/shard_map/ppermute | solution.py:623

commit v3 on v2

--- a/solution.py
+++ b/solution.py
@@ -94,8 +94,16 @@
 
 
 def tile(ref, i, x):
+    if isinstance(ref, tuple):
+        return ref[x][8 * i : 8 * i + 8, :]
     k = i * ROWS + x * 8
     return ref[k : k + 8, :]
+
+
+def halves(ref):
+    if isinstance(ref, tuple):
+        return [ref[0][...], ref[1][...]]
+    return [ref[0:8, :], ref[8:16, :]]
 
 
 def transposed(w_ref, b_ref, pad_ref):
@@ -112,21 +120,24 @@
     return jnp.transpose(pad_ref[...])
 
 
-def across(ref, r0, rows):
+def across(ref, c):
+    n, step = CH // LANES, ref.shape[0] // KP
     return jnp.concatenate(
-        [ref[pl.ds(r0 + j, KP, stride=ROWS), :] for j in range(rows)], axis=1
-    )
-
-
-def back(ref, r0, value):
-    for j in range(value.shape[1] // LANES):
-        ref[pl.ds(r0 + j, KP, stride=ROWS), :] = value[:, j * LANES : (j + 1) * LANES]
+        [ref[pl.ds(c * n + j, KP, stride=step), :] for j in range(n)], axis=1
+    )
+
+
+def back(ref, c, value):
+    n, step = CH // LANES, ref.shape[0] // KP
+    for j in range(n):
+        ref[pl.ds(c * n + j, KP, stride=step), :] = value[:, j * LANES : (j + 1) * LANES]
 
 
 def fill_features(s_ref, f_ref):
-    s_ref[0 : Q * ROWS, :] = f_ref[...]
-    s_ref[Q * ROWS : (Q + 1) * ROWS, :] = jnp.ones((ROWS, LANES), F32)
-    s_ref[(Q + 1) * ROWS :, :] = jnp.zeros(((KP - Q - 1) * ROWS, LANES), F32)
+    rows = s_ref.shape[0] // KP
+    s_ref[0 : Q * rows, :] = f_ref[...]
+    s_ref[Q * rows : (Q + 1) * rows, :] = jnp.ones((rows, LANES), F32)
+    s_ref[(Q + 1) * rows :, :] = jnp.zeros(((KP - Q - 1) * rows, LANES), F32)
 
 
 def wide(b):
@@ -190,7 +201,7 @@
 
 def warm_neighbours(t_ref, rims, x):
     below, above, leftward, rightward = rims
-    t = [t_ref[0:8, :], t_ref[8:16, :]]
+    t = halves(t_ref)
     lower = below if x == 0 else t[0]
     upper = t[1] if x == 0 else above
     return [
@@ -242,25 +253,24 @@
     return h1, h1x, h2
 
 
-def network_back(fx, h1, h1x, h2, d, w3b, w2b, w1b, acc2, acc1, acc3, accb, first):
+def network_back(h1, h2, d, w3b, w2b, w1b):
     dx = stacked(d)
-    p2 = product(w3b, dx, HID) * (1.0 - h2 * h2)
-    px = stacked(p2)
-    p1 = product(w2b, px, HID) * (1.0 - h1 * h1)
-    qx = stacked(p1)
-    df = product(w1b, qx, KP)
-    parts = (
-        (acc2, nt(h1x, px)),
-        (acc1, nt(fx, jnp.concatenate([qx, px], axis=0))),
-        (acc3, nt(dx, stacked(h2))),
-        (accb, sum(d[:, j * LANES : (j + 1) * LANES] for j in range(CH // LANES))),
-    )
-    for ref, value in parts:
-        if first:
-            ref[...] = value
-        else:
-            ref[...] = ref[...] + value
-    return df
+    px = stacked(product(w3b, dx, HID) * (1.0 - h2 * h2))
+    qx = stacked(product(w2b, px, HID) * (1.0 - h1 * h1))
+    return product(w1b, qx, KP), dx, px, qx
+
+
+def folded(d):
+    return sum(d[:, j * LANES : (j + 1) * LANES] for j in range(CH // LANES))
+
+
+def gather(accs, values, first):
+    for ref, value in zip(accs, values):
+        ref[...] = value if first else ref[...] + value
+
+
+def weight_products(fx, h1x, h2x, dx, px, qx):
+    return nt(h1x, px), nt(fx, jnp.concatenate([qx, px], axis=0)), nt(dx, h2x)
 
 
 def write_pack(pack, acc2, acc1, acc3, accb, pad_ref):
@@ -300,13 +310,12 @@
     b3t = wide(column(b3, Q, pad)[0:KP])
     copies[6].wait()
     fill_features(feat, f)
-    n = CH // LANES
     for c in range(ROWS * LANES // CH):
-        fx = stacked(across(feat, c * n, n))
+        fx = stacked(across(feat, c))
         h1, h1x, h2 = hidden(fx, l1, l2, b2t)
         h1s[c] = h1
         h2s[c] = h2
-        back(outs, c * n, product(l3, stacked(h2), KP) + b3t)
+        back(outs, c, product(l3, stacked(h2), KP) + b3t)
     for c in copies[7:]:
         c.wait()
     put_messages(lambda i, x: tile(adj, i, x), -1, xp, xm, yp, ym, 48, 12)
@@ -341,26 +350,6 @@
     )
 
 
-def stream_kernel(post, f, t, code, below, above, leftward, rightward, f1, t1):
-    halo = (below, above, leftward, rightward, 0, 0, 88)
-    for i in range(Q):
-        for x in range(2):
-            k = i * ROWS + 8 * x
-            f1[k : k + 8, :] = streamed(post, halo, 1, i, x)
-    rims = rims_of(below, above, leftward, rightward, 40, 10)
-    for x in range(2):
-        u = motion(f, x)
-        here = t[8 * x : 8 * x + 8, :]
-        total = 0.4 * here
-        for a, (plus, minus) in enumerate(warm_neighbours(t, rims, x)):
-            total = total + (CONDUCTIVITY - 0.5 * u[a]) * plus
-            total = total + (CONDUCTIVITY + 0.5 * u[a]) * minus
-        kind = code[8 * x : 8 * x + 8, :]
-        t1[8 * x : 8 * x + 8, :] = jnp.where(
-            kind == 0, total, jnp.where(kind == 1, here, HEATER)
-        )
-
-
 def collision_gradient(adj, halo, code, grad, masked, lift):
     for x in range(2):
         fluid = code[8 * x : 8 * x + 8, :] == 0
@@ -388,36 +377,64 @@
     return w3b, w2b, w1b
 
 
-def last_step_kernel(
-    f, adj, below, above, leftward, rightward, code, w1, b1, w2, b2, w3,
-    fbar, lift, pack,
-    feat, grad, masked, dfs, pad, acc2, acc1, acc3, accb,
+def middle_kernel(
+    x, post, f, t, code, adj, face, leftward, rightward, w1, b1, w2, b2, w3,
+    f1, t1, fbar, lift, accb, fxs, h1xs, h2xs, dxs, pxs, qxs,
+    feat, grad, masked, dfs, pad,
 ):
-    halo = (below, above, leftward, rightward, 48, 12, 90)
-    collision_gradient(adj, halo, code, grad, masked, lift)
-    fill_features(feat, f)
+    kind = code[8 * x : 8 * x + 8, :]
+    fluid = kind == 0
+    halo = (face, face, leftward, rightward, 0, 0, 88)
+    adj_halo = (face, face, leftward, rightward, 48, 12, 90)
+    warmth = None
+    for i in range(Q):
+        k = 8 * i
+        f1[k : k + 8, :] = streamed(post, halo, 1, i, x)
+        g = streamed(adj, adj_halo, -1, i, x)
+        grad[k : k + 8, :] = g
+        g = jnp.where(fluid, g, 0.0)
+        masked[k : k + 8, :] = g
+        if BUOYANCY[i]:
+            warmth = BUOYANCY[i] * g if warmth is None else warmth + BUOYANCY[i] * g
+    lift[...] = warmth
+    masked[8 * Q :, :] = jnp.zeros(((KP - Q) * 8, LANES), F32)
+    u = motion(f, x)
+    here = t[8 * x : 8 * x + 8, :]
+    total = 0.4 * here
+    rims = rims_of(face, face, leftward, rightward, 40, 10)
+    for a, (plus, minus) in enumerate(warm_neighbours(t, rims, x)):
+        total = total + (CONDUCTIVITY - 0.5 * u[a]) * plus
+        total = total + (CONDUCTIVITY + 0.5 * u[a]) * minus
+    t1[...] = jnp.where(fluid, total, jnp.where(kind == 1, here, HEATER))
+    fill_features(feat, f1)
     l1 = left_narrow(jnp.transpose(transposed(w1, b1, pad)))
     l2 = left(jnp.transpose(w2[...]))
     b2t = wide(column(b2, HID, pad))
     w3b, w2b, w1b = back_weights(w1, w2, w3, pad)
-    n = CH // LANES
-    for c in range(ROWS * LANES // CH):
-        fx = stacked(across(feat, c * n, n))
+    for c in range(8 * LANES // CH):
+        fx = stacked(across(feat, c))
         h1, h1x, h2 = hidden(fx, l1, l2, b2t)
-        d = across(masked, c * n, n)
-        df = network_back(fx, h1, h1x, h2, d, w3b, w2b, w1b, acc2, acc1, acc3, accb, c == 0)
-        back(dfs, c * n, df)
-    fluid = code[...] == 0
+        d = across(masked, c)
+        df, dx, px, qx = network_back(h1, h2, d, w3b, w2b, w1b)
+        gather((accb,), (folded(d),), c == 0)
+        back(dfs, c, df)
+        fxs[c], h1xs[c], h2xs[c] = fx, h1x, stacked(h2)
+        dxs[c], pxs[c], qxs[c] = dx, px, qx
     for i in range(Q):
-        k, o = i * ROWS, OPPOSITE[i] * ROWS
-        fbar[k : k + ROWS, :] = jnp.where(
-            fluid, grad[k : k + ROWS, :] + dfs[k : k + ROWS, :], grad[o : o + ROWS, :]
+        k, o = 8 * i, 8 * OPPOSITE[i]
+        fbar[k : k + 8, :] = jnp.where(
+            fluid, grad[k : k + 8, :] + dfs[k : k + 8, :], grad[o : o + 8, :]
         )
-    write_pack(pack, acc2, acc1, acc3, accb, pad)
-
-
-def halves(ref):
-    return [ref[0:8, :], ref[8:16, :]]
+
+
+def weights_kernel(*refs):
+    first, second, (_, pack, pad, accb, *accs) = refs[:7], refs[7:14], refs[14:]
+    accb[...] = first[0][...] + second[0][...]
+    for plane in (first, second):
+        for c in range(plane[1].shape[0]):
+            values = weight_products(*(v[c] for v in plane[1:]))
+            gather(accs, values, plane is first and c == 0)
+    write_pack(pack, *accs, accb, pad)
 
 
 def coefficient(u, a, s, kind):
@@ -447,7 +464,13 @@
     return [ref[at + x : at + x + 1, :] for x in range(2)]
 
 
-def along_y_kernel(fbar, lift, f1, t1, f0, theta, code, yp, ym):
+def paired(refs):
+    return [tuple(refs[2 * k : 2 * k + 2]) for k in range(4)]
+
+
+def along_y_kernel(*refs):
+    fbar, lift, f1, t1 = paired(refs)
+    f0, theta, code, yp, ym = refs[8:]
     codes, liquids, us, adj, warm = adjoint_parts(
         fbar, lift, f1, t1, theta, code, no_rims(), no_rims()
     )
@@ -464,9 +487,9 @@
         out[21:22, :] = flux(us[0], 0, -1, liquids[0])[e : e + 1]
 
 
-def along_x_kernel(
-    fbar, lift, f1, t1, f0, theta, code, leftward, rightward, xp, xm, yl, yr
-):
+def along_x_kernel(*refs):
+    fbar, lift, f1, t1 = paired(refs)
+    f0, theta, code, leftward, rightward, xp, xm, yl, yr = refs[8:]
     zero, _, _, _ = no_rims()
     codes, liquids, us, adj, warm = adjoint_parts(
         fbar, lift, f1, t1, theta, code,
@@ -549,35 +572,28 @@
     return (*faces, *edges)
 
 
-def halves(ref):
-    return [ref[0:8, :], ref[8:16, :]]
-
-
 def first_step_kernel(
-    scale,
-    fbar1, lift1, f1, t1, theta2, f, t, below, above, yl, yr,
+    scale, known,
+    theta2, f, t, below, above, yl, yr,
     tbelow, tabove, tleft, tright, code, h1s, h2s, w1, w2, w3, pack1,
     fbar, thetabar, pack,
     feat, grad, masked, dfs, pad, acc2, acc1, acc3, accb, lift, total,
     adj, theta, hbelow, habove, hleft, hright,
 ):
     flux_rims = complete(
-        fbar1, lift1, f1, t1, theta2, code, below, above, yl, yr,
+        *paired(known), theta2, code, below, above, yl, yr,
         adj, theta, hbelow, habove, hleft, hright,
     )
     halo = (hbelow, habove, hleft, hright, 0, 0, 40)
     collision_gradient(adj, halo, code, grad, masked, lift)
     fill_features(feat, f)
     w3b, w2b, w1b = back_weights(w1, w2, w3, pad)
-    n = CH // LANES
     for c in range(ROWS * LANES // CH):
-        fx = stacked(across(feat, c * n, n))
-        h1 = h1s[c]
-        d = across(masked, c * n, n)
-        df = network_back(
-            fx, h1, stacked(h1), h2s[c], d, w3b, w2b, w1b, acc2, acc1, acc3, accb, c == 0
-        )
-        back(dfs, c * n, df)
+        fx, h1, h2, d = stacked(across(feat, c)), h1s[c], h2s[c], across(masked, c)
+        df, dx, px, qx = network_back(h1, h2, d, w3b, w2b, w1b)
+        values = weight_products(fx, stacked(h1), stacked(h2), dx, px, qx)
+        gather((acc2, acc1, acc3, accb), (*values, folded(d)), c == 0)
+        back(dfs, c, df)
     write_pack(total, acc2, acc1, acc3, accb, pad)
     parts, part, _ = pack.shape
     total[PACK:, :] = jnp.zeros((parts * part - PACK, HID), F32)
@@ -715,36 +731,51 @@
     )(*(pltpu.with_memory_space_constraint(v, pltpu.HBM) for v in (f, t, code, adj, w1, b1, w2, b2, w3, b3)))
     post, h1s, h2s = outs[:3]
     halo0 = exchange(*outs[3:], ((1, 0, 88), (-1, 12, 90)))
-    f1, t1 = call(stream_kernel, [POPS, WARM], [], "stream")(post, f, t, code, *halo0)
     accs = [(2 * HID, 2 * HID), (2 * KP, 4 * HID), (2 * KP, 2 * HID), (KP, LANES)]
-    fbar, lift, pack1 = call(
-        last_step_kernel,
-        [POPS, WARM, struct(PACK, HID)],
-        [FULL, (Q * ROWS, LANES), FULL, FULL, (HID, HID), *accs],
-        "last_step",
-    )(f1, adj, *halo0, code, w1, b1, w2, b2, w3)
-    known = (fbar, lift, f1, t1, f, theta, code)
+    plane, half = struct(8 * Q, LANES), struct(8, LANES)
+    small, large = (
+        jax.ShapeDtypeStruct((8 * LANES // CH, 2 * n, CH), BF16) for n in (KP, HID)
+    )
+    below, above, *sides = halo0
+    planes = [
+        call(
+            lambda *refs, x=x: middle_kernel(x, *refs),
+            [plane, half, plane, half, struct(KP, LANES), small, large, large, small, large, large],
+            [(8 * KP, LANES), (8 * Q, LANES), (8 * KP, LANES), (8 * KP, LANES), (HID, HID)],
+            "middle",
+        )(post, f, t, code, adj, face, *sides, w1, b1, w2, b2, w3)
+        for x, face in enumerate((below, above))
+    ]
+    parts = [planes[x][k] for k in (2, 3, 0, 1) for x in range(2)]
+    known = (*parts, f, theta, code)
     yp, ym = call(along_y_kernel, [struct(24, LANES)] * 2, [], "along_y")(*known)
     come = along("gy", yp, ym)
     xp, xm, yl, yr = call(
         along_x_kernel, [struct(88, LANES)] * 2 + [struct(24, LANES)] * 2, [], "along_x"
     )(*known, *come)
     faces = along("gx", xp, xm)
+    pack1 = call(
+        weights_kernel,
+        struct(PACK, HID),
+        [(HID, HID), (KP, LANES), *accs[:3]],
+        "weights",
+        in_specs=[pl.BlockSpec(memory_space=pltpu.VMEM)] * 14 + [pl.BlockSpec(memory_space=pl.ANY)],
+    )(*planes[0][4:], *planes[1][4:], xp)
     scale = 1.0 / math.sqrt(cells)
-    parts = outer_of(lax.axis_size("gx")) * lax.axis_size("gy")
-    part = -(-(PACK + 8) // parts)
+    shares = outer_of(lax.axis_size("gx")) * lax.axis_size("gy")
+    part = -(-(PACK + 8) // shares)
     fbar0, theta0, pack = call(
-        lambda *refs: first_step_kernel(scale, *refs),
-        [POPS, WARM, struct(parts, part, HID)],
-        [FULL, (Q * ROWS, LANES), FULL, FULL, (HID, HID), *accs, (ROWS, LANES), (parts * part, HID),
+        lambda *refs: first_step_kernel(scale, refs[:8], *refs[8:]),
+        [POPS, WARM, struct(shares, part, HID)],
+        [FULL, (Q * ROWS, LANES), FULL, FULL, (HID, HID), *accs, (ROWS, LANES), (shares * part, HID),
          (Q * ROWS, LANES), (ROWS, LANES), (48, LANES), (48, LANES), (16, LANES), (16, LANES)],
         "first_step",
-    )(fbar, lift, f1, t1, theta, f, t, *faces, yl, yr, *halo0, code, h1s, h2s, w1, w2, w3, pack1)
+    )(*parts, theta, f, t, *faces, yl, yr, *halo0, code, h1s, h2s, w1, w2, w3, pack1)
     total = reduced(pack)
     g1, gb1, g2, gb2, g3, gb3 = call(
         unpack_kernel,
         [struct(Q, HID), struct(1, HID), struct(HID, HID), struct(1, HID), struct(Q, HID), struct(1, Q)],
-        [(parts * part, HID)],
+        [(shares * part, HID)],
         "unpack",
     )(total)
     return (

time: 130 us -> 127 us (0.977)
  waiting for transfers between devices: 5.1 us -> 16.7 us
  blocking collectives: 57.4 us -> 47.2 us
  starting transfers between devices: 52.1 us -> 47.8 us
    ppermute x8, waiting for transfers between devices: 5.1 us -> 16.7 us  [shifted(): lax.ppermute(value, axis, [(s, (s + by) % count) for s in range(count)])]
    all_to_all x3, blocking collectives: 57.4 us -> 47.2 us  [swapped(): lax.all_to_all(value, ('gx', 'gy'), 0, 0, axis_index_groups=groups, tiled...]
    ppermute x8, starting transfers between devices: 52.1 us -> 47.8 us  [shifted(): lax.ppermute(value, axis, [(s, (s + by) % count) for s in range(count)])]
    pallas_call x3 -> x4, Pallas kernels: 8.55 us -> 8.85 us  [the longest x1 3.92 us: per_device(): call(lambda *refs: first_step_kernel(scale, refs[:8], *refs[8:]), [POPS,...]
  transfers between devices with their start and end apart: 8 -> 8, of which waited for: 4 -> 4; matrix products, arithmetic and copies ran while one was open for 0% -> 0% of each run, Pallas kernels for 0% -> 2%
where the time goes in v3:
time: 127 us; the launch traced here: 126 us
  starting transfers between devices  47.8 us (38%)
  blocking collectives  47.2 us (37%)
  waiting for transfers between devices  16.7 us (13%)
  Pallas kernels  13.1 us (10%)
    ppermute x8, starting transfers between devices, shifted(): lax.ppermute(value, axis, [(s, (s + by) % count) for s in range(count)])  47.8 us
    all_to_all x3, blocking collectives, swapped(): lax.all_to_all(value, ('gx', 'gy'), 0, 0, axis_index_groups=groups, tiled...  47.2 us
    ppermute x8, waiting for transfers between devices, shifted(): lax.ppermute(value, axis, [(s, (s + by) % count) for s in range(count)])  16.7 us
    pallas_call x1, Pallas kernels, per_device(): call(lambda *refs: first_step_kernel(scale, refs[:8], *refs[8:]), [POPS,...  3.92 us
    pallas_call x2, Pallas kernels, per_device(): call(lambda *refs, x=x: middle_kernel(x, *refs), [plane, half, plane, hal...  3.62 us
    pallas_call x1, Pallas kernels, per_device(): call(forward_kernel, [POPS, chunks, chunks, struct(96, LANES), struct(96,...  3.32 us
  transfers between devices with their start and end apart: 8, of which 4 were waited for; matrix products, arithmetic and copies ran while one was open for 0% of the time, Pallas kernels for 2%

profile of v3, /device:TPU:1, one launch (start us, length us, event | category | flops | bytes accessed | tf_op | source)
XLA Modules:
  0.0 126.5 jit_solution(2154464745562573222)
XLA Ops:
  0.6 0.0 copy-start
  0.7 3.3 %forward.1 = (f32[304,128]{1,0:T(8,128)S(1)}, f32[4,128,512]{2,1,0:T(8,128)S(1)}, f32[4,128,512]{2,1,0:T(8,128)S(1)}, f32[96,128]{1,0:T(8,128)S(1)}, f32[96,128]...) custom-call(f32[304,128]{1,0:T(8,128)} %bitcast.15, f32[16,128]{1,0:T(8,128)} %bitcast.34, ...), custom_call_target="tpu_custom_call" | custom-call | tf_op jit(solution)/shard_map/forward/pallas_call | solution.py:723
  4.0 4.6 %collective-permute-start = (f32[24,128]{1,0:T(8,128)S(1)}, f32[24,128]{1,0:T(8,128)S(1)}, u32[]{:S(2)}, u32[]{:S(2)}) collective-permute-start(f32[24,128]{1,0:T(8,128)S(1)} %get-tuple-element.57), channel_id=1, source_target_pairs={{0,1},{1,2},{2,3},{3,4},{4,5},{5,6},{6,7},{7,0},{8,9},{9,10},{10,1... | collective-permute-start | bytes 36872 | tf_op jit(solution)/shard_map/ppermute | solution.py:639
  8.6 9.7 %collective-permute-start.1 = (f32[24,128]{1,0:T(8,128)S(1)}, f32[24,128]{1,0:T(8,128)S(1)}, u32[]{:S(2)}, u32[]{:S(2)}) collective-permute-start(f32[24,128]{1,0:T(8,128)S(1)} %get-tuple-element.58), channel_id=1, source_target_pairs={{0,7},{1,0},{2,1},{3,2},{4,3},{5,4},{6,5},{7,6},{8,15},{9,8},{10,9... | collective-permute-start | bytes 36872 | tf_op jit(solution)/shard_map/ppermute | solution.py:639
  18.3 0.0 collective-permute-done.refs_2_.refs_6_.refs_17_
  18.3 0.8 collective-permute-done.1.refs_3_.refs_7_.refs_18_
  19.2 15.5 %collective-permute-start.3 = (f32[96,128]{1,0:T(8,128)S(1)}, f32[96,128]{1,0:T(8,128)S(1)}, u32[]{:S(2)}, u32[]{:S(2)}) collective-permute-start(f32[96,128]{1,0:T(8,128)S(1)} %get-tuple-element.61), channel_id=1, source_target_pairs={{0,760},{8,0},{16,8},{24,16},{32,24},{40,32},{48,40},{56,48},{64,5... | collective-permute-start | bytes 147464 | tf_op jit(solution)/shard_map/ppermute | solution.py:639
  34.6 0.0 copy-start.8
  34.6 0.0 copy-start.9
  34.7 1.9 %collective-permute-start.2 = (f32[96,128]{1,0:T(8,128)S(1)}, f32[96,128]{1,0:T(8,128)S(1)}, u32[]{:S(2)}, u32[]{:S(2)}) collective-permute-start(f32[96,128]{1,0:T(8,128)S(1)} %get-tuple-element.59), channel_id=1, source_target_pairs={{0,8},{8,16},{16,24},{24,32},{32,40},{40,48},{48,56},{56,64},{64,7... | collective-permute-start | bytes 147464 | tf_op jit(solution)/shard_map/ppermute | solution.py:639
  36.6 0.0 collective-permute-done.3.refs_5_.refs_16_
  36.7 1.8 %middle.3 = (f32[152,128]{1,0:T(8,128)S(1)}, f32[8,128]{1,0:T(8,128)S(1)}, f32[152,128]{1,0:T(8,128)S(1)}, f32[8,128]{1,0:T(8,128)S(1)}, f32[32,128]{1,0:T(8,128...) custom-call(f32[304,128]{1,0:T(8,128)S(1)} %get-tuple-element.54.ref, ...), custom_call_target="tpu_custom_call" | custom-call | tf_op jit(solution)/shard_map/middle/pallas_call | solution.py:741
  38.5 9.1 %collective-permute-done.2.refs_5_.refs_15_ = f32[96,128]{1,0:T(8,128)S(1)} collective-permute-done((f32[96,128]{1,0:T(8,128)S(1)}, f32[96,128]{1,0:T(8,128)S(1)}, u32[]{:S(2)}, u32[]{:S(2)}) %collective-permute-start.2) | collective-permute-done | bytes 49184 | tf_op jit(solution)/shard_map/ppermute | solution.py:639
  47.6 1.8 %middle.2 = (f32[152,128]{1,0:T(8,128)S(1)}, f32[8,128]{1,0:T(8,128)S(1)}, f32[152,128]{1,0:T(8,128)S(1)}, f32[8,128]{1,0:T(8,128)S(1)}, f32[32,128]{1,0:T(8,128...) custom-call(f32[304,128]{1,0:T(8,128)S(1)} %get-tuple-element.54.ref, ...), custom_call_target="tpu_custom_call" | custom-call | tf_op jit(solution)/shard_map/middle/pallas_call | solution.py:741
  49.4 0.0 copy-start.7
  49.5 0.7 copy-done.7
  50.1 0.1 along_y.1
  50.2 3.4 %collective-permute-start.4 = (f32[24,128]{1,0:T(8,128)S(1)}, f32[24,128]{1,0:T(8,128)S(1)}, u32[]{:S(2)}, u32[]{:S(2)}) collective-permute-start(f32[24,128]{1,0:T(8,128)S(1)} %get-tuple-element.69), channel_id=1, source_target_pairs={{0,1},{1,2},{2,3},{3,4},{4,5},{5,6},{6,7},{7,0},{8,9},{9,10},{10,1... | collective-permute-start | bytes 36872 | tf_op jit(solution)/shard_map/ppermute | solution.py:639
  53.7 3.5 %collective-permute-start.5 = (f32[24,128]{1,0:T(8,128)S(1)}, f32[24,128]{1,0:T(8,128)S(1)}, u32[]{:S(2)}, u32[]{:S(2)}) collective-permute-start(f32[24,128]{1,0:T(8,128)S(1)} %get-tuple-element.70), channel_id=1, source_target_pairs={{0,7},{1,0},{2,1},{3,2},{4,3},{5,4},{6,5},{7,6},{8,15},{9,8},{10,9... | collective-permute-start | bytes 36872 | tf_op jit(solution)/shard_map/ppermute | solution.py:639
  57.1 0.0 collective-permute-done.4.refs_11_
  57.2 1.8 %collective-permute-done.5.refs_12_ = f32[24,128]{1,0:T(8,128)S(1)} collective-permute-done((f32[24,128]{1,0:T(8,128)S(1)}, f32[24,128]{1,0:T(8,128)S(1)}, u32[]{:S(2)}, u32[]{:S(2)}) %collective-permute-start.5) | collective-permute-done | bytes 12320 | tf_op jit(solution)/shard_map/ppermute | solution.py:639
  59.0 0.1 along_x.1
  59.1 2.4 %collective-permute-start.7 = (f32[88,128]{1,0:T(8,128)S(1)}, f32[88,128]{1,0:T(8,128)S(1)}, u32[]{:S(2)}, u32[]{:S(2)}) collective-permute-start(f32[88,128]{1,0:T(8,128)S(1)} %get-tuple-element.72), channel_id=1, source_target_pairs={{0,760},{8,0},{16,8},{24,16},{32,24},{40,32},{48,40},{56,48},{64,5... | collective-permute-start | bytes 135176 | tf_op jit(solution)/shard_map/ppermute | solution.py:639
  61.5 6.8 %collective-permute-start.6 = (f32[88,128]{1,0:T(8,128)S(1)}, f32[88,128]{1,0:T(8,128)S(1)}, u32[]{:S(2)}, u32[]{:S(2)}) collective-permute-start(f32[88,128]{1,0:T(8,128)S(1)} %get-tuple-element.71.refs_14_), channel_id=1, source_target_pairs={{0,8},{8,16},{16,24},{24,32},{32,40},{40,48},{48,56},{56,64},{64,7... | collective-permute-start | bytes 135176 | tf_op jit(solution)/shard_map/ppermute | solution.py:639
  68.3 1.3 %weights.1.refs_25_ = f32[176,128]{1,0:T(8,128)S(1)} custom-call(f32[32,128]{1,0:T(8,128)S(1)} %get-tuple-element.77.refs_0_, bf16[2,64,512]{2,1,0:T(8,128)(2,1)S(1)} %get-tuple-element.78.refs_1_, bf16[2,256,512]{2,1,0:T(8,128)(2,1)S(1)} %get-tuple-element.79.refs_2_, bf16[2,256,512]{2,1,0:T(8,128)(2,1)S(1)} %get-tuple-element.80.refs_3_, ...), custom_call_target="tpu_custom_call" | custom-call | tf_op jit(solution)/shard_map/weights/pallas_call | solution.py:757
  69.6 0.0 collective-permute-done.7.refs_12_
  69.6 5.0 %collective-permute-done.6.refs_11_ = f32[88,128]{1,0:T(8,128)S(1)} collective-permute-done((f32[88,128]{1,0:T(8,128)S(1)}, f32[88,128]{1,0:T(8,128)S(1)}, u32[]{:S(2)}, u32[]{:S(2)}) %collective-permute-start.6) | collective-permute-done | bytes 45088 | tf_op jit(solution)/shard_map/ppermute | solution.py:639
  74.6 3.9 %first_step.1 = (f32[304,128]{1,0:T(8,128)}, f32[16,128]{1,0:T(8,128)}, f32[32,6,128]{2,1,0:T(8,128)S(1)}) custom-call(f32[152,128]{1,0:T(8,128)S(1)} %get-tuple-element.60.refs_0_, f32[152,128]{1,0:T(8,128)S(1)} %get-tuple-element.62.refs_1_, f32[8,128]{1,0:T(8,128)S(1)} %get-tuple-element.63.refs_2_, f32[8,128]{1,0:T(8,128)S(1)} %get-tuple-element.64.refs_3_, ...), custom_call_target="tpu_custom_call" | custom-call | tf_op jit(solution)/shard_map/first_step/pallas_call | solution.py:767
  78.5 16.3 %all_to_all.15.parts = f32[32,6,128]{2,1,0:T(8,128)S(1)} all-to-all(f32[32,6,128]{2,1,0:T(8,128)S(1)} %get-tuple-element.93), channel_id=1, replica_groups={{0,1,2,3,4,5,6,7,192,193,194,195,196,197,198,199,384,385,386,387,388,38..., dimensions={0} | all-to-all | bytes 196608 | tf_op jit(solution)/shard_map/all_to_all | solution.py:666
  94.9 16.6 %all_to_all.16.parts = f32[24,6,128]{2,1,0:T(8,128)S(1)} all-to-all(f32[24,6,128]{2,1,0:T(8,128)S(1)} %total.2), channel_id=1, replica_groups={{0,8,16,24,32,40,48,56,64,72,80,88,96,104,112,120,128,136,144,152,160,1..., dimensions={0} | all-to-all | bytes 147456 | tf_op jit(solution)/shard_map/all_to_all | solution.py:666
  111.5 14.3 %all_to_all.17.parts = f32[32,6,128]{2,1,0:T(8,128)S(1)} all-to-all(f32[32,6,128]{2,1,0:T(8,128)S(1)} %total.3), channel_id=1, replica_groups={{0,1,2,3,4,5,6,7,192,193,194,195,196,197,198,199,384,385,386,387,388,38..., dimensions={0} | all-to-all | bytes 196608 | tf_op jit(solution)/shard_map/all_to_all | solution.py:666
  125.8 0.7 unpack.1
  (18 shorter events, 0.1 us)
Async XLA Ops:
  0.6 36.0 %copy-start = (f32[19,2,8,128]{3,2,1,0:T(8,128)S(1)}, f32[19,2,8,128]{3,2,1,0:T(8,128)}, u32[]{:S(2)}) copy-start(f32[19,2,8,128]{3,2,1,0:T(8,128)} %param.11) | copy-start | bytes 466948
  0.6 36.0 %copy-start.1 = (f32[19,2,8,128]{3,2,1,0:T(8,128)S(1)}, f32[19,2,8,128]{3,2,1,0:T(8,128)}, u32[]{:S(2)}) copy-start(f32[19,2,8,128]{3,2,1,0:T(8,128)} %param.20) | copy-start | bytes 466948
  4.0 14.3 %collective-permute-start = (f32[24,128]{1,0:T(8,128)S(1)}, f32[24,128]{1,0:T(8,128)S(1)}, u32[]{:S(2)}, u32[]{:S(2)}) collective-permute-start(f32[24,128]{1,0:T(8,128)S(1)} %get-tuple-element.57), channel_id=1, source_target_pairs={{0,1},{1,2},{2,3},{3,4},{4,5},{5,6},{6,7},{7,0},{8,9},{9,10},{10,1... | collective-permute-start | bytes 36872 | tf_op jit(solution)/shard_map/ppermute | solution.py:639
  8.6 10.5 %collective-permute-start.1 = (f32[24,128]{1,0:T(8,128)S(1)}, f32[24,128]{1,0:T(8,128)S(1)}, u32[]{:S(2)}, u32[]{:S(2)}) collective-permute-start(f32[24,128]{1,0:T(8,128)S(1)} %get-tuple-element.58), channel_id=1, source_target_pairs={{0,7},{1,0},{2,1},{3,2},{4,3},{5,4},{6,5},{7,6},{8,15},{9,8},{10,9... | collective-permute-start | bytes 36872 | tf_op jit(solution)/shard_map/ppermute | solution.py:639
  19.1 17.5 %copy-start.2 = (f32[128,128]{1,0:T(8,128)S(1)}, f32[128,128]{1,0:T(8,128)}, u32[]{:S(2)}) copy-start(f32[128,128]{1,0:T(8,128)} %refs_23_.1) | copy-start | bytes 196612
  19.1 17.5 %copy-start.3 = (s32[2,8,128]{2,1,0:T(8,128)S(1)}, s32[2,8,128]{2,1,0:T(8,128)}, u32[]{:S(2)}) copy-start(s32[2,8,128]{2,1,0:T(8,128)} %param.13) | copy-start | bytes 24580
  19.1 17.5 %copy-start.4 = (f32[19,128]{1,0:T(8,128)S(1)}, f32[19,128]{1,0:T(8,128)}, u32[]{:S(2)}) copy-start(f32[19,128]{1,0:T(8,128)} %refs_22_.1) | copy-start | bytes 29188
  19.1 17.5 %copy-start.5 = (f32[128,19]{0,1:T(8,128)S(1)}, f32[128,19]{0,1:T(8,128)}, u32[]{:S(2)}) copy-start(f32[128,19]{0,1:T(8,128)} %param.18) | copy-start | bytes 29188
  19.1 17.5 %copy-start.6 = (f32[2,8,128]{2,1,0:T(8,128)S(1)}, f32[2,8,128]{2,1,0:T(8,128)}, u32[]{:S(2)}) copy-start(f32[2,8,128]{2,1,0:T(8,128)} %param.12) | copy-start | bytes 24580
  19.2 17.4 %collective-permute-start.3 = (f32[96,128]{1,0:T(8,128)S(1)}, f32[96,128]{1,0:T(8,128)S(1)}, u32[]{:S(2)}, u32[]{:S(2)}) collective-permute-start(f32[96,128]{1,0:T(8,128)S(1)} %get-tuple-element.61), channel_id=1, source_target_pairs={{0,760},{8,0},{16,8},{24,16},{32,24},{40,32},{48,40},{56,48},{64,5... | collective-permute-start | bytes 147464 | tf_op jit(solution)/shard_map/ppermute | solution.py:639
  34.6 2.0 %copy-start.8 = (f32[128]{0:T(128)S(1)}, f32[128]{0:T(128)}, u32[]{:S(2)}) copy-start(f32[128]{0:T(128)} %param.15) | copy-start | bytes 1540
  34.6 2.0 %copy-start.9 = (f32[128]{0:T(128)S(1)}, f32[128]{0:T(128)}, u32[]{:S(2)}) copy-start(f32[128]{0:T(128)} %param.17) | copy-start | bytes 1540
  34.7 13.0 %collective-permute-start.2 = (f32[96,128]{1,0:T(8,128)S(1)}, f32[96,128]{1,0:T(8,128)S(1)}, u32[]{:S(2)}, u32[]{:S(2)}) collective-permute-start(f32[96,128]{1,0:T(8,128)S(1)} %get-tuple-element.59), channel_id=1, source_target_pairs={{0,8},{8,16},{16,24},{24,32},{32,40},{40,48},{48,56},{56,64},{64,7... | collective-permute-start | bytes 147464 | tf_op jit(solution)/shard_map/ppermute | solution.py:639
  49.4 0.7 copy-start.7
  50.2 6.9 %collective-permute-start.4 = (f32[24,128]{1,0:T(8,128)S(1)}, f32[24,128]{1,0:T(8,128)S(1)}, u32[]{:S(2)}, u32[]{:S(2)}) collective-permute-start(f32[24,128]{1,0:T(8,128)S(1)} %get-tuple-element.69), channel_id=1, source_target_pairs={{0,1},{1,2},{2,3},{3,4},{4,5},{5,6},{6,7},{7,0},{8,9},{9,10},{10,1... | collective-permute-start | bytes 36872 | tf_op jit(solution)/shard_map/ppermute | solution.py:639
  53.7 5.3 %collective-permute-start.5 = (f32[24,128]{1,0:T(8,128)S(1)}, f32[24,128]{1,0:T(8,128)S(1)}, u32[]{:S(2)}, u32[]{:S(2)}) collective-permute-start(f32[24,128]{1,0:T(8,128)S(1)} %get-tuple-element.70), channel_id=1, source_target_pairs={{0,7},{1,0},{2,1},{3,2},{4,3},{5,4},{6,5},{7,6},{8,15},{9,8},{10,9... | collective-permute-start | bytes 36872 | tf_op jit(solution)/shard_map/ppermute | solution.py:639
  59.1 10.5 %collective-permute-start.7 = (f32[88,128]{1,0:T(8,128)S(1)}, f32[88,128]{1,0:T(8,128)S(1)}, u32[]{:S(2)}, u32[]{:S(2)}) collective-permute-start(f32[88,128]{1,0:T(8,128)S(1)} %get-tuple-element.72), channel_id=1, source_target_pairs={{0,760},{8,0},{16,8},{24,16},{32,24},{40,32},{48,40},{56,48},{64,5... | collective-permute-start | bytes 135176 | tf_op jit(solution)/shard_map/ppermute | solution.py:639
  61.5 13.1 %collective-permute-start.6 = (f32[88,128]{1,0:T(8,128)S(1)}, f32[88,128]{1,0:T(8,128)S(1)}, u32[]{:S(2)}, u32[]{:S(2)}) collective-permute-start(f32[88,128]{1,0:T(8,128)S(1)} %get-tuple-element.71.refs_14_), channel_id=1, source_target_pairs={{0,8},{8,16},{16,24},{24,32},{32,40},{40,48},{48,56},{56,64},{64,7... | collective-permute-start | bytes 135176 | tf_op jit(solution)/shard_map/ppermute | solution.py:639

commit v4 on v3

--- a/solution.py
+++ b/solution.py
@@ -120,17 +120,21 @@
     return jnp.transpose(pad_ref[...])
 
 
+def rows_in(ref, c):
+    n, step = CH // LANES, ref.shape[0] // KP
+    order = range(step) if step != ROWS else [0, 7, 8, 15, *range(1, 7), *range(9, 15)]
+    return order[c * n : (c + 1) * n], step
+
+
 def across(ref, c):
-    n, step = CH // LANES, ref.shape[0] // KP
-    return jnp.concatenate(
-        [ref[pl.ds(c * n + j, KP, stride=step), :] for j in range(n)], axis=1
-    )
+    rows, step = rows_in(ref, c)
+    return jnp.concatenate([ref[pl.ds(r, KP, stride=step), :] for r in rows], axis=1)
 
 
 def back(ref, c, value):
-    n, step = CH // LANES, ref.shape[0] // KP
-    for j in range(n):
-        ref[pl.ds(c * n + j, KP, stride=step), :] = value[:, j * LANES : (j + 1) * LANES]
+    rows, step = rows_in(ref, c)
+    for j, r in enumerate(rows):
+        ref[pl.ds(r, KP, stride=step), :] = value[:, j * LANES : (j + 1) * LANES]
 
 
 def fill_features(s_ref, f_ref):
@@ -144,11 +148,14 @@
     return jnp.concatenate([b] * (CH // LANES), axis=1)
 
 
-def put_messages(value, orient, xp, xm, yp, ym, at, row):
+def put_x(value, orient, xp, xm, at):
     for k, i in enumerate(moving(0, 1, orient)):
         xp[at + 8 * k : at + 8 * k + 8, :] = value(i, 1)
     for k, i in enumerate(moving(0, -1, orient)):
         xm[at + 8 * k : at + 8 * k + 8, :] = value(i, 0)
+
+
+def put_y(value, orient, yp, ym, row):
     for k, i in enumerate(moving(1, 1, orient)):
         for x in range(2):
             yp[row + 2 * k + x : row + 2 * k + x + 1, :] = value(i, x)[7:8]
@@ -253,10 +260,10 @@
     return h1, h1x, h2
 
 
-def network_back(h1, h2, d, w3b, w2b, w1b):
+def network_back(s1, s2, d, w3b, w2b, w1b):
     dx = stacked(d)
-    px = stacked(product(w3b, dx, HID) * (1.0 - h2 * h2))
-    qx = stacked(product(w2b, px, HID) * (1.0 - h1 * h1))
+    px = stacked(product(w3b, dx, HID) * s2)
+    qx = stacked(product(w2b, px, HID) * s1)
     return product(w1b, qx, KP), dx, px, qx
 
 
@@ -289,51 +296,88 @@
     pack[HID + 22 : HID + 23, :] = b3
 
 
-def forward_kernel(
-    f_in, t_in, code_in, adj_in, w1_in, b1_in, w2_in, b2_in, w3_in, b3_in,
-    post, h1s, h2s, xp, xm, yp, ym,
-    feat, outs, pad, f, t, code, adj, w1, b1, w2, b2, w3, b3, sems,
+def collided(f, t, code, outs, i):
+    k = i * ROWS
+    relaxed = f[k : k + ROWS, :] + outs[k : k + ROWS, :]
+    if BUOYANCY[i]:
+        relaxed = relaxed + BUOYANCY[i] * t[...]
+    o = OPPOSITE[i] * ROWS
+    return jnp.where(code[...] == 0, relaxed, f[o : o + ROWS, :])
+
+
+def forward_chunk(feat, c, l1, l2, l3, b2t, b3t):
+    h1, _, h2 = hidden(stacked(across(feat, c)), l1, l2, b2t)
+    return h1, h2, product(l3, stacked(h2), KP) + b3t
+
+
+def edge_rows_kernel(
+    w1_in, b1_in, w2_in, b2_in, w3_in, b3_in, f_in, t_in, code_in, adj_in, theta_in,
+    w1, w2, w3, f, t, code, adj, theta, l1, l2, l3, b2t, b3t, h1s, h2s, out0, yp, ym,
+    feat, outs, pad, b1, b2, b3, sems,
 ):
-    ins = (w1_in, b1_in, w2_in, b2_in, w3_in, b3_in, f_in, t_in, code_in, adj_in)
-    here = (w1, b1, w2, b2, w3, b3, f, t, code, adj)
+    ins = (w1_in, b1_in, w2_in, b2_in, w3_in, b3_in, f_in, t_in, code_in, adj_in, theta_in)
+    here = (w1, b1, w2, b2, w3, b3, f, t, code, adj, theta)
     copies = [pltpu.make_async_copy(a, b, sems.at[k]) for k, (a, b) in enumerate(zip(ins, here))]
     for c in copies:
         c.start()
     for c in copies[:6]:
         c.wait()
-    l1 = left_narrow(jnp.transpose(transposed(w1, b1, pad)))
-    l2 = left(jnp.transpose(w2[...]))
+    l1[...] = left_narrow(jnp.transpose(transposed(w1, b1, pad)))
+    l2[...] = left(jnp.transpose(w2[...]))
     pad[...] = jnp.zeros((HID, HID), F32)
     pad[0:Q, :] = w3[...]
-    l3 = left(pad[0:KP, :])
-    b2t = wide(column(b2, HID, pad))
-    b3t = wide(column(b3, Q, pad)[0:KP])
+    l3[...] = left(pad[0:KP, :])
+    b2t[...] = wide(column(b2, HID, pad))
+    b3t[...] = wide(column(b3, Q, pad)[0:KP])
     copies[6].wait()
     fill_features(feat, f)
-    for c in range(ROWS * LANES // CH):
-        fx = stacked(across(feat, c))
-        h1, h1x, h2 = hidden(fx, l1, l2, b2t)
-        h1s[c] = h1
-        h2s[c] = h2
-        back(outs, c, product(l3, stacked(h2), KP) + b3t)
+    h1, h2, out = forward_chunk(feat, 0, l1[...], l2[...], l3[...], b2t[...], b3t[...])
+    h1s[0], h2s[0], out0[...] = h1, h2, out
+    outs[...] = jnp.zeros(outs.shape, F32)
+    back(outs, 0, out)
     for c in copies[7:]:
         c.wait()
-    put_messages(lambda i, x: tile(adj, i, x), -1, xp, xm, yp, ym, 48, 12)
-    fluid = code[...] == 0
-    warm = t[...]
-    for i in range(Q):
-        k = i * ROWS
-        relaxed = f[k : k + ROWS, :] + outs[k : k + ROWS, :]
-        if BUOYANCY[i]:
-            relaxed = relaxed + BUOYANCY[i] * warm
-        o = OPPOSITE[i] * ROWS
-        post[k : k + ROWS, :] = jnp.where(fluid, relaxed, f[o : o + ROWS, :])
-    put_messages(lambda i, x: tile(post, i, x), 1, xp, xm, yp, ym, 0, 0)
-    xp[40:48, :] = t[8:16, :]
-    xm[40:48, :] = t[0:8, :]
+    put_y(lambda i, x: tile(adj, i, x), -1, yp, ym, 12)
+
+    def value(i, x):
+        return collided(f, t, code, outs, i)[8 * x : 8 * x + 8]
+
+    put_y(value, 1, yp, ym, 0)
     for x in range(2):
         yp[10 + x : 11 + x, :] = t[8 * x + 7 : 8 * x + 8, :]
         ym[10 + x : 11 + x, :] = t[8 * x : 8 * x + 1, :]
+
+
+def other_rows_kernel(
+    f, t, code, adj, l1, l2, l3, b2t, b3t, out0,
+    post, h1s, h2s, xp, xm,
+    feat, outs,
+):
+    fill_features(feat, f)
+    back(outs, 0, out0[...])
+    for c in range(1, ROWS * LANES // CH):
+        h1, h2, out = forward_chunk(feat, c, l1[...], l2[...], l3[...], b2t[...], b3t[...])
+        h1s[c - 1], h2s[c - 1] = h1, h2
+        back(outs, c, out)
+    for i in range(Q):
+        post[i * ROWS : (i + 1) * ROWS, :] = collided(f, t, code, outs, i)
+    put_x(lambda i, x: tile(adj, i, x), -1, xp, xm, 48)
+    put_x(lambda i, x: tile(post, i, x), 1, xp, xm, 0)
+    xp[40:48, :] = t[8:16, :]
+    xm[40:48, :] = t[0:8, :]
+
+
+def prepare_kernel(
+    f, h1a, h2a, h1b, h2b, w1, w2, w3, _,
+    w3b, w2b, w1b, fxs, h1xs, h2xs, s1, s2,
+    feat, pad,
+):
+    w3b[...], w2b[...], w1b[...] = back_weights(w1, w2, w3, pad)
+    fill_features(feat, f)
+    for c in range(ROWS * LANES // CH):
+        h1, h2 = (h1a[0], h2a[0]) if c == 0 else (h1b[c - 1], h2b[c - 1])
+        fxs[c], h1xs[c], h2xs[c] = stacked(across(feat, c)), stacked(h1), stacked(h2)
+        s1[c], s2[c] = 1.0 - h1 * h1, 1.0 - h2 * h2
 
 
 def left_narrow(w):
@@ -378,9 +422,9 @@
 
 
 def middle_kernel(
-    x, post, f, t, code, adj, face, leftward, rightward, w1, b1, w2, b2, w3,
+    x, post, f, t, code, adj, face, leftward, rightward, l1, l2, b2t, w3b, w2b, w1b,
     f1, t1, fbar, lift, accb, fxs, h1xs, h2xs, dxs, pxs, qxs,
-    feat, grad, masked, dfs, pad,
+    feat, grad, masked, dfs,
 ):
     kind = code[8 * x : 8 * x + 8, :]
     fluid = kind == 0
@@ -407,15 +451,13 @@
         total = total + (CONDUCTIVITY + 0.5 * u[a]) * minus
     t1[...] = jnp.where(fluid, total, jnp.where(kind == 1, here, HEATER))
     fill_features(feat, f1)
-    l1 = left_narrow(jnp.transpose(transposed(w1, b1, pad)))
-    l2 = left(jnp.transpose(w2[...]))
-    b2t = wide(column(b2, HID, pad))
-    w3b, w2b, w1b = back_weights(w1, w2, w3, pad)
     for c in range(8 * LANES // CH):
         fx = stacked(across(feat, c))
-        h1, h1x, h2 = hidden(fx, l1, l2, b2t)
+        h1, h1x, h2 = hidden(fx, l1[...], l2[...], b2t[...])
         d = across(masked, c)
-        df, dx, px, qx = network_back(h1, h2, d, w3b, w2b, w1b)
+        df, dx, px, qx = network_back(
+            1.0 - h1 * h1, 1.0 - h2 * h2, d, w3b[...], w2b[...], w1b[...]
+        )
         gather((accb,), (folded(d),), c == 0)
         back(dfs, c, df)
         fxs[c], h1xs[c], h2xs[c] = fx, h1x, stacked(h2)
@@ -575,9 +617,9 @@
 def first_step_kernel(
     scale, known,
     theta2, f, t, below, above, yl, yr,
-    tbelow, tabove, tleft, tright, code, h1s, h2s, w1, w2, w3, pack1,
+    tbelow, tabove, tleft, tright, code, w3b, w2b, w1b, fxs, h1xs, h2xs, s1, s2, pack1,
     fbar, thetabar, pack,
-    feat, grad, masked, dfs, pad, acc2, acc1, acc3, accb, lift, total,
+    grad, masked, dfs, pad, acc2, acc1, acc3, accb, lift, total,
     adj, theta, hbelow, habove, hleft, hright,
 ):
     flux_rims = complete(
@@ -586,12 +628,10 @@
     )
     halo = (hbelow, habove, hleft, hright, 0, 0, 40)
     collision_gradient(adj, halo, code, grad, masked, lift)
-    fill_features(feat, f)
-    w3b, w2b, w1b = back_weights(w1, w2, w3, pad)
     for c in range(ROWS * LANES // CH):
-        fx, h1, h2, d = stacked(across(feat, c)), h1s[c], h2s[c], across(masked, c)
-        df, dx, px, qx = network_back(h1, h2, d, w3b, w2b, w1b)
-        values = weight_products(fx, stacked(h1), stacked(h2), dx, px, qx)
+        d = across(masked, c)
+        df, dx, px, qx = network_back(s1[c], s2[c], d, w3b[...], w2b[...], w1b[...])
+        values = weight_products(fxs[c], h1xs[c], h2xs[c], dx, px, qx)
         gather((acc2, acc1, acc3, accb), (*values, folded(d)), c == 0)
         back(dfs, c, df)
     write_pack(total, acc2, acc1, acc3, accb, pad)
@@ -650,34 +690,29 @@
         put_corners(leftward, rightward, orient, xp_out, xm_out, row, at)
 
 
-def exchange(xp, xm, yp, ym, blocks):
-    leftward, rightward = along("gy", yp, ym)
-    xp, xm = call(
-        lambda *refs: edge_kernel(blocks, *refs),
-        [struct(*xp.shape), struct(*xm.shape)],
-        [],
-        "edge",
-    )(xp, xm, leftward, rightward)
-    below, above = along("gx", xp, xm)
-    return below, above, leftward, rightward
-
-
 def swapped(value, groups):
     return lax.all_to_all(
         value, ("gx", "gy"), 0, 0, axis_index_groups=groups, tiled=True
     )
 
 
-def outer_of(nx):
-    return nx // 24 if nx % 24 == 0 else (2 if nx % 2 == 0 else 1)
+def factors_of(nx):
+    near = 2 if nx % 2 == 0 else 1
+    far = nx // 24 if nx % 24 == 0 else 1
+    return far, nx // (far * near), near
+
+
+def shares_of(nx, ny):
+    far, _, near = factors_of(nx)
+    return far * near * ny
 
 
 def groups_of(nx, ny):
-    outer = outer_of(nx)
-    at = np.arange(nx * ny).reshape(outer, nx // outer, ny)
+    far, mid, near = factors_of(nx)
+    at = np.arange(nx * ny).reshape(far, mid, near, ny)
     return (
-        at.transpose(1, 0, 2).reshape(nx // outer, outer * ny).tolist(),
-        at.transpose(0, 2, 1).reshape(outer * ny, nx // outer).tolist(),
+        at.transpose(1, 0, 2, 3).reshape(mid, -1).tolist(),
+        at.transpose(0, 2, 3, 1).reshape(-1, mid).tolist(),
     )
 
 
@@ -719,31 +754,58 @@
     t, code, theta = (v.reshape(ROWS, LANES) for v in (t, code, theta))
     b1, b2, b3 = (v.reshape(1, -1) for v in (b1, b2, b3))
     w3 = w3.T
-    chunks = struct(ROWS * LANES // CH, HID, CH)
+    ins = (w1, b1, w2, b2, w3, b3, f, t, code, adj, theta)
+    like = [jax.ShapeDtypeStruct(v.shape, v.dtype) for v in ins]
+    held = [v for k, v in enumerate(like) if k not in (1, 3, 5)]
+    count = ROWS * LANES // CH
+
+    def narrow(*shape):
+        return jax.ShapeDtypeStruct(shape, BF16)
+
     outs = call(
-        forward_kernel,
-        [POPS, chunks, chunks, struct(96, LANES), struct(96, LANES), struct(24, LANES), struct(24, LANES)],
+        edge_rows_kernel,
+        [*held, narrow(2 * HID, 2 * KP), narrow(2 * HID, 2 * HID), narrow(2 * KP, 2 * HID),
+         struct(HID, CH), struct(KP, CH), struct(1, HID, CH), struct(1, HID, CH),
+         struct(KP, CH), struct(24, LANES), struct(24, LANES)],
         [FULL, FULL, (HID, HID)],
-        "forward",
-        [pltpu.VMEM(v.shape, v.dtype) for v in (f, t, code, adj, w1, b1, w2, b2, w3, b3)]
-        + [pltpu.SemaphoreType.DMA((10,))],
-        in_specs=[pl.BlockSpec(memory_space=pltpu.HBM)] * 10,
-    )(*(pltpu.with_memory_space_constraint(v, pltpu.HBM) for v in (f, t, code, adj, w1, b1, w2, b2, w3, b3)))
-    post, h1s, h2s = outs[:3]
-    halo0 = exchange(*outs[3:], ((1, 0, 88), (-1, 12, 90)))
+        "edge_rows",
+        [pltpu.VMEM(v.shape, v.dtype) for v in (b1, b2, b3)] + [pltpu.SemaphoreType.DMA((11,))],
+        in_specs=[pl.BlockSpec(memory_space=pltpu.HBM)] * 11,
+    )(*(pltpu.with_memory_space_constraint(v, pltpu.HBM) for v in ins))
+    w1, w2, w3, f, t, code, adj, theta, l1, l2, l3, b2t, b3t, h1a, h2a, out0, yp, ym = outs
+    sides = along("gy", yp, ym)
+    post, h1b, h2b, xp, xm = call(
+        other_rows_kernel,
+        [POPS, *[struct(count - 1, HID, CH)] * 2, struct(96, LANES), struct(96, LANES)],
+        [FULL, FULL],
+        "other_rows",
+    )(f, t, code, adj, l1, l2, l3, b2t, b3t, out0)
+    blocks = ((1, 0, 88), (-1, 12, 90))
+    xp, xm = call(
+        lambda *refs: edge_kernel(blocks, *refs), [struct(96, LANES)] * 2, [], "corners"
+    )(xp, xm, *sides)
+    below, above = along("gx", xp, xm)
+    halo0 = (below, above, *sides)
+    w3b, w2b, w1b, *kept = call(
+        prepare_kernel,
+        [narrow(2 * HID, 2 * KP), narrow(2 * HID, 2 * HID), narrow(2 * KP, 2 * HID),
+         narrow(count, 2 * KP, CH), *[narrow(count, 2 * HID, CH)] * 2, *[struct(count, HID, CH)] * 2],
+        [FULL, (HID, HID)],
+        "prepare",
+        in_specs=[pl.BlockSpec(memory_space=pltpu.VMEM)] * 8 + [pl.BlockSpec(memory_space=pl.ANY)],
+    )(f, h1a, h2a, h1b, h2b, w1, w2, w3, xp)
     accs = [(2 * HID, 2 * HID), (2 * KP, 4 * HID), (2 * KP, 2 * HID), (KP, LANES)]
     plane, half = struct(8 * Q, LANES), struct(8, LANES)
     small, large = (
         jax.ShapeDtypeStruct((8 * LANES // CH, 2 * n, CH), BF16) for n in (KP, HID)
     )
-    below, above, *sides = halo0
     planes = [
         call(
             lambda *refs, x=x: middle_kernel(x, *refs),
             [plane, half, plane, half, struct(KP, LANES), small, large, large, small, large, large],
-            [(8 * KP, LANES), (8 * Q, LANES), (8 * KP, LANES), (8 * KP, LANES), (HID, HID)],
+            [(8 * KP, LANES), (8 * Q, LANES), (8 * KP, LANES), (8 * KP, LANES)],
             "middle",
-        )(post, f, t, code, adj, face, *sides, w1, b1, w2, b2, w3)
+        )(post, f, t, code, adj, face, *sides, l1, l2, b2t, w3b, w2b, w1b)
         for x, face in enumerate((below, above))
     ]
     parts = [planes[x][k] for k in (2, 3, 0, 1) for x in range(2)]
@@ -762,15 +824,15 @@
         in_specs=[pl.BlockSpec(memory_space=pltpu.VMEM)] * 14 + [pl.BlockSpec(memory_space=pl.ANY)],
     )(*planes[0][4:], *planes[1][4:], xp)
     scale = 1.0 / math.sqrt(cells)
-    shares = outer_of(lax.axis_size("gx")) * lax.axis_size("gy")
+    shares = shares_of(lax.axis_size("gx"), lax.axis_size("gy"))
     part = -(-(PACK + 8) // shares)
     fbar0, theta0, pack = call(
         lambda *refs: first_step_kernel(scale, refs[:8], *refs[8:]),
         [POPS, WARM, struct(shares, part, HID)],
-        [FULL, (Q * ROWS, LANES), FULL, FULL, (HID, HID), *accs, (ROWS, LANES), (shares * part, HID),
+        [(Q * ROWS, LANES), FULL, FULL, (HID, HID), *accs, (ROWS, LANES), (shares * part, HID),
          (Q * ROWS, LANES), (ROWS, LANES), (48, LANES), (48, LANES), (16, LANES), (16, LANES)],
         "first_step",
-    )(*parts, theta, f, t, *faces, yl, yr, *halo0, code, h1s, h2s, w1, w2, w3, pack1)
+    )(*parts, theta, f, t, *faces, yl, yr, *halo0, code, w3b, w2b, w1b, *kept, pack1)
     total = reduced(pack)
     g1, gb1, g2, gb2, g3, gb3 = call(
         unpack_kernel,

time: 127 us -> 124 us (0.976)
  blocking collectives: 47.2 us -> 45.6 us
    all_to_all x3, blocking collectives: 47.2 us -> 45.6 us  [swapped(): lax.all_to_all(value, ('gx', 'gy'), 0, 0, axis_index_groups=groups, tiled...]
    pallas_call x2 -> x4, Pallas kernels: 3.34 us -> 4.39 us  [the longest x1 1.88 us: per_device(): call(edge_rows_kernel, [*held, narrow(2 * HID, 2 * KP), narrow(2 * HID, 2...]
  transfers between devices with their start and end apart: 8 -> 8, of which waited for: 4 -> 3; matrix products, arithmetic and copies ran while one was open for 0% -> 0% of each run, Pallas kernels for 2% -> 5%
where the time goes in v4:
time: 124 us; the launch traced here: 123 us
  starting transfers between devices  47 us (38%)
  blocking collectives  45.6 us (37%)
  waiting for transfers between devices  15.7 us (13%)
  Pallas kernels  13.9 us (11%)
    ppermute x8, starting transfers between devices, shifted(): lax.ppermute(value, axis, [(s, (s + by) % count) for s in range(count)])  47 us
    all_to_all x3, blocking collectives, swapped(): lax.all_to_all(value, ('gx', 'gy'), 0, 0, axis_index_groups=groups, tiled...  45.6 us
    ppermute x8, waiting for transfers between devices, shifted(): lax.ppermute(value, axis, [(s, (s + by) % count) for s in range(count)])  15.7 us
    pallas_call x1, Pallas kernels, per_device(): call(lambda *refs: first_step_kernel(scale, refs[:8], *refs[8:]), [POPS,...  3.71 us
    pallas_call x2, Pallas kernels, per_device(): call(lambda *refs, x=x: middle_kernel(x, *refs), [plane, half, plane, hal...  3.52 us
  transfers between devices with their start and end apart: 8, of which 3 were waited for; matrix products, arithmetic and copies ran while one was open for 0% of the time, Pallas kernels for 5%

profile of v4, /device:TPU:1, one launch (start us, length us, event | category | flops | bytes accessed | tf_op | source)
XLA Modules:
  0.0 123.0 jit_solution(13339570821058129023)
XLA Ops:
  0.6 1.9 %edge_rows.1 = (f32[19,128]{1,0:T(8,128)S(1)}, f32[128,128]{1,0:T(8,128)S(1)}, f32[19,128]{1,0:T(8,128)S(1)}, f32[304,128]{1,0:T(8,128)S(1)}, f32[16,128]{1,0:T(...) custom-call(f32[19,128]{1,0:T(8,128)} %w1_in.1, ...), custom_call_target="tpu_custom_call" | custom-call | tf_op jit(solution)/shard_map/edge_rows/pallas_call | solution.py:765
  2.5 4.6 %collective-permute-start = (f32[24,128]{1,0:T(8,128)S(1)}, f32[24,128]{1,0:T(8,128)S(1)}, u32[]{:S(2)}, u32[]{:S(2)}) collective-permute-start(f32[24,128]{1,0:T(8,128)S(1)} %get-tuple-element.91), channel_id=1, source_target_pairs={{0,1},{1,2},{2,3},{3,4},{4,5},{5,6},{6,7},{7,0},{8,9},{9,10},{10,1... | collective-permute-start | bytes 36872 | tf_op jit(solution)/shard_map/ppermute | solution.py:679
  7.1 9.7 %collective-permute-start.1 = (f32[24,128]{1,0:T(8,128)S(1)}, f32[24,128]{1,0:T(8,128)S(1)}, u32[]{:S(2)}, u32[]{:S(2)}) collective-permute-start(f32[24,128]{1,0:T(8,128)S(1)} %get-tuple-element.92), channel_id=1, source_target_pairs={{0,7},{1,0},{2,1},{3,2},{4,3},{5,4},{6,5},{7,6},{8,15},{9,8},{10,9... | collective-permute-start | bytes 36872 | tf_op jit(solution)/shard_map/ppermute | solution.py:679
  16.8 1.6 %other_rows.1 = (f32[304,128]{1,0:T(8,128)S(1)}, f32[3,128,512]{2,1,0:T(8,128)S(1)}, f32[3,128,512]{2,1,0:T(8,128)S(1)}, f32[96,128]{1,0:T(8,128)S(1)}, f32[96,128]{1,0:T(8,128)S(1)}) custom-call(f32[304,128]{1,0:T(8,128)S(1)} %get-tuple-element.78.f.refs_1_.refs_8_.refs_9_, f32[16,128]{1,0:T(8,128)S(1)} %get-tuple-element.79.t.refs_2_.refs_10_, ...), custom_call_target="tpu_custom_call" | custom-call | tf_op jit(solution)/shard_map/other_rows/pallas_call | solution.py:777
  18.4 0.0 collective-permute-done.refs_2_.refs_6_.refs_17_
  18.5 0.0 collective-permute-done.1.refs_3_.refs_7_.refs_18_
  18.5 14.5 %collective-permute-start.3 = (f32[96,128]{1,0:T(8,128)S(1)}, f32[96,128]{1,0:T(8,128)S(1)}, u32[]{:S(2)}, u32[]{:S(2)}) collective-permute-start(f32[96,128]{1,0:T(8,128)S(1)} %get-tuple-element.105), channel_id=1, source_target_pairs={{0,760},{8,0},{16,8},{24,16},{32,24},{40,32},{48,40},{56,48},{64,5... | collective-permute-start | bytes 147464 | tf_op jit(solution)/shard_map/ppermute | solution.py:679
  33.0 1.9 %collective-permute-start.2 = (f32[96,128]{1,0:T(8,128)S(1)}, f32[96,128]{1,0:T(8,128)S(1)}, u32[]{:S(2)}, u32[]{:S(2)}) collective-permute-start(f32[96,128]{1,0:T(8,128)S(1)} %get-tuple-element.93._), channel_id=1, source_target_pairs={{0,8},{8,16},{16,24},{24,32},{32,40},{40,48},{48,56},{56,64},{64,7... | collective-permute-start | bytes 147464 | tf_op jit(solution)/shard_map/ppermute | solution.py:679
  34.9 0.9 prepare.1
  35.9 0.0 collective-permute-done.3.refs_5_.refs_16_
  35.9 1.8 %middle.3 = (f32[152,128]{1,0:T(8,128)S(1)}, f32[8,128]{1,0:T(8,128)S(1)}, f32[152,128]{1,0:T(8,128)S(1)}, f32[8,128]{1,0:T(8,128)S(1)}, f32[32,128]{1,0:T(8,128...) custom-call(f32[304,128]{1,0:T(8,128)S(1)} %get-tuple-element.88.ref, ...), custom_call_target="tpu_custom_call" | custom-call | tf_op jit(solution)/shard_map/middle/pallas_call | solution.py:803
  37.6 8.3 %collective-permute-done.2.refs_5_.refs_15_ = f32[96,128]{1,0:T(8,128)S(1)} collective-permute-done((f32[96,128]{1,0:T(8,128)S(1)}, f32[96,128]{1,0:T(8,128)S(1)}, u32[]{:S(2)}, u32[]{:S(2)}) %collective-permute-start.2) | collective-permute-done | bytes 49184 | tf_op jit(solution)/shard_map/ppermute | solution.py:679
  46.0 1.8 %middle.2 = (f32[152,128]{1,0:T(8,128)S(1)}, f32[8,128]{1,0:T(8,128)S(1)}, f32[152,128]{1,0:T(8,128)S(1)}, f32[8,128]{1,0:T(8,128)S(1)}, f32[32,128]{1,0:T(8,128...) custom-call(f32[304,128]{1,0:T(8,128)S(1)} %get-tuple-element.88.ref, ...), custom_call_target="tpu_custom_call" | custom-call | tf_op jit(solution)/shard_map/middle/pallas_call | solution.py:803
  47.7 0.1 along_y.1
  47.8 3.6 %collective-permute-start.4 = (f32[24,128]{1,0:T(8,128)S(1)}, f32[24,128]{1,0:T(8,128)S(1)}, u32[]{:S(2)}, u32[]{:S(2)}) collective-permute-start(f32[24,128]{1,0:T(8,128)S(1)} %get-tuple-element.114), channel_id=1, source_target_pairs={{0,1},{1,2},{2,3},{3,4},{4,5},{5,6},{6,7},{7,0},{8,9},{9,10},{10,1... | collective-permute-start | bytes 36872 | tf_op jit(solution)/shard_map/ppermute | solution.py:679
  51.5 3.4 %collective-permute-start.5 = (f32[24,128]{1,0:T(8,128)S(1)}, f32[24,128]{1,0:T(8,128)S(1)}, u32[]{:S(2)}, u32[]{:S(2)}) collective-permute-start(f32[24,128]{1,0:T(8,128)S(1)} %get-tuple-element.115), channel_id=1, source_target_pairs={{0,7},{1,0},{2,1},{3,2},{4,3},{5,4},{6,5},{7,6},{8,15},{9,8},{10,9... | collective-permute-start | bytes 36872 | tf_op jit(solution)/shard_map/ppermute | solution.py:679
  54.9 0.0 collective-permute-done.4.refs_11_
  54.9 2.6 %collective-permute-done.5.refs_12_ = f32[24,128]{1,0:T(8,128)S(1)} collective-permute-done((f32[24,128]{1,0:T(8,128)S(1)}, f32[24,128]{1,0:T(8,128)S(1)}, u32[]{:S(2)}, u32[]{:S(2)}) %collective-permute-start.5) | collective-permute-done | bytes 12320 | tf_op jit(solution)/shard_map/ppermute | solution.py:679
  57.5 0.1 along_x.1
  57.6 1.9 %collective-permute-start.7 = (f32[88,128]{1,0:T(8,128)S(1)}, f32[88,128]{1,0:T(8,128)S(1)}, u32[]{:S(2)}, u32[]{:S(2)}) collective-permute-start(f32[88,128]{1,0:T(8,128)S(1)} %get-tuple-element.117), channel_id=1, source_target_pairs={{0,760},{8,0},{16,8},{24,16},{32,24},{40,32},{48,40},{56,48},{64,5... | collective-permute-start | bytes 135176 | tf_op jit(solution)/shard_map/ppermute | solution.py:679
  59.6 7.3 %collective-permute-start.6 = (f32[88,128]{1,0:T(8,128)S(1)}, f32[88,128]{1,0:T(8,128)S(1)}, u32[]{:S(2)}, u32[]{:S(2)}) collective-permute-start(f32[88,128]{1,0:T(8,128)S(1)} %get-tuple-element.116.refs_14_), channel_id=1, source_target_pairs={{0,8},{8,16},{16,24},{24,32},{32,40},{40,48},{48,56},{56,64},{64,7... | collective-permute-start | bytes 135176 | tf_op jit(solution)/shard_map/ppermute | solution.py:679
  66.8 1.3 %weights.1.refs_28_ = f32[176,128]{1,0:T(8,128)S(1)} custom-call(f32[32,128]{1,0:T(8,128)S(1)} %get-tuple-element.125.refs_0_, bf16[2,64,512]{2,1,0:T(8,128)(2,1)S(1)} %get-tuple-element.126.refs_1_, bf16[2,256,512]{2,1,0:T(8,128)(2,1)S(1)} %get-tuple-element.127.refs_2_, bf16[2,256,512]{2,1,0:T(8,128)(2,1)S(1)} %get-tuple-element.128.refs_3_, ...), custom_call_target="tpu_custom_call" | custom-call | tf_op jit(solution)/shard_map/weights/pallas_call | solution.py:819
  68.1 0.0 collective-permute-done.7.refs_12_
  68.2 4.8 %collective-permute-done.6.refs_11_ = f32[88,128]{1,0:T(8,128)S(1)} collective-permute-done((f32[88,128]{1,0:T(8,128)S(1)}, f32[88,128]{1,0:T(8,128)S(1)}, u32[]{:S(2)}, u32[]{:S(2)}) %collective-permute-start.6) | collective-permute-done | bytes 45088 | tf_op jit(solution)/shard_map/ppermute | solution.py:679
  72.9 3.7 %first_step.1 = (f32[304,128]{1,0:T(8,128)}, f32[16,128]{1,0:T(8,128)}, f32[64,3,128]{2,1,0:T(4,128)S(1)}) custom-call(f32[152,128]{1,0:T(8,128)S(1)} %get-tuple-element.104.refs_0_, f32[152,128]{1,0:T(8,128)S(1)} %get-tuple-element.106.refs_1_, f32[8,128]{1,0:T(8,128)S(1)} %get-tuple-element.107.refs_2_, f32[8,128]{1,0:T(8,128)S(1)} %get-tuple-element.108.refs_3_, ...), custom_call_target="tpu_custom_call" | custom-call | tf_op jit(solution)/shard_map/first_step/pallas_call | solution.py:829
  76.6 17.7 %all_to_all.15.parts = f32[64,3,128]{2,1,0:T(4,128)S(1)} all-to-all(f32[64,3,128]{2,1,0:T(4,128)S(1)} %get-tuple-element.141), channel_id=1, replica_groups={{0,1,2,3,4,5,6,7,8,9,10,11,12,13,14,15,192,193,194,195,196,197,198,199,..., dimensions={0} | all-to-all | bytes 196608 | tf_op jit(solution)/shard_map/all_to_all | solution.py:694
  94.3 0.1 total.2
  94.4 11.8 %all_to_all.16.parts = f32[12,3,128]{2,1,0:T(4,128)S(1)} all-to-all(f32[12,3,128]{2,1,0:T(4,128)S(1)} %total.2), channel_id=1, replica_groups={{0,16,32,48,64,80,96,112,128,144,160,176},{1,17,33,49,65,81,97,113,129,..., dimensions={0} | all-to-all | bytes 36864 | tf_op jit(solution)/shard_map/all_to_all | solution.py:694
  106.2 16.2 %all_to_all.17.parts = f32[64,3,128]{2,1,0:T(4,128)S(1)} all-to-all(f32[64,3,128]{2,1,0:T(4,128)S(1)} %total.3), channel_id=1, replica_groups={{0,1,2,3,4,5,6,7,8,9,10,11,12,13,14,15,192,193,194,195,196,197,198,199,..., dimensions={0} | all-to-all | bytes 196608 | tf_op jit(solution)/shard_map/all_to_all | solution.py:694
  122.4 0.7 unpack.1
  (2 shorter events, 0.0 us)
Async XLA Ops:
  2.5 15.9 %collective-permute-start = (f32[24,128]{1,0:T(8,128)S(1)}, f32[24,128]{1,0:T(8,128)S(1)}, u32[]{:S(2)}, u32[]{:S(2)}) collective-permute-start(f32[24,128]{1,0:T(8,128)S(1)} %get-tuple-element.91), channel_id=1, source_target_pairs={{0,1},{1,2},{2,3},{3,4},{4,5},{5,6},{6,7},{7,0},{8,9},{9,10},{10,1... | collective-permute-start | bytes 36872 | tf_op jit(solution)/shard_map/ppermute | solution.py:679
  7.1 11.3 %collective-permute-start.1 = (f32[24,128]{1,0:T(8,128)S(1)}, f32[24,128]{1,0:T(8,128)S(1)}, u32[]{:S(2)}, u32[]{:S(2)}) collective-permute-start(f32[24,128]{1,0:T(8,128)S(1)} %get-tuple-element.92), channel_id=1, source_target_pairs={{0,7},{1,0},{2,1},{3,2},{4,3},{5,4},{6,5},{7,6},{8,15},{9,8},{10,9... | collective-permute-start | bytes 36872 | tf_op jit(solution)/shard_map/ppermute | solution.py:679
  18.5 17.4 %collective-permute-start.3 = (f32[96,128]{1,0:T(8,128)S(1)}, f32[96,128]{1,0:T(8,128)S(1)}, u32[]{:S(2)}, u32[]{:S(2)}) collective-permute-start(f32[96,128]{1,0:T(8,128)S(1)} %get-tuple-element.105), channel_id=1, source_target_pairs={{0,760},{8,0},{16,8},{24,16},{32,24},{40,32},{48,40},{56,48},{64,5... | collective-permute-start | bytes 147464 | tf_op jit(solution)/shard_map/ppermute | solution.py:679
  33.0 13.0 %collective-permute-start.2 = (f32[96,128]{1,0:T(8,128)S(1)}, f32[96,128]{1,0:T(8,128)S(1)}, u32[]{:S(2)}, u32[]{:S(2)}) collective-permute-start(f32[96,128]{1,0:T(8,128)S(1)} %get-tuple-element.93._), channel_id=1, source_target_pairs={{0,8},{8,16},{16,24},{24,32},{32,40},{40,48},{48,56},{56,64},{64,7... | collective-permute-start | bytes 147464 | tf_op jit(solution)/shard_map/ppermute | solution.py:679
  47.8 7.1 %collective-permute-start.4 = (f32[24,128]{1,0:T(8,128)S(1)}, f32[24,128]{1,0:T(8,128)S(1)}, u32[]{:S(2)}, u32[]{:S(2)}) collective-permute-start(f32[24,128]{1,0:T(8,128)S(1)} %get-tuple-element.114), channel_id=1, source_target_pairs={{0,1},{1,2},{2,3},{3,4},{4,5},{5,6},{6,7},{7,0},{8,9},{9,10},{10,1... | collective-permute-start | bytes 36872 | tf_op jit(solution)/shard_map/ppermute | solution.py:679
  51.5 6.1 %collective-permute-start.5 = (f32[24,128]{1,0:T(8,128)S(1)}, f32[24,128]{1,0:T(8,128)S(1)}, u32[]{:S(2)}, u32[]{:S(2)}) collective-permute-start(f32[24,128]{1,0:T(8,128)S(1)} %get-tuple-element.115), channel_id=1, source_target_pairs={{0,7},{1,0},{2,1},{3,2},{4,3},{5,4},{6,5},{7,6},{8,15},{9,8},{10,9... | collective-permute-start | bytes 36872 | tf_op jit(solution)/shard_map/ppermute | solution.py:679
  57.6 10.5 %collective-permute-start.7 = (f32[88,128]{1,0:T(8,128)S(1)}, f32[88,128]{1,0:T(8,128)S(1)}, u32[]{:S(2)}, u32[]{:S(2)}) collective-permute-start(f32[88,128]{1,0:T(8,128)S(1)} %get-tuple-element.117), channel_id=1, source_target_pairs={{0,760},{8,0},{16,8},{24,16},{32,24},{40,32},{48,40},{56,48},{64,5... | collective-permute-start | bytes 135176 | tf_op jit(solution)/shard_map/ppermute | solution.py:679
  59.6 13.4 %collective-permute-start.6 = (f32[88,128]{1,0:T(8,128)S(1)}, f32[88,128]{1,0:T(8,128)S(1)}, u32[]{:S(2)}, u32[]{:S(2)}) collective-permute-start(f32[88,128]{1,0:T(8,128)S(1)} %get-tuple-element.116.refs_14_), channel_id=1, source_target_pairs={{0,8},{8,16},{16,24},{24,32},{32,40},{40,48},{48,56},{56,64},{64,7... | collective-permute-start | bytes 135176 | tf_op jit(solution)/shard_map/ppermute | solution.py:679

commit v5 on v4

--- a/solution.py
+++ b/solution.py
@@ -262,9 +262,10 @@
 
 def network_back(s1, s2, d, w3b, w2b, w1b):
     dx = stacked(d)
-    px = stacked(product(w3b, dx, HID) * s2)
+    p = product(w3b, dx, HID) * s2
+    px = stacked(p)
     qx = stacked(product(w2b, px, HID) * s1)
-    return product(w1b, qx, KP), dx, px, qx
+    return product(w1b, qx, KP), (folded(d), folded(p)), dx, px, qx
 
 
 def folded(d):
@@ -277,23 +278,18 @@
 
 
 def weight_products(fx, h1x, h2x, dx, px, qx):
-    return nt(h1x, px), nt(fx, jnp.concatenate([qx, px], axis=0)), nt(dx, h2x)
-
-
-def write_pack(pack, acc2, acc1, acc3, accb, pad_ref):
+    return nt(h1x, px), nt(fx, qx), nt(dx, h2x)
+
+
+def write_pack(pack, acc2, acc1, acc3, accb, accp, pad_ref):
     pack[0:HID, :] = four_blocks(acc2[...], HID)
-    d = acc1[...]
-    w1 = four_blocks(d[:, : 2 * HID], KP)
-    pack[HID : HID + 24, :] = w1[0:24]
-    d3 = acc3[...]
-    w3 = four_blocks(d3, KP)
-    pack[HID + 24 : HID + 48, :] = w3[0:24]
-    b2 = four_blocks(d[:, 2 * HID :], KP)[Q : Q + 1]
+    pack[HID : HID + 24, :] = four_blocks(acc1[...], KP)[0:24]
+    pack[HID + 24 : HID + 48, :] = four_blocks(acc3[...], KP)[0:24]
     pad_ref[...] = jnp.zeros((HID, HID), F32)
     pad_ref[0:KP, :] = accb[...]
-    b3 = jnp.sum(jnp.transpose(pad_ref[...]), axis=0, keepdims=True)
-    pack[HID + 21 : HID + 22, :] = b2
-    pack[HID + 22 : HID + 23, :] = b3
+    for k, sums in ((21, accp[...]), (22, pad_ref[...])):
+        row = jnp.sum(jnp.transpose(sums), axis=0, keepdims=True)
+        pack[HID + k : HID + k + 1, :] = row
 
 
 def collided(f, t, code, outs, i):
@@ -349,10 +345,11 @@
 
 
 def other_rows_kernel(
-    f, t, code, adj, l1, l2, l3, b2t, b3t, out0,
-    post, h1s, h2s, xp, xm,
-    feat, outs,
+    f, t, code, adj, l1, l2, l3, b2t, b3t, out0, w1, w2, w3,
+    post, h1s, h2s, xp, xm, w3b, w2b, w1b,
+    feat, outs, pad,
 ):
+    w3b[...], w2b[...], w1b[...] = back_weights(w1, w2, w3, pad)
     fill_features(feat, f)
     back(outs, 0, out0[...])
     for c in range(1, ROWS * LANES // CH):
@@ -368,11 +365,10 @@
 
 
 def prepare_kernel(
-    f, h1a, h2a, h1b, h2b, w1, w2, w3, _,
-    w3b, w2b, w1b, fxs, h1xs, h2xs, s1, s2,
-    feat, pad,
+    f, h1a, h2a, h1b, h2b, _,
+    fxs, h1xs, h2xs, s1, s2,
+    feat,
 ):
-    w3b[...], w2b[...], w1b[...] = back_weights(w1, w2, w3, pad)
     fill_features(feat, f)
     for c in range(ROWS * LANES // CH):
         h1, h2 = (h1a[0], h2a[0]) if c == 0 else (h1b[c - 1], h2b[c - 1])
@@ -423,7 +419,7 @@
 
 def middle_kernel(
     x, post, f, t, code, adj, face, leftward, rightward, l1, l2, b2t, w3b, w2b, w1b,
-    f1, t1, fbar, lift, accb, fxs, h1xs, h2xs, dxs, pxs, qxs,
+    f1, t1, fbar, lift, accb, accp, fxs, h1xs, h2s, dxs, pxs, qxs,
     feat, grad, masked, dfs,
 ):
     kind = code[8 * x : 8 * x + 8, :]
@@ -455,12 +451,12 @@
         fx = stacked(across(feat, c))
         h1, h1x, h2 = hidden(fx, l1[...], l2[...], b2t[...])
         d = across(masked, c)
-        df, dx, px, qx = network_back(
+        df, sums, dx, px, qx = network_back(
             1.0 - h1 * h1, 1.0 - h2 * h2, d, w3b[...], w2b[...], w1b[...]
         )
-        gather((accb,), (folded(d),), c == 0)
+        gather((accb, accp), sums, c == 0)
         back(dfs, c, df)
-        fxs[c], h1xs[c], h2xs[c] = fx, h1x, stacked(h2)
+        fxs[c], h1xs[c], h2s[c] = fx, h1x, h2
         dxs[c], pxs[c], qxs[c] = dx, px, qx
     for i in range(Q):
         k, o = 8 * i, 8 * OPPOSITE[i]
@@ -470,13 +466,15 @@
 
 
 def weights_kernel(*refs):
-    first, second, (_, pack, pad, accb, *accs) = refs[:7], refs[7:14], refs[14:]
+    first, second, (_, pack, pad, accb, accp, *accs) = refs[:8], refs[8:16], refs[16:]
     accb[...] = first[0][...] + second[0][...]
+    accp[...] = first[1][...] + second[1][...]
     for plane in (first, second):
-        for c in range(plane[1].shape[0]):
-            values = weight_products(*(v[c] for v in plane[1:]))
+        for c in range(plane[2].shape[0]):
+            fx, h1x, h2, dx, px, qx = (v[c] for v in plane[2:])
+            values = weight_products(fx, h1x, stacked(h2), dx, px, qx)
             gather(accs, values, plane is first and c == 0)
-    write_pack(pack, *accs, accb, pad)
+    write_pack(pack, *accs, accb, accp, pad)
 
 
 def coefficient(u, a, s, kind):
@@ -619,7 +617,7 @@
     theta2, f, t, below, above, yl, yr,
     tbelow, tabove, tleft, tright, code, w3b, w2b, w1b, fxs, h1xs, h2xs, s1, s2, pack1,
     fbar, thetabar, pack,
-    grad, masked, dfs, pad, acc2, acc1, acc3, accb, lift, total,
+    grad, masked, dfs, pad, acc2, acc1, acc3, accb, accp, lift, total,
     adj, theta, hbelow, habove, hleft, hright,
 ):
     flux_rims = complete(
@@ -630,11 +628,11 @@
     collision_gradient(adj, halo, code, grad, masked, lift)
     for c in range(ROWS * LANES // CH):
         d = across(masked, c)
-        df, dx, px, qx = network_back(s1[c], s2[c], d, w3b[...], w2b[...], w1b[...])
+        df, sums, dx, px, qx = network_back(s1[c], s2[c], d, w3b[...], w2b[...], w1b[...])
         values = weight_products(fxs[c], h1xs[c], h2xs[c], dx, px, qx)
-        gather((acc2, acc1, acc3, accb), (*values, folded(d)), c == 0)
+        gather((acc2, acc1, acc3, accb, accp), (*values, *sums), c == 0)
         back(dfs, c, df)
-    write_pack(total, acc2, acc1, acc3, accb, pad)
+    write_pack(total, acc2, acc1, acc3, accb, accp, pad)
     parts, part, _ = pack.shape
     total[PACK:, :] = jnp.zeros((parts * part - PACK, HID), F32)
     total[0:PACK, :] = (total[0:PACK, :] + pack1[...]) * scale
@@ -774,27 +772,20 @@
     )(*(pltpu.with_memory_space_constraint(v, pltpu.HBM) for v in ins))
     w1, w2, w3, f, t, code, adj, theta, l1, l2, l3, b2t, b3t, h1a, h2a, out0, yp, ym = outs
     sides = along("gy", yp, ym)
-    post, h1b, h2b, xp, xm = call(
+    post, h1b, h2b, xp, xm, w3b, w2b, w1b = call(
         other_rows_kernel,
-        [POPS, *[struct(count - 1, HID, CH)] * 2, struct(96, LANES), struct(96, LANES)],
-        [FULL, FULL],
+        [POPS, *[struct(count - 1, HID, CH)] * 2, struct(96, LANES), struct(96, LANES),
+         narrow(2 * HID, 2 * KP), narrow(2 * HID, 2 * HID), narrow(2 * KP, 2 * HID)],
+        [FULL, FULL, (HID, HID)],
         "other_rows",
-    )(f, t, code, adj, l1, l2, l3, b2t, b3t, out0)
+    )(f, t, code, adj, l1, l2, l3, b2t, b3t, out0, w1, w2, w3)
     blocks = ((1, 0, 88), (-1, 12, 90))
     xp, xm = call(
         lambda *refs: edge_kernel(blocks, *refs), [struct(96, LANES)] * 2, [], "corners"
     )(xp, xm, *sides)
     below, above = along("gx", xp, xm)
     halo0 = (below, above, *sides)
-    w3b, w2b, w1b, *kept = call(
-        prepare_kernel,
-        [narrow(2 * HID, 2 * KP), narrow(2 * HID, 2 * HID), narrow(2 * KP, 2 * HID),
-         narrow(count, 2 * KP, CH), *[narrow(count, 2 * HID, CH)] * 2, *[struct(count, HID, CH)] * 2],
-        [FULL, (HID, HID)],
-        "prepare",
-        in_specs=[pl.BlockSpec(memory_space=pltpu.VMEM)] * 8 + [pl.BlockSpec(memory_space=pl.ANY)],
-    )(f, h1a, h2a, h1b, h2b, w1, w2, w3, xp)
-    accs = [(2 * HID, 2 * HID), (2 * KP, 4 * HID), (2 * KP, 2 * HID), (KP, LANES)]
+    accs = [(2 * HID, 2 * HID), (2 * KP, 2 * HID), (2 * KP, 2 * HID), (KP, LANES), (HID, LANES)]
     plane, half = struct(8 * Q, LANES), struct(8, LANES)
     small, large = (
         jax.ShapeDtypeStruct((8 * LANES // CH, 2 * n, CH), BF16) for n in (KP, HID)
@@ -802,7 +793,8 @@
     planes = [
         call(
             lambda *refs, x=x: middle_kernel(x, *refs),
-            [plane, half, plane, half, struct(KP, LANES), small, large, large, small, large, large],
+            [plane, half, plane, half, struct(KP, LANES), struct(HID, LANES), small, large,
+             struct(8 * LANES // CH, HID, CH), small, large, large],
             [(8 * KP, LANES), (8 * Q, LANES), (8 * KP, LANES), (8 * KP, LANES)],
             "middle",
         )(post, f, t, code, adj, face, *sides, l1, l2, b2t, w3b, w2b, w1b)
@@ -816,12 +808,19 @@
         along_x_kernel, [struct(88, LANES)] * 2 + [struct(24, LANES)] * 2, [], "along_x"
     )(*known, *come)
     faces = along("gx", xp, xm)
+    kept = call(
+        prepare_kernel,
+        [narrow(count, 2 * KP, CH), *[narrow(count, 2 * HID, CH)] * 2, *[struct(count, HID, CH)] * 2],
+        [FULL],
+        "prepare",
+        in_specs=[pl.BlockSpec(memory_space=pltpu.VMEM)] * 5 + [pl.BlockSpec(memory_space=pl.ANY)],
+    )(f, h1a, h2a, h1b, h2b, xp)
     pack1 = call(
         weights_kernel,
         struct(PACK, HID),
-        [(HID, HID), (KP, LANES), *accs[:3]],
+        [(HID, HID), *accs[3:], *accs[:3]],
         "weights",
-        in_specs=[pl.BlockSpec(memory_space=pltpu.VMEM)] * 14 + [pl.BlockSpec(memory_space=pl.ANY)],
+        in_specs=[pl.BlockSpec(memory_space=pltpu.VMEM)] * 16 + [pl.BlockSpec(memory_space=pl.ANY)],
     )(*planes[0][4:], *planes[1][4:], xp)
     scale = 1.0 / math.sqrt(cells)
     shares = shares_of(lax.axis_size("gx"), lax.axis_size("gy"))

time: 124 us -> 123 us (level)
  transfers between devices with their start and end apart: 8 -> 8, of which waited for: 3 -> 3; matrix products, arithmetic and copies ran while one was open for 0% -> 0% of each run, Pallas kernels for 5% -> 4%
where the time goes in v5:
time: 123 us; the launch traced here: 122 us
  starting transfers between devices  47 us (38%)
  blocking collectives  45.7 us (37%)
  waiting for transfers between devices  15.6 us (13%)
  Pallas kernels  13.2 us (11%)
    ppermute x8, starting transfers between devices, shifted(): lax.ppermute(value, axis, [(s, (s + by) % count) for s in range(count)])  47 us
    all_to_all x3, blocking collectives, swapped(): lax.all_to_all(value, ('gx', 'gy'), 0, 0, axis_index_groups=groups, tiled...  45.7 us
    ppermute x8, waiting for transfers between devices, shifted(): lax.ppermute(value, axis, [(s, (s + by) % count) for s in range(count)])  15.6 us
    pallas_call x2, Pallas kernels, per_device(): call(lambda *refs, x=x: middle_kernel(x, *refs), [plane, half, plane, hal...  3.53 us
    pallas_call x1, Pallas kernels, per_device(): call(lambda *refs: first_step_kernel(scale, refs[:8], *refs[8:]), [POPS,...  3.34 us
  transfers between devices with their start and end apart: 8, of which 3 were waited for; matrix products, arithmetic and copies ran while one was open for 0% of the time, Pallas kernels for 4%

profile of v5, /device:TPU:1, one launch (start us, length us, event | category | flops | bytes accessed | tf_op | source)
XLA Modules:
  0.0 122.3 jit_solution(11406287732301482805)
XLA Ops:
  0.6 1.9 %edge_rows.1 = (f32[19,128]{1,0:T(8,128)S(1)}, f32[128,128]{1,0:T(8,128)S(1)}, f32[19,128]{1,0:T(8,128)S(1)}, f32[304,128]{1,0:T(8,128)S(1)}, f32[16,128]{1,0:T(...) custom-call(f32[19,128]{1,0:T(8,128)} %w1_in.1, ...), custom_call_target="tpu_custom_call" | custom-call | tf_op jit(solution)/shard_map/edge_rows/pallas_call | solution.py:763
  2.5 4.6 %collective-permute-start = (f32[24,128]{1,0:T(8,128)S(1)}, f32[24,128]{1,0:T(8,128)S(1)}, u32[]{:S(2)}, u32[]{:S(2)}) collective-permute-start(f32[24,128]{1,0:T(8,128)S(1)} %get-tuple-element.96), channel_id=1, source_target_pairs={{0,1},{1,2},{2,3},{3,4},{4,5},{5,6},{6,7},{7,0},{8,9},{9,10},{10,1... | collective-permute-start | bytes 36872 | tf_op jit(solution)/shard_map/ppermute | solution.py:677
  7.1 9.7 %collective-permute-start.1 = (f32[24,128]{1,0:T(8,128)S(1)}, f32[24,128]{1,0:T(8,128)S(1)}, u32[]{:S(2)}, u32[]{:S(2)}) collective-permute-start(f32[24,128]{1,0:T(8,128)S(1)} %get-tuple-element.97), channel_id=1, source_target_pairs={{0,7},{1,0},{2,1},{3,2},{4,3},{5,4},{6,5},{7,6},{8,15},{9,8},{10,9... | collective-permute-start | bytes 36872 | tf_op jit(solution)/shard_map/ppermute | solution.py:677
  16.9 1.6 %other_rows.1 = (f32[304,128]{1,0:T(8,128)S(1)}, f32[3,128,512]{2,1,0:T(8,128)S(1)}, f32[3,128,512]{2,1,0:T(8,128)S(1)}, f32[96,128]{1,0:T(8,128)S(1)}, f32[96,1...) custom-call(f32[304,128]{1,0:T(8,128)S(1)} %get-tuple-element.80.f.refs, ...), custom_call_target="tpu_custom_call" | custom-call | tf_op jit(solution)/shard_map/other_rows/pallas_call | solution.py:775
  18.4 0.0 collective-permute-done.refs_2_.refs_6_.refs_17_
  18.5 0.0 collective-permute-done.1.refs_3_.refs_7_.refs_18_
  18.5 14.5 %collective-permute-start.3 = (f32[96,128]{1,0:T(8,128)S(1)}, f32[96,128]{1,0:T(8,128)S(1)}, u32[]{:S(2)}, u32[]{:S(2)}) collective-permute-start(f32[96,128]{1,0:T(8,128)S(1)} %get-tuple-element.103), channel_id=1, source_target_pairs={{0,760},{8,0},{16,8},{24,16},{32,24},{40,32},{48,40},{56,48},{64,5... | collective-permute-start | bytes 147464 | tf_op jit(solution)/shard_map/ppermute | solution.py:677
  33.0 1.9 %collective-permute-start.2 = (f32[96,128]{1,0:T(8,128)S(1)}, f32[96,128]{1,0:T(8,128)S(1)}, u32[]{:S(2)}, u32[]{:S(2)}) collective-permute-start(f32[96,128]{1,0:T(8,128)S(1)} %get-tuple-element.98), channel_id=1, source_target_pairs={{0,8},{8,16},{16,24},{24,32},{32,40},{40,48},{48,56},{56,64},{64,7... | collective-permute-start | bytes 147464 | tf_op jit(solution)/shard_map/ppermute | solution.py:677
  34.9 0.0 collective-permute-done.3.refs_5_.refs_16_
  35.0 1.8 %middle.3 = (f32[152,128]{1,0:T(8,128)S(1)}, f32[8,128]{1,0:T(8,128)S(1)}, f32[152,128]{1,0:T(8,128)S(1)}, f32[8,128]{1,0:T(8,128)S(1)}, f32[32,128]{1,0:T(8,128...) custom-call(f32[304,128]{1,0:T(8,128)S(1)} %get-tuple-element.93.ref, ...), custom_call_target="tpu_custom_call" | custom-call | tf_op jit(solution)/shard_map/middle/pallas_call | solution.py:794
  36.7 9.2 %collective-permute-done.2.refs_5_.refs_15_ = f32[96,128]{1,0:T(8,128)S(1)} collective-permute-done((f32[96,128]{1,0:T(8,128)S(1)}, f32[96,128]{1,0:T(8,128)S(1)}, u32[]{:S(2)}, u32[]{:S(2)}) %collective-permute-start.2) | collective-permute-done | bytes 49184 | tf_op jit(solution)/shard_map/ppermute | solution.py:677
  46.0 1.8 %middle.2 = (f32[152,128]{1,0:T(8,128)S(1)}, f32[8,128]{1,0:T(8,128)S(1)}, f32[152,128]{1,0:T(8,128)S(1)}, f32[8,128]{1,0:T(8,128)S(1)}, f32[32,128]{1,0:T(8,128...) custom-call(f32[304,128]{1,0:T(8,128)S(1)} %get-tuple-element.93.ref, ...), custom_call_target="tpu_custom_call" | custom-call | tf_op jit(solution)/shard_map/middle/pallas_call | solution.py:794
  47.8 0.1 along_y.1
  47.9 3.6 %collective-permute-start.4 = (f32[24,128]{1,0:T(8,128)S(1)}, f32[24,128]{1,0:T(8,128)S(1)}, u32[]{:S(2)}, u32[]{:S(2)}) collective-permute-start(f32[24,128]{1,0:T(8,128)S(1)} %get-tuple-element.112), channel_id=1, source_target_pairs={{0,1},{1,2},{2,3},{3,4},{4,5},{5,6},{6,7},{7,0},{8,9},{9,10},{10,1... | collective-permute-start | bytes 36872 | tf_op jit(solution)/shard_map/ppermute | solution.py:677
  51.5 3.5 %collective-permute-start.5 = (f32[24,128]{1,0:T(8,128)S(1)}, f32[24,128]{1,0:T(8,128)S(1)}, u32[]{:S(2)}, u32[]{:S(2)}) collective-permute-start(f32[24,128]{1,0:T(8,128)S(1)} %get-tuple-element.113), channel_id=1, source_target_pairs={{0,7},{1,0},{2,1},{3,2},{4,3},{5,4},{6,5},{7,6},{8,15},{9,8},{10,9... | collective-permute-start | bytes 36872 | tf_op jit(solution)/shard_map/ppermute | solution.py:677
  54.9 0.0 collective-permute-done.4.refs_11_
  55.0 2.6 %collective-permute-done.5.refs_12_ = f32[24,128]{1,0:T(8,128)S(1)} collective-permute-done((f32[24,128]{1,0:T(8,128)S(1)}, f32[24,128]{1,0:T(8,128)S(1)}, u32[]{:S(2)}, u32[]{:S(2)}) %collective-permute-start.5) | collective-permute-done | bytes 12320 | tf_op jit(solution)/shard_map/ppermute | solution.py:677
  57.5 0.1 along_x.1
  57.6 1.9 %collective-permute-start.7 = (f32[88,128]{1,0:T(8,128)S(1)}, f32[88,128]{1,0:T(8,128)S(1)}, u32[]{:S(2)}, u32[]{:S(2)}) collective-permute-start(f32[88,128]{1,0:T(8,128)S(1)} %get-tuple-element.115), channel_id=1, source_target_pairs={{0,760},{8,0},{16,8},{24,16},{32,24},{40,32},{48,40},{56,48},{64,5... | collective-permute-start | bytes 135176 | tf_op jit(solution)/shard_map/ppermute | solution.py:677
  59.6 7.3 %collective-permute-start.6 = (f32[88,128]{1,0:T(8,128)S(1)}, f32[88,128]{1,0:T(8,128)S(1)}, u32[]{:S(2)}, u32[]{:S(2)}) collective-permute-start(f32[88,128]{1,0:T(8,128)S(1)} %get-tuple-element.114._.refs_16_), channel_id=1, source_target_pairs={{0,8},{8,16},{16,24},{24,32},{32,40},{40,48},{48,56},{56,64},{64,7... | collective-permute-start | bytes 135176 | tf_op jit(solution)/shard_map/ppermute | solution.py:677
  66.8 0.8 prepare.1
  67.6 1.0 weights.1.refs_28_
  68.7 0.0 collective-permute-done.7.refs_12_
  68.7 3.8 %collective-permute-done.6.refs_11_ = f32[88,128]{1,0:T(8,128)S(1)} collective-permute-done((f32[88,128]{1,0:T(8,128)S(1)}, f32[88,128]{1,0:T(8,128)S(1)}, u32[]{:S(2)}, u32[]{:S(2)}) %collective-permute-start.6) | collective-permute-done | bytes 45088 | tf_op jit(solution)/shard_map/ppermute | solution.py:677
  72.5 3.3 %first_step.1 = (f32[304,128]{1,0:T(8,128)}, f32[16,128]{1,0:T(8,128)}, f32[64,3,128]{2,1,0:T(4,128)S(1)}) custom-call(f32[152,128]{1,0:T(8,128)S(1)} %get-tuple-element.102.refs_0_, f32[152,128]{1,0:T(8,128)S(1)} %get-tuple-element.104.refs_1_, f32[8,128]{1,0:T(8,128)S(1)} %get-tuple-element.105.refs_2_, f32[8,128]{1,0:T(8,128)S(1)} %get-tuple-element.106.refs_3_, ...), custom_call_target="tpu_custom_call" | custom-call | tf_op jit(solution)/shard_map/first_step/pallas_call | solution.py:828
  75.8 17.8 %all_to_all.15.parts = f32[64,3,128]{2,1,0:T(4,128)S(1)} all-to-all(f32[64,3,128]{2,1,0:T(4,128)S(1)} %get-tuple-element.145), channel_id=1, replica_groups={{0,1,2,3,4,5,6,7,8,9,10,11,12,13,14,15,192,193,194,195,196,197,198,199,..., dimensions={0} | all-to-all | bytes 196608 | tf_op jit(solution)/shard_map/all_to_all | solution.py:692
  93.6 0.1 total.2
  93.7 11.8 %all_to_all.16.parts = f32[12,3,128]{2,1,0:T(4,128)S(1)} all-to-all(f32[12,3,128]{2,1,0:T(4,128)S(1)} %total.2), channel_id=1, replica_groups={{0,16,32,48,64,80,96,112,128,144,160,176},{1,17,33,49,65,81,97,113,129,..., dimensions={0} | all-to-all | bytes 36864 | tf_op jit(solution)/shard_map/all_to_all | solution.py:692
  105.5 16.2 %all_to_all.17.parts = f32[64,3,128]{2,1,0:T(4,128)S(1)} all-to-all(f32[64,3,128]{2,1,0:T(4,128)S(1)} %total.3), channel_id=1, replica_groups={{0,1,2,3,4,5,6,7,8,9,10,11,12,13,14,15,192,193,194,195,196,197,198,199,..., dimensions={0} | all-to-all | bytes 196608 | tf_op jit(solution)/shard_map/all_to_all | solution.py:692
  121.7 0.7 unpack.1
  (2 shorter events, 0.0 us)
Async XLA Ops:
  2.5 15.9 %collective-permute-start = (f32[24,128]{1,0:T(8,128)S(1)}, f32[24,128]{1,0:T(8,128)S(1)}, u32[]{:S(2)}, u32[]{:S(2)}) collective-permute-start(f32[24,128]{1,0:T(8,128)S(1)} %get-tuple-element.96), channel_id=1, source_target_pairs={{0,1},{1,2},{2,3},{3,4},{4,5},{5,6},{6,7},{7,0},{8,9},{9,10},{10,1... | collective-permute-start | bytes 36872 | tf_op jit(solution)/shard_map/ppermute | solution.py:677
  7.1 11.3 %collective-permute-start.1 = (f32[24,128]{1,0:T(8,128)S(1)}, f32[24,128]{1,0:T(8,128)S(1)}, u32[]{:S(2)}, u32[]{:S(2)}) collective-permute-start(f32[24,128]{1,0:T(8,128)S(1)} %get-tuple-element.97), channel_id=1, source_target_pairs={{0,7},{1,0},{2,1},{3,2},{4,3},{5,4},{6,5},{7,6},{8,15},{9,8},{10,9... | collective-permute-start | bytes 36872 | tf_op jit(solution)/shard_map/ppermute | solution.py:677
  18.5 16.5 %collective-permute-start.3 = (f32[96,128]{1,0:T(8,128)S(1)}, f32[96,128]{1,0:T(8,128)S(1)}, u32[]{:S(2)}, u32[]{:S(2)}) collective-permute-start(f32[96,128]{1,0:T(8,128)S(1)} %get-tuple-element.103), channel_id=1, source_target_pairs={{0,760},{8,0},{16,8},{24,16},{32,24},{40,32},{48,40},{56,48},{64,5... | collective-permute-start | bytes 147464 | tf_op jit(solution)/shard_map/ppermute | solution.py:677
  33.0 13.0 %collective-permute-start.2 = (f32[96,128]{1,0:T(8,128)S(1)}, f32[96,128]{1,0:T(8,128)S(1)}, u32[]{:S(2)}, u32[]{:S(2)}) collective-permute-start(f32[96,128]{1,0:T(8,128)S(1)} %get-tuple-element.98), channel_id=1, source_target_pairs={{0,8},{8,16},{16,24},{24,32},{32,40},{40,48},{48,56},{56,64},{64,7... | collective-permute-start | bytes 147464 | tf_op jit(solution)/shard_map/ppermute | solution.py:677
  47.9 7.1 %collective-permute-start.4 = (f32[24,128]{1,0:T(8,128)S(1)}, f32[24,128]{1,0:T(8,128)S(1)}, u32[]{:S(2)}, u32[]{:S(2)}) collective-permute-start(f32[24,128]{1,0:T(8,128)S(1)} %get-tuple-element.112), channel_id=1, source_target_pairs={{0,1},{1,2},{2,3},{3,4},{4,5},{5,6},{6,7},{7,0},{8,9},{9,10},{10,1... | collective-permute-start | bytes 36872 | tf_op jit(solution)/shard_map/ppermute | solution.py:677
  51.5 6.1 %collective-permute-start.5 = (f32[24,128]{1,0:T(8,128)S(1)}, f32[24,128]{1,0:T(8,128)S(1)}, u32[]{:S(2)}, u32[]{:S(2)}) collective-permute-start(f32[24,128]{1,0:T(8,128)S(1)} %get-tuple-element.113), channel_id=1, source_target_pairs={{0,7},{1,0},{2,1},{3,2},{4,3},{5,4},{6,5},{7,6},{8,15},{9,8},{10,9... | collective-permute-start | bytes 36872 | tf_op jit(solution)/shard_map/ppermute | solution.py:677
  57.6 11.0 %collective-permute-start.7 = (f32[88,128]{1,0:T(8,128)S(1)}, f32[88,128]{1,0:T(8,128)S(1)}, u32[]{:S(2)}, u32[]{:S(2)}) collective-permute-start(f32[88,128]{1,0:T(8,128)S(1)} %get-tuple-element.115), channel_id=1, source_target_pairs={{0,760},{8,0},{16,8},{24,16},{32,24},{40,32},{48,40},{56,48},{64,5... | collective-permute-start | bytes 135176 | tf_op jit(solution)/shard_map/ppermute | solution.py:677
  59.6 12.9 %collective-permute-start.6 = (f32[88,128]{1,0:T(8,128)S(1)}, f32[88,128]{1,0:T(8,128)S(1)}, u32[]{:S(2)}, u32[]{:S(2)}) collective-permute-start(f32[88,128]{1,0:T(8,128)S(1)} %get-tuple-element.114._.refs_16_), channel_id=1, source_target_pairs={{0,8},{8,16},{16,24},{24,32},{32,40},{40,48},{48,56},{56,64},{64,7... | collective-permute-start | bytes 135176 | tf_op jit(solution)/shard_map/ppermute | solution.py:677

commit v6 on v5

--- a/solution.py
+++ b/solution.py
@@ -25,7 +25,7 @@
 KP = 32
 ROWS = 16
 LANES = 128
-CH = 512
+CH = 1024
 PACK = 176
 F32 = jnp.float32
 BF16 = jnp.bfloat16

time: 123 us -> 122 us (level)
  Pallas kernels: 13.2 us -> 10.6 us
  transfers between devices with their start and end apart: 8 -> 8, of which waited for: 3 -> 3; matrix products, arithmetic and copies ran while one was open for 0% -> 0% of each run, Pallas kernels for 4% -> 3%
where the time goes in v6:
time: 122 us; the launch traced here: 121 us
  starting transfers between devices  47.6 us (39%)
  blocking collectives  46.8 us (38%)
  waiting for transfers between devices  15.6 us (13%)
  Pallas kernels  10.6 us (9%)
    ppermute x8, starting transfers between devices, shifted(): lax.ppermute(value, axis, [(s, (s + by) % count) for s in range(count)])  47.6 us
    all_to_all x3, blocking collectives, swapped(): lax.all_to_all(value, ('gx', 'gy'), 0, 0, axis_index_groups=groups, tiled...  46.8 us
    ppermute x8, waiting for transfers between devices, shifted(): lax.ppermute(value, axis, [(s, (s + by) % count) for s in range(count)])  15.6 us
    pallas_call x1, Pallas kernels, per_device(): call(lambda *refs: first_step_kernel(scale, refs[:8], *refs[8:]), [POPS,...  2.57 us
  transfers between devices with their start and end apart: 8, of which 3 were waited for; matrix products, arithmetic and copies ran while one was open for 0% of the time, Pallas kernels for 3%

profile of v6, /device:TPU:1, one launch (start us, length us, event | category | flops | bytes accessed | tf_op | source)
XLA Modules:
  0.0 121.3 jit_solution(11646715936584737995)
XLA Ops:
  0.6 2.0 %edge_rows.1 = (f32[19,128]{1,0:T(8,128)S(1)}, f32[128,128]{1,0:T(8,128)S(1)}, f32[19,128]{1,0:T(8,128)S(1)}, f32[304,128]{1,0:T(8,128)S(1)}, f32[16,128]{1,0:T(...) custom-call(f32[19,128]{1,0:T(8,128)} %w1_in.1, ...), custom_call_target="tpu_custom_call" | custom-call | tf_op jit(solution)/shard_map/edge_rows/pallas_call | solution.py:763
  2.6 4.6 %collective-permute-start = (f32[24,128]{1,0:T(8,128)S(1)}, f32[24,128]{1,0:T(8,128)S(1)}, u32[]{:S(2)}, u32[]{:S(2)}) collective-permute-start(f32[24,128]{1,0:T(8,128)S(1)} %get-tuple-element.96), channel_id=1, source_target_pairs={{0,1},{1,2},{2,3},{3,4},{4,5},{5,6},{6,7},{7,0},{8,9},{9,10},{10,1... | collective-permute-start | bytes 36872 | tf_op jit(solution)/shard_map/ppermute | solution.py:677
  7.2 9.7 %collective-permute-start.1 = (f32[24,128]{1,0:T(8,128)S(1)}, f32[24,128]{1,0:T(8,128)S(1)}, u32[]{:S(2)}, u32[]{:S(2)}) collective-permute-start(f32[24,128]{1,0:T(8,128)S(1)} %get-tuple-element.97), channel_id=1, source_target_pairs={{0,7},{1,0},{2,1},{3,2},{4,3},{5,4},{6,5},{7,6},{8,15},{9,8},{10,9... | collective-permute-start | bytes 36872 | tf_op jit(solution)/shard_map/ppermute | solution.py:677
  16.9 0.8 other_rows.1
  17.7 0.0 collective-permute-done.refs_2_.refs_6_.refs_17_
  17.7 0.0 collective-permute-done.1.refs_3_.refs_7_.refs_18_
  17.8 15.3 %collective-permute-start.3 = (f32[96,128]{1,0:T(8,128)S(1)}, f32[96,128]{1,0:T(8,128)S(1)}, u32[]{:S(2)}, u32[]{:S(2)}) collective-permute-start(f32[96,128]{1,0:T(8,128)S(1)} %get-tuple-element.103), channel_id=1, source_target_pairs={{0,760},{8,0},{16,8},{24,16},{32,24},{40,32},{48,40},{56,48},{64,5... | collective-permute-start | bytes 147464 | tf_op jit(solution)/shard_map/ppermute | solution.py:677
  33.1 1.9 %collective-permute-start.2 = (f32[96,128]{1,0:T(8,128)S(1)}, f32[96,128]{1,0:T(8,128)S(1)}, u32[]{:S(2)}, u32[]{:S(2)}) collective-permute-start(f32[96,128]{1,0:T(8,128)S(1)} %get-tuple-element.98), channel_id=1, source_target_pairs={{0,8},{8,16},{16,24},{24,32},{32,40},{40,48},{48,56},{56,64},{64,7... | collective-permute-start | bytes 147464 | tf_op jit(solution)/shard_map/ppermute | solution.py:677
  35.0 0.0 collective-permute-done.3.refs_5_.refs_16_
  35.1 1.2 middle.3
  36.2 9.8 %collective-permute-done.2.refs_5_.refs_15_ = f32[96,128]{1,0:T(8,128)S(1)} collective-permute-done((f32[96,128]{1,0:T(8,128)S(1)}, f32[96,128]{1,0:T(8,128)S(1)}, u32[]{:S(2)}, u32[]{:S(2)}) %collective-permute-start.2) | collective-permute-done | bytes 49184 | tf_op jit(solution)/shard_map/ppermute | solution.py:677
  46.1 1.2 middle.2
  47.3 0.1 along_y.1
  47.4 3.4 %collective-permute-start.4 = (f32[24,128]{1,0:T(8,128)S(1)}, f32[24,128]{1,0:T(8,128)S(1)}, u32[]{:S(2)}, u32[]{:S(2)}) collective-permute-start(f32[24,128]{1,0:T(8,128)S(1)} %get-tuple-element.112), channel_id=1, source_target_pairs={{0,1},{1,2},{2,3},{3,4},{4,5},{5,6},{6,7},{7,0},{8,9},{9,10},{10,1... | collective-permute-start | bytes 36872 | tf_op jit(solution)/shard_map/ppermute | solution.py:677
  50.8 3.5 %collective-permute-start.5 = (f32[24,128]{1,0:T(8,128)S(1)}, f32[24,128]{1,0:T(8,128)S(1)}, u32[]{:S(2)}, u32[]{:S(2)}) collective-permute-start(f32[24,128]{1,0:T(8,128)S(1)} %get-tuple-element.113), channel_id=1, source_target_pairs={{0,7},{1,0},{2,1},{3,2},{4,3},{5,4},{6,5},{7,6},{8,15},{9,8},{10,9... | collective-permute-start | bytes 36872 | tf_op jit(solution)/shard_map/ppermute | solution.py:677
  54.2 0.0 collective-permute-done.4.refs_11_
  54.3 1.8 %collective-permute-done.5.refs_12_ = f32[24,128]{1,0:T(8,128)S(1)} collective-permute-done((f32[24,128]{1,0:T(8,128)S(1)}, f32[24,128]{1,0:T(8,128)S(1)}, u32[]{:S(2)}, u32[]{:S(2)}) %collective-permute-start.5) | collective-permute-done | bytes 12320 | tf_op jit(solution)/shard_map/ppermute | solution.py:677
  56.1 0.1 along_x.1
  56.2 1.9 %collective-permute-start.7 = (f32[88,128]{1,0:T(8,128)S(1)}, f32[88,128]{1,0:T(8,128)S(1)}, u32[]{:S(2)}, u32[]{:S(2)}) collective-permute-start(f32[88,128]{1,0:T(8,128)S(1)} %get-tuple-element.115), channel_id=1, source_target_pairs={{0,760},{8,0},{16,8},{24,16},{32,24},{40,32},{48,40},{56,48},{64,5... | collective-permute-start | bytes 135176 | tf_op jit(solution)/shard_map/ppermute | solution.py:677
  58.1 7.3 %collective-permute-start.6 = (f32[88,128]{1,0:T(8,128)S(1)}, f32[88,128]{1,0:T(8,128)S(1)}, u32[]{:S(2)}, u32[]{:S(2)}) collective-permute-start(f32[88,128]{1,0:T(8,128)S(1)} %get-tuple-element.114._.refs_16_), channel_id=1, source_target_pairs={{0,8},{8,16},{16,24},{24,32},{32,40},{40,48},{48,56},{56,64},{64,7... | collective-permute-start | bytes 135176 | tf_op jit(solution)/shard_map/ppermute | solution.py:677
  65.4 0.9 prepare.1
  66.3 1.0 weights.1.refs_28_
  67.3 0.0 collective-permute-done.7.refs_12_
  67.3 3.9 %collective-permute-done.6.refs_11_ = f32[88,128]{1,0:T(8,128)S(1)} collective-permute-done((f32[88,128]{1,0:T(8,128)S(1)}, f32[88,128]{1,0:T(8,128)S(1)}, u32[]{:S(2)}, u32[]{:S(2)}) %collective-permute-start.6) | collective-permute-done | bytes 45088 | tf_op jit(solution)/shard_map/ppermute | solution.py:677
  71.2 2.6 %first_step.1 = (f32[304,128]{1,0:T(8,128)}, f32[16,128]{1,0:T(8,128)}, f32[64,3,128]{2,1,0:T(4,128)S(1)}) custom-call(f32[152,128]{1,0:T(8,128)S(1)} %get-tuple-element.102.refs_0_, f32[152,128]{1,0:T(8,128)S(1)} %get-tuple-element.104.refs_1_, f32[8,128]{1,0:T(8,128)S(1)} %get-tuple-element.105.refs_2_, f32[8,128]{1,0:T(8,128)S(1)} %get-tuple-element.106.refs_3_, ...), custom_call_target="tpu_custom_call" | custom-call | tf_op jit(solution)/shard_map/first_step/pallas_call | solution.py:828
  73.8 18.8 %all_to_all.15.parts = f32[64,3,128]{2,1,0:T(4,128)S(1)} all-to-all(f32[64,3,128]{2,1,0:T(4,128)S(1)} %get-tuple-element.145), channel_id=1, replica_groups={{0,1,2,3,4,5,6,7,8,9,10,11,12,13,14,15,192,193,194,195,196,197,198,199,..., dimensions={0} | all-to-all | bytes 196608 | tf_op jit(solution)/shard_map/all_to_all | solution.py:692
  92.6 0.1 total.2
  92.7 11.8 %all_to_all.16.parts = f32[12,3,128]{2,1,0:T(4,128)S(1)} all-to-all(f32[12,3,128]{2,1,0:T(4,128)S(1)} %total.2), channel_id=1, replica_groups={{0,16,32,48,64,80,96,112,128,144,160,176},{1,17,33,49,65,81,97,113,129,..., dimensions={0} | all-to-all | bytes 36864 | tf_op jit(solution)/shard_map/all_to_all | solution.py:692
  104.5 16.2 %all_to_all.17.parts = f32[64,3,128]{2,1,0:T(4,128)S(1)} all-to-all(f32[64,3,128]{2,1,0:T(4,128)S(1)} %total.3), channel_id=1, replica_groups={{0,1,2,3,4,5,6,7,8,9,10,11,12,13,14,15,192,193,194,195,196,197,198,199,..., dimensions={0} | all-to-all | bytes 196608 | tf_op jit(solution)/shard_map/all_to_all | solution.py:692
  120.7 0.7 unpack.1
  (2 shorter events, 0.0 us)
Async XLA Ops:
  2.6 15.1 %collective-permute-start = (f32[24,128]{1,0:T(8,128)S(1)}, f32[24,128]{1,0:T(8,128)S(1)}, u32[]{:S(2)}, u32[]{:S(2)}) collective-permute-start(f32[24,128]{1,0:T(8,128)S(1)} %get-tuple-element.96), channel_id=1, source_target_pairs={{0,1},{1,2},{2,3},{3,4},{4,5},{5,6},{6,7},{7,0},{8,9},{9,10},{10,1... | collective-permute-start | bytes 36872 | tf_op jit(solution)/shard_map/ppermute | solution.py:677
  7.2 10.5 %collective-permute-start.1 = (f32[24,128]{1,0:T(8,128)S(1)}, f32[24,128]{1,0:T(8,128)S(1)}, u32[]{:S(2)}, u32[]{:S(2)}) collective-permute-start(f32[24,128]{1,0:T(8,128)S(1)} %get-tuple-element.97), channel_id=1, source_target_pairs={{0,7},{1,0},{2,1},{3,2},{4,3},{5,4},{6,5},{7,6},{8,15},{9,8},{10,9... | collective-permute-start | bytes 36872 | tf_op jit(solution)/shard_map/ppermute | solution.py:677
  17.8 17.3 %collective-permute-start.3 = (f32[96,128]{1,0:T(8,128)S(1)}, f32[96,128]{1,0:T(8,128)S(1)}, u32[]{:S(2)}, u32[]{:S(2)}) collective-permute-start(f32[96,128]{1,0:T(8,128)S(1)} %get-tuple-element.103), channel_id=1, source_target_pairs={{0,760},{8,0},{16,8},{24,16},{32,24},{40,32},{48,40},{56,48},{64,5... | collective-permute-start | bytes 147464 | tf_op jit(solution)/shard_map/ppermute | solution.py:677
  33.1 13.0 %collective-permute-start.2 = (f32[96,128]{1,0:T(8,128)S(1)}, f32[96,128]{1,0:T(8,128)S(1)}, u32[]{:S(2)}, u32[]{:S(2)}) collective-permute-start(f32[96,128]{1,0:T(8,128)S(1)} %get-tuple-element.98), channel_id=1, source_target_pairs={{0,8},{8,16},{16,24},{24,32},{32,40},{40,48},{48,56},{56,64},{64,7... | collective-permute-start | bytes 147464 | tf_op jit(solution)/shard_map/ppermute | solution.py:677
  47.4 6.9 %collective-permute-start.4 = (f32[24,128]{1,0:T(8,128)S(1)}, f32[24,128]{1,0:T(8,128)S(1)}, u32[]{:S(2)}, u32[]{:S(2)}) collective-permute-start(f32[24,128]{1,0:T(8,128)S(1)} %get-tuple-element.112), channel_id=1, source_target_pairs={{0,1},{1,2},{2,3},{3,4},{4,5},{5,6},{6,7},{7,0},{8,9},{9,10},{10,1... | collective-permute-start | bytes 36872 | tf_op jit(solution)/shard_map/ppermute | solution.py:677
  50.8 5.3 %collective-permute-start.5 = (f32[24,128]{1,0:T(8,128)S(1)}, f32[24,128]{1,0:T(8,128)S(1)}, u32[]{:S(2)}, u32[]{:S(2)}) collective-permute-start(f32[24,128]{1,0:T(8,128)S(1)} %get-tuple-element.113), channel_id=1, source_target_pairs={{0,7},{1,0},{2,1},{3,2},{4,3},{5,4},{6,5},{7,6},{8,15},{9,8},{10,9... | collective-permute-start | bytes 36872 | tf_op jit(solution)/shard_map/ppermute | solution.py:677
  56.2 11.1 %collective-permute-start.7 = (f32[88,128]{1,0:T(8,128)S(1)}, f32[88,128]{1,0:T(8,128)S(1)}, u32[]{:S(2)}, u32[]{:S(2)}) collective-permute-start(f32[88,128]{1,0:T(8,128)S(1)} %get-tuple-element.115), channel_id=1, source_target_pairs={{0,760},{8,0},{16,8},{24,16},{32,24},{40,32},{48,40},{56,48},{64,5... | collective-permute-start | bytes 135176 | tf_op jit(solution)/shard_map/ppermute | solution.py:677
  58.1 13.1 %collective-permute-start.6 = (f32[88,128]{1,0:T(8,128)S(1)}, f32[88,128]{1,0:T(8,128)S(1)}, u32[]{:S(2)}, u32[]{:S(2)}) collective-permute-start(f32[88,128]{1,0:T(8,128)S(1)} %get-tuple-element.114._.refs_16_), channel_id=1, source_target_pairs={{0,8},{8,16},{16,24},{24,32},{32,40},{40,48},{48,56},{56,64},{64,7... | collective-permute-start | bytes 135176 | tf_op jit(solution)/shard_map/ppermute | solution.py:677
